TPU v7x, 128 devices: a whole 4x4x4 slice. The times are simulated.
128 devices in a mesh: gx: 8 (over z, core), gy: 16 (over x, y).
Axes of the slice: x: 4, y: 4, z: 4, core: 2. Of those that a mesh axis runs over, the one named last changes fastest.
Arguments:
- velocity: float32 [3, 768, 256, 128], P(None, 'gx', 'gy'), may hold values from -6 to 6
- states: float32 [2, 768, 256, 128], P(None, 'gx', 'gy'), may hold values from -6 to 6
- pull_plan: int32 [48, 16], P('gx', 'gy'), may hold values from 0 to 31, as said below
- send_plan: int32 [8, 16, 16, 2], P('gx', 'gy'), may hold values from -1 to 5, as said below
- codes: int32 [3, 48, 16], P(None, 'gx', 'gy'), may hold values from 0 to 1023, as said below
Outputs:
- hessian_velocity: float32 [3, 768, 256, 128], P(None, 'gx', 'gy')
Inputs may be any that keep to these rules, and one draw needn't show every extreme that they name: `pull_plan`: the bricks of one device name distinct slots; slot p of device (g, h) is filled by device (g, p // 2) along gy. Every device uses 2 slots from at least one supplying device, and at most 2 from any. send_plan[g, s, h, e] is the brick of device (g, s), in order of brick rows then brick columns within the device, that fills slot s * 2 + e of device (g, h), or -1 where no brick of device (g, h) names that slot; it agrees with pull_plan. codes[0] and codes[1] lie in 0 .. 7; codes[2] is the depth position in units of 1 / 8 cell.
All inputs are finite; a program needn't handle non-finite values.
Results may differ from a plain program's by a relative error of at most 0.00013.
Values sent between devices are 32-bit elements; how exact they have to be, the bound alone decides.
No kernel may reach another device: no remote copies, remote signals or barrier semaphores. Data moves between devices by JAX's collectives and lax.ppermute only.
A program may use at most 128 MiB of HBM per device.

v0:
```python
import jax
import jax.numpy as jnp
from jax import lax
from jax.sharding import PartitionSpec as P

BX = 16
BY = 16
CAP = 2
QF = 8
STEPS = 2


def with_halo(cells, sides, width):
    for axis, dim in sides:
        count = lax.axis_size(axis)
        head = lax.slice_in_dim(cells, 0, width, axis=dim)
        tail = lax.slice_in_dim(cells, cells.shape[dim] - width, cells.shape[dim], axis=dim)
        cells = jnp.concatenate(
            [
                lax.ppermute(tail, axis, [(i, (i + 1) % count) for i in range(count)]),
                cells,
                lax.ppermute(head, axis, [((i + 1) % count, i) for i in range(count)]),
            ],
            axis=dim,
        )
    return cells


def cubic_weights(fraction):
    return (
        -fraction * (fraction - 1.0) * (fraction - 2.0) / 6.0,
        (fraction + 1.0) * (fraction - 1.0) * (fraction - 2.0) / 2.0,
        -(fraction + 1.0) * fraction * (fraction - 2.0) / 2.0,
        (fraction + 1.0) * fraction * (fraction - 1.0) / 6.0,
    )


def band_matrix(code_row, cells):
    fraction = code_row.astype(jnp.float32) / QF
    weights = cubic_weights(fraction[:, None, None])
    row_index = jnp.arange(cells)[None, :, None]
    col_index = jnp.arange(cells + 3)[None, None, :]
    total = jnp.zeros((code_row.shape[0], cells, cells + 3), jnp.float32)
    for offset in range(4):
        total = total + weights[offset] * (col_index == row_index + offset).astype(jnp.float32)
    return total


def circulant(code_row, cells):
    shift_cells = code_row // QF
    fraction = (code_row % QF).astype(jnp.float32) / QF
    weights = cubic_weights(fraction[:, None, None])
    row_index = jnp.arange(cells)[None, :, None]
    col_index = jnp.arange(cells)[None, None, :]
    total = jnp.zeros((code_row.shape[0], cells, cells), jnp.float32)
    for offset in range(4):
        target = (row_index + shift_cells[:, None, None] + offset - 1) % cells
        total = total + weights[offset] * (col_index == target).astype(jnp.float32)
    return total


def interpolate(windows, weight_rows, weight_cols, weight_depth):
    high = lax.Precision.HIGHEST
    along_depth = jnp.einsum("nabz,ncz->nabc", windows, weight_depth, precision=high)
    along_rows = jnp.einsum("nia,nabc->nibc", weight_rows, along_depth, precision=high)
    return jnp.einsum("njb,nibc->nijc", weight_cols, along_rows, precision=high)


def interpolate_adjoint(values, weight_rows, weight_cols, weight_depth):
    high = lax.Precision.HIGHEST
    along_cols = jnp.einsum("njb,nijc->nibc", weight_cols, values, precision=high)
    along_rows = jnp.einsum("nia,nibc->nabc", weight_rows, along_cols, precision=high)
    return jnp.einsum("ncz,nabc->nabz", weight_depth, along_rows, precision=high)


def extend(stacked):
    return with_halo(stacked, (("gx", 1), ("gy", 2)), 2)


def cut_windows(extended, brick_rows):
    pieces = []
    for row_brick in range(brick_rows):
        pieces.append(extended[row_brick * BX + 1 : row_brick * BX + BX + 4, 1 : BY + 4])
    return jnp.stack(pieces)


def place_windows(collected, brick_rows, brick_cols, rows_dev, cols_dev, depth_cells):
    accumulate = jnp.zeros((rows_dev + 4, cols_dev + 4, depth_cells), jnp.float32)
    for row_brick in range(brick_rows):
        accumulate = accumulate.at[row_brick * BX + 1 : row_brick * BX + BX + 4, 1 : BY + 4].add(
            collected[row_brick * brick_cols]
        )
    return accumulate


def fold_margins(accumulate, rows_dev, cols_dev, depth_cells):
    strips = jnp.zeros((3, rows_dev, cols_dev, depth_cells), jnp.float32)
    strips = strips.at[0, 0:2].set(accumulate[0:2, 2 : cols_dev + 2])
    strips = strips.at[0, rows_dev - 2 :].set(accumulate[rows_dev + 2 :, 2 : cols_dev + 2])
    strips = strips.at[1, :, 0:2].set(accumulate[2 : rows_dev + 2, 0:2])
    strips = strips.at[1, :, cols_dev - 2 :].set(accumulate[2 : rows_dev + 2, cols_dev + 2 :])
    strips = strips.at[2, 0:2, 0:2].set(accumulate[0:2, 0:2])
    strips = strips.at[2, 0:2, cols_dev - 2 :].set(accumulate[0:2, cols_dev + 2 :])
    strips = strips.at[2, rows_dev - 2 :, 0:2].set(accumulate[rows_dev + 2 :, 0:2])
    strips = strips.at[2, rows_dev - 2 :, cols_dev - 2 :].set(
        accumulate[rows_dev + 2 :, cols_dev + 2 :]
    )
    arrived = with_halo(strips, (("gx", 1), ("gy", 2)), 2)
    result = accumulate[2 : rows_dev + 2, 2 : cols_dev + 2]
    result = result.at[0:2].add(arrived[0, 0:2, 2 : cols_dev + 2])
    result = result.at[rows_dev - 2 :].add(arrived[0, rows_dev + 2 :, 2 : cols_dev + 2])
    result = result.at[:, 0:2].add(arrived[1, 2 : rows_dev + 2, 0:2])
    result = result.at[:, cols_dev - 2 :].add(arrived[1, 2 : rows_dev + 2, cols_dev + 2 :])
    result = result.at[0:2, 0:2].add(arrived[2, 0:2, 0:2])
    result = result.at[0:2, cols_dev - 2 :].add(arrived[2, 0:2, cols_dev + 2 :])
    result = result.at[rows_dev - 2 :, 0:2].add(arrived[2, rows_dev + 2 :, 0:2])
    result = result.at[rows_dev - 2 :, cols_dev - 2 :].add(
        arrived[2, rows_dev + 2 :, cols_dev + 2 :]
    )
    return result


def body(velocity, states, pull_plan, send_plan, codes):
    rows_dev = velocity.shape[1]
    cols_dev = velocity.shape[2]
    depth_cells = velocity.shape[3]
    brick_rows = rows_dev // BX
    brick_cols = cols_dev // BY
    bricks = brick_rows * brick_cols
    peer_count = lax.axis_size("gy")
    slot_count = peer_count * CAP
    step_size = 1.0 / STEPS
    high = lax.Precision.HIGHEST
    pull_flat = pull_plan.reshape(bricks)
    owners = send_plan.reshape(slot_count)
    send_flat = jnp.maximum(owners, 0)
    code_flat = codes.reshape(3, bricks)
    selector = (owners[None, :] == jnp.arange(bricks)[:, None]).astype(jnp.float32)
    weight_rows = band_matrix(code_flat[0], BX)
    weight_cols = band_matrix(code_flat[1], BY)
    weight_depth = circulant(code_flat[2], depth_cells)
    extended_states = extend(states)
    centre = extended_states[:, 2 : rows_dev + 2, 2 : cols_dev + 2]
    grad_rows = (
        extended_states[:, 3 : rows_dev + 3, 2 : cols_dev + 2]
        - extended_states[:, 1 : rows_dev + 1, 2 : cols_dev + 2]
    ) * 0.5
    grad_cols = (
        extended_states[:, 2 : rows_dev + 2, 3 : cols_dev + 3]
        - extended_states[:, 2 : rows_dev + 2, 1 : cols_dev + 1]
    ) * 0.5
    grad_depth = (jnp.roll(centre, -1, 3) - jnp.roll(centre, 1, 3)) * 0.5
    gradients = jnp.stack([grad_rows, grad_cols, grad_depth], axis=1)
    tangent = jnp.zeros((rows_dev, cols_dev, depth_cells), jnp.float32)
    for step in range(STEPS):
        extended = extend(
            (tangent - step_size * jnp.sum(velocity * gradients[step], axis=0))[None]
        )[0]
        windows = cut_windows(extended, brick_rows)
        pull_outbox = jnp.take(windows, send_flat, axis=0).reshape(
            peer_count, CAP, BX + 3, BY + 3, depth_cells
        )
        pull_inbox = lax.all_to_all(
            pull_outbox, "gy", split_axis=0, concat_axis=0, tiled=True
        ).reshape(slot_count, BX + 3, BY + 3, depth_cells)
        chosen = jnp.take(pull_inbox, pull_flat, axis=0)
        tangent = (
            interpolate(chosen, weight_rows, weight_cols, weight_depth)
            .reshape(brick_rows, brick_cols, BX, BY, depth_cells)
            .transpose(0, 2, 1, 3, 4)
            .reshape(rows_dev, cols_dev, depth_cells)
        )
    adjoint = tangent
    force = jnp.zeros((3, rows_dev, cols_dev, depth_cells), jnp.float32)
    for step in reversed(range(STEPS)):
        adjoint_windows = interpolate_adjoint(
            adjoint.reshape(brick_rows, BX, brick_cols, BY, depth_cells)
            .transpose(0, 2, 1, 3, 4)
            .reshape(bricks, BX, BY, depth_cells),
            weight_rows,
            weight_cols,
            weight_depth,
        )
        outbox = (
            jnp.zeros((slot_count, BX + 3, BY + 3, depth_cells), jnp.float32)
            .at[pull_flat]
            .set(adjoint_windows)
            .reshape(peer_count, CAP, BX + 3, BY + 3, depth_cells)
        )
        inbox = lax.all_to_all(outbox, "gy", split_axis=0, concat_axis=0, tiled=True).reshape(
            slot_count, BX + 3, BY + 3, depth_cells
        )
        collected = jnp.einsum("ks,sabz->kabz", selector, inbox, precision=high)
        accumulate = place_windows(
            collected, brick_rows, brick_cols, rows_dev, cols_dev, depth_cells
        )
        adjoint = fold_margins(accumulate, rows_dev, cols_dev, depth_cells)
        force = force - step_size * adjoint[None] * gradients[step]
    return force


def solution(mesh):
    return jax.shard_map(
        body,
        mesh=mesh,
        in_specs=(
            P(None, "gx", "gy", None),
            P(None, "gx", "gy", None),
            P("gx", "gy"),
            P("gx", "gy", None, None),
            P(None, "gx", "gy"),
        ),
        out_specs=P(None, "gx", "gy", None),
        check_vma=False,
    )
```

profile of v0, /device:TPU:0, one launch (start us, length us, event | category | flops | bytes accessed | tf_op | source)
XLA Modules:
  0.0 665.0 jit_solution(8308263304278767041)
XLA Ops:
  20.7 5.3 collective-permute-start.2
  29.3 5.8 collective-permute-done.3
  44.1 5.5 collective-permute-start.7
  53.0 4.0 gather_fusion
  56.9 6.7 %broadcast_select_fusion.1 = f32[32,19,19,128]{3,2,1,0:T(8,128)} fusion(f32[32,19,19,128]{3,2,1,0:T(8,128)} %gather_fusion, pred[32]{0:T(512)(128)(4,1)S(1)} %broadcast_compare_fusion), kind=kLoop, calls=%fused_computation.8 | loop fusion | flops 1478656 | bytes 11829280 | tf_op jit(solution)/shard_map/jit(_take)/select_n | solution.py:160
  63.6 8.8 %copy.112 = f32[16,2,19,19,128]{4,1,3,2,0:T(2,128)} copy(f32[16,2,19,19,128]{4,3,2,1,0:T(8,128)} %bitcast.454) | data formatting | bytes 11829248 | tf_op jit(solution)/shard_map/reshape | solution.py:160
  72.4 7.1 %all-to-all-start = ((f32[16,2,19,19,128]{4,1,3,2,0:T(2,128)}), f32[16,2,19,19,128]{4,1,3,2,0:T(2,128)}, u32[]{:S(2)}, u32[]{:S(2)}) async-start(f32[16,2,19,19,128]{4,1,3,2,0:T(2,128)} %copy.112), calls=%async_computation | async-start | bytes 11829248 | tf_op jit(solution)/shard_map/all_to_all | solution.py:163
  79.9 92.3 %all-to-all-done = f32[16,2,19,19,128]{4,1,3,2,0:T(2,128)} async-done(((f32[16,2,19,19,128]{4,1,3,2,0:T(2,128)}), f32[16,2,19,19,128]{4,1,3,2,0:T(2,128)}, u32[]{:S(2)}, u32[]{:S(2)}) %all-to-all-start) | async-done | bytes 5914656 | tf_op jit(solution)/shard_map/all_to_all | solution.py:163
  172.2 6.1 copy.113
  178.3 6.4 copy.114
  184.7 3.8 gather_fusion.1
  199.8 16.9 %collective-permute-start.11 = (f32[1,100,2,128]{3,2,1,0:T(2,128)S(1)}, f32[1,100,2,128]{3,2,1,0:T(2,128)S(1)}, u32[]{:S(2)}, u32[]{:S(2)}) collective-permute-start(f32[1,100,2,128]{3,2,1,0:T(2,128)S(1)} %get-tuple-element.571), channel_id=1, source_target_pairs={{1,0},{2,1},{3,2},{4,3},{5,4},{6,5},{7,6},{8,7},{9,8},{10,9},{11,1... | collective-permute-start | bytes 307208 | tf_op jit(solution)/shard_map/ppermute | solution.py:22
  219.3 4.0 gather_fusion.2
  223.2 6.7 %broadcast_select_fusion = f32[32,19,19,128]{3,2,1,0:T(8,128)} fusion(f32[32,19,19,128]{3,2,1,0:T(8,128)} %gather_fusion.2, pred[32]{0:T(512)(128)(4,1)S(1)} %broadcast_compare_fusion), kind=kLoop, calls=%fused_computation.7 | loop fusion | flops 1478656 | bytes 11829280 | tf_op jit(solution)/shard_map/jit(_take)/select_n | solution.py:160
  229.9 8.8 %copy.117 = f32[16,2,19,19,128]{4,1,3,2,0:T(2,128)} copy(f32[16,2,19,19,128]{4,3,2,1,0:T(8,128)} %bitcast.453) | data formatting | bytes 11829248 | tf_op jit(solution)/shard_map/reshape | solution.py:160
  238.7 12.7 %all-to-all-start.1 = ((f32[16,2,19,19,128]{4,1,3,2,0:T(2,128)}), f32[16,2,19,19,128]{4,1,3,2,0:T(2,128)}, u32[]{:S(2)}, u32[]{:S(2)}) async-start(f32[16,2,19,19,128]{4,1,3,2,0:T(2,128)} %copy.117), calls=%async_computation.1 | async-start | bytes 11829248 | tf_op jit(solution)/shard_map/all_to_all | solution.py:163
  251.4 82.3 %all-to-all-done.1 = f32[16,2,19,19,128]{4,1,3,2,0:T(2,128)} async-done(((f32[16,2,19,19,128]{4,1,3,2,0:T(2,128)}), f32[16,2,19,19,128]{4,1,3,2,0:T(2,128)}, u32[]{:S(2)}, u32[]{:S(2)}) %all-to-all-start.1) | async-done | bytes 5914656 | tf_op jit(solution)/shard_map/all_to_all | solution.py:163
  333.7 6.1 copy.118
  339.7 6.4 copy.119
  346.2 3.8 gather_fusion.3
  368.2 8.8 %copy.124 = f32[16,2,19,19,128]{4,1,3,2,0:T(2,128)} copy(f32[16,2,19,19,128]{4,3,2,1,0:T(8,128)} %bitcast.452) | data formatting | bytes 11829248 | tf_op jit(solution)/shard_map/reshape | solution.py:188
  377.0 27.7 %all-to-all-start.2 = ((f32[16,2,19,19,128]{4,1,3,2,0:T(2,128)}), f32[16,2,19,19,128]{4,1,3,2,0:T(2,128)}, u32[]{:S(2)}, u32[]{:S(2)}) async-start(f32[16,2,19,19,128]{4,1,3,2,0:T(2,128)} %copy.124), calls=%async_computation.2 | async-start | bytes 11829248 | tf_op jit(solution)/shard_map/all_to_all | solution.py:190
  406.7 91.5 %all-to-all-done.2 = f32[16,2,19,19,128]{4,1,3,2,0:T(2,128)} async-done(((f32[16,2,19,19,128]{4,1,3,2,0:T(2,128)}), f32[16,2,19,19,128]{4,1,3,2,0:T(2,128)}, u32[]{:S(2)}, u32[]{:S(2)}) %all-to-all-start.2) | async-done | bytes 5914656 | tf_op jit(solution)/shard_map/all_to_all | solution.py:190
  498.2 6.1 copy.125
  516.3 5.3 collective-permute-start.15
  521.6 4.8 collective-permute-done.14
  542.4 6.2 copy.133
  548.5 79.5 %all_to_all.20 = f32[16,2,19,19,128]{4,1,3,2,0:T(2,128)} all-to-all(f32[16,2,19,19,128]{4,1,3,2,0:T(2,128)S(1)} %copy.133), channel_id=1, replica_groups=mesh['gx'=8,'gy'=16] {'gy'}, dimensions={0} | all-to-all | bytes 11829248 | tf_op jit(solution)/shard_map/all_to_all | solution.py:190
  628.0 6.1 copy.134
  646.5 4.9 collective-permute-start.19
  651.4 4.8 collective-permute-done.18
  660.6 4.2 multiply_subtract_fusion
  (208 shorter events, 114.8 us)
Async XLA Ops:
  0.8 19.5 %collective-permute-start.1 = (f32[2,2,16,128]{3,2,1,0:T(8,128)S(1)}, f32[2,2,16,128]{3,2,1,0:T(8,128)S(1)}, u32[]{:S(2)}, u32[]{:S(2)}) collective-permute-start(f32[2,2,16,128]{3,2,1,0:T(8,128)S(1)} %get-tuple-element.553), channel_id=1, source_target_pairs={{0,16},{16,32},{32,48},{48,64},{64,80},{80,96},{96,112},{112,0},{1... | collective-permute-start | bytes 98312 | tf_op jit(solution)/shard_map/ppermute | solution.py:20
  0.8 7.2 %copy-start.1 = (f32[2,96,16,128]{3,2,1,0:T(8,128)S(1)}, f32[2,96,16,128]{3,2,1,0:T(8,128)}, u32[]{:S(2)}) copy-start(f32[2,96,16,128]{3,2,1,0:T(8,128)} %param.98) | copy-start | bytes 4718596
  0.8 19.5 %collective-permute-start = (f32[2,2,16,128]{3,2,1,0:T(8,128)S(1)}, f32[2,2,16,128]{3,2,1,0:T(8,128)S(1)}, u32[]{:S(2)}, u32[]{:S(2)}) collective-permute-start(f32[2,2,16,128]{3,2,1,0:T(8,128)S(1)} %get-tuple-element.552), channel_id=1, source_target_pairs={{16,0},{32,16},{48,32},{64,48},{80,64},{96,80},{112,96},{0,112},{1... | collective-permute-start | bytes 98312 | tf_op jit(solution)/shard_map/ppermute | solution.py:22
  16.4 3.7 copy-start.9
  20.3 484.0 %copy-start.4 = (s32[32]{0:T(128)}, s32[32]{0:T(128)S(1)}, u32[]{:S(2)}) copy-start(s32[32]{0:T(128)S(1)} %eq.198) | copy-start | bytes 388
  20.7 8.6 %collective-permute-start.2 = (f32[2,100,2,128]{3,2,1,0:T(2,128)S(1)}, f32[2,100,2,128]{3,2,1,0:T(2,128)S(1)}, u32[]{:S(2)}, u32[]{:S(2)}) collective-permute-start(f32[2,100,2,128]{3,2,1,0:T(2,128)S(1)} %get-tuple-element.548), channel_id=1, source_target_pairs={{1,0},{2,1},{3,2},{4,3},{5,4},{6,5},{7,6},{8,7},{9,8},{10,9},{11,1... | collective-permute-start | bytes 614408 | tf_op jit(solution)/shard_map/ppermute | solution.py:22
  26.0 9.1 %collective-permute-start.3 = (f32[2,100,2,128]{3,2,1,0:T(2,128)S(1)}, f32[2,100,2,128]{3,2,1,0:T(2,128)S(1)}, u32[]{:S(2)}, u32[]{:S(2)}) collective-permute-start(f32[2,100,2,128]{3,2,1,0:T(2,128)S(1)} %get-tuple-element.549), channel_id=1, source_target_pairs={{0,1},{1,2},{2,3},{3,4},{4,5},{5,6},{6,7},{7,8},{8,9},{9,10},{10,1... | collective-permute-start | bytes 614408 | tf_op jit(solution)/shard_map/ppermute | solution.py:20
  39.5 4.4 collective-permute-start.4
  39.5 4.4 collective-permute-start.5
  44.0 8.6 %collective-permute-start.6 = (f32[1,100,2,128]{3,2,1,0:T(2,128)S(1)}, f32[1,100,2,128]{3,2,1,0:T(2,128)S(1)}, u32[]{:S(2)}, u32[]{:S(2)}) collective-permute-start(f32[1,100,2,128]{3,2,1,0:T(2,128)S(1)} %get-tuple-element.572), channel_id=1, source_target_pairs={{0,1},{1,2},{2,3},{3,4},{4,5},{5,6},{6,7},{7,8},{8,9},{9,10},{10,1... | collective-permute-start | bytes 307208 | tf_op jit(solution)/shard_map/ppermute | solution.py:20
  44.1 8.5 %collective-permute-start.7 = (f32[1,100,2,128]{3,2,1,0:T(2,128)S(1)}, f32[1,100,2,128]{3,2,1,0:T(2,128)S(1)}, u32[]{:S(2)}, u32[]{:S(2)}) collective-permute-start(f32[1,100,2,128]{3,2,1,0:T(2,128)S(1)} %get-tuple-element.573), channel_id=1, source_target_pairs={{1,0},{2,1},{3,2},{4,3},{5,4},{6,5},{7,6},{8,7},{9,8},{10,9},{11,1... | collective-permute-start | bytes 307208 | tf_op jit(solution)/shard_map/ppermute | solution.py:22
  72.4 7.2 %copy-start.12 = (s32[6,1]{0,1:T(1,128)S(1)}, s32[6,1]{0,1:T(1,128)}, u32[]{:S(2)}) copy-start(s32[6,1]{0,1:T(1,128)} %param.99) | copy-start | bytes 76
  72.4 7.2 %copy-start.8 = (s32[3,6,1]{1,2,0:T(1,128)S(1)}, s32[3,6,1]{1,2,0:T(1,128)}, u32[]{:S(2)}) copy-start(s32[3,6,1]{1,2,0:T(1,128)} %param.101) | copy-start | bytes 220
  72.4 99.8 %all-to-all-start = ((f32[16,2,19,19,128]{4,1,3,2,0:T(2,128)}), f32[16,2,19,19,128]{4,1,3,2,0:T(2,128)}, u32[]{:S(2)}, u32[]{:S(2)}) async-start(f32[16,2,19,19,128]{4,1,3,2,0:T(2,128)} %copy.112), calls=%async_computation | async-start | bytes 11829248 | tf_op jit(solution)/shard_map/all_to_all | solution.py:163
  194.0 4.4 collective-permute-start.8
  194.0 5.6 collective-permute-start.9
  199.7 16.9 %collective-permute-start.10 = (f32[1,100,2,128]{3,2,1,0:T(2,128)S(1)}, f32[1,100,2,128]{3,2,1,0:T(2,128)S(1)}, u32[]{:S(2)}, u32[]{:S(2)}) collective-permute-start(f32[1,100,2,128]{3,2,1,0:T(2,128)S(1)} %get-tuple-element.570), channel_id=1, source_target_pairs={{0,1},{1,2},{2,3},{3,4},{4,5},{5,6},{6,7},{7,8},{8,9},{9,10},{10,1... | collective-permute-start | bytes 307208 | tf_op jit(solution)/shard_map/ppermute | solution.py:20
  199.8 19.1 %collective-permute-start.11 = (f32[1,100,2,128]{3,2,1,0:T(2,128)S(1)}, f32[1,100,2,128]{3,2,1,0:T(2,128)S(1)}, u32[]{:S(2)}, u32[]{:S(2)}) collective-permute-start(f32[1,100,2,128]{3,2,1,0:T(2,128)S(1)} %get-tuple-element.571), channel_id=1, source_target_pairs={{1,0},{2,1},{3,2},{4,3},{5,4},{6,5},{7,6},{8,7},{9,8},{10,9},{11,1... | collective-permute-start | bytes 307208 | tf_op jit(solution)/shard_map/ppermute | solution.py:22
  238.7 95.0 %all-to-all-start.1 = ((f32[16,2,19,19,128]{4,1,3,2,0:T(2,128)}), f32[16,2,19,19,128]{4,1,3,2,0:T(2,128)}, u32[]{:S(2)}, u32[]{:S(2)}) async-start(f32[16,2,19,19,128]{4,1,3,2,0:T(2,128)} %copy.117), calls=%async_computation.1 | async-start | bytes 11829248 | tf_op jit(solution)/shard_map/all_to_all | solution.py:163
  251.3 113.5 %copy-start.6 = (s32[6]{0:T(128)}, s32[6]{0:T(128)S(1)}, u32[]{:S(2)}) copy-start(s32[6]{0:T(128)S(1)} %fusion.201) | copy-start | bytes 76
  377.0 28.3 %copy-start.11 = (s32[3]{0:T(128)S(1)}, s32[3]{0:T(128)}, u32[]{:S(2)}) copy-start(s32[3]{0:T(128)} %constant.1250.clone.1) | copy-start | bytes 40
  377.0 29.0 %copy-start.10 = (s32[4]{0:T(128)S(1)}, s32[4]{0:T(128)}, u32[]{:S(2)}) copy-start(s32[4]{0:T(128)} %constant.1247.clone.1) | copy-start | bytes 52
  377.0 121.3 %all-to-all-start.2 = ((f32[16,2,19,19,128]{4,1,3,2,0:T(2,128)}), f32[16,2,19,19,128]{4,1,3,2,0:T(2,128)}, u32[]{:S(2)}, u32[]{:S(2)}) async-start(f32[16,2,19,19,128]{4,1,3,2,0:T(2,128)} %copy.124), calls=%async_computation.2 | async-start | bytes 11829248 | tf_op jit(solution)/shard_map/all_to_all | solution.py:190
  511.2 4.7 collective-permute-start.12
  511.3 4.7 collective-permute-start.13
  516.2 10.2 %collective-permute-start.14 = (f32[3,100,2,128]{3,2,1,0:T(2,128)S(1)}, f32[3,100,2,128]{3,2,1,0:T(2,128)S(1)}, u32[]{:S(2)}, u32[]{:S(2)}) collective-permute-start(f32[3,100,2,128]{3,2,1,0:T(2,128)S(1)} %get-tuple-element.543), channel_id=1, source_target_pairs={{0,1},{1,2},{2,3},{3,4},{4,5},{5,6},{6,7},{7,8},{8,9},{9,10},{10,1... | collective-permute-start | bytes 921608 | tf_op jit(solution)/shard_map/ppermute | solution.py:20
  516.3 10.3 %collective-permute-start.15 = (f32[3,100,2,128]{3,2,1,0:T(2,128)S(1)}, f32[3,100,2,128]{3,2,1,0:T(2,128)S(1)}, u32[]{:S(2)}, u32[]{:S(2)}) collective-permute-start(f32[3,100,2,128]{3,2,1,0:T(2,128)S(1)} %get-tuple-element.542), channel_id=1, source_target_pairs={{1,0},{2,1},{3,2},{4,3},{5,4},{6,5},{7,6},{8,7},{9,8},{10,9},{11,1... | collective-permute-start | bytes 921608 | tf_op jit(solution)/shard_map/ppermute | solution.py:22
  628.0 6.1 copy-start.5
  641.0 4.7 collective-permute-start.16
  641.0 4.7 collective-permute-start.17
  646.0 10.2 %collective-permute-start.18 = (f32[3,100,2,128]{3,2,1,0:T(2,128)S(1)}, f32[3,100,2,128]{3,2,1,0:T(2,128)S(1)}, u32[]{:S(2)}, u32[]{:S(2)}) collective-permute-start(f32[3,100,2,128]{3,2,1,0:T(2,128)S(1)} %get-tuple-element.541), channel_id=1, source_target_pairs={{0,1},{1,2},{2,3},{3,4},{4,5},{5,6},{6,7},{7,8},{8,9},{9,10},{10,1... | collective-permute-start | bytes 921608 | tf_op jit(solution)/shard_map/ppermute | solution.py:20
  646.5 9.8 %collective-permute-start.19 = (f32[3,100,2,128]{3,2,1,0:T(2,128)S(1)}, f32[3,100,2,128]{3,2,1,0:T(2,128)S(1)}, u32[]{:S(2)}, u32[]{:S(2)}) collective-permute-start(f32[3,100,2,128]{3,2,1,0:T(2,128)S(1)} %get-tuple-element.540), channel_id=1, source_target_pairs={{1,0},{2,1},{3,2},{4,3},{5,4},{6,5},{7,6},{8,7},{9,8},{10,9},{11,1... | collective-permute-start | bytes 921608 | tf_op jit(solution)/shard_map/ppermute | solution.py:22
  (4 other events, 8.4 us)
where the time goes:
time: 666 us; the launch traced here: 665 us
  waiting for transfers between devices  296 us (44%)
  local copies, waits for them, and re-layouts  125 us (19%)
  starting transfers between devices  102 us (15%)
  blocking collectives  79.5 us (12%)
  other arithmetic  35.2 us (5%)
  matrix products  26.5 us (4%)
    all_to_all x2, waiting for transfers between devices, body(): lax.all_to_all(pull_outbox, 'gy', split_axis=0, concat_axis=0, tiled=True)  175 us
    all_to_all x1, waiting for transfers between devices, body(): lax.all_to_all(outbox, 'gy', split_axis=0, concat_axis=0, tiled=True)  91.5 us
    all_to_all x1, blocking collectives, body(): lax.all_to_all(outbox, 'gy', split_axis=0, concat_axis=0, tiled=True)  79.5 us
    ppermute x10, starting transfers between devices, with_halo(): lax.ppermute(head, axis, [((i + 1) % count, i) for i in range(count)])  53.2 us
    all_to_all x1, starting transfers between devices, body(): lax.all_to_all(outbox, 'gy', split_axis=0, concat_axis=0, tiled=True)  27.7 us
    ppermute x10, waiting for transfers between devices, with_halo(): lax.ppermute(tail, axis, [(i, (i + 1) % count) for i in range(count)])  23.1 us
    all_to_all x2, starting transfers between devices, body(): lax.all_to_all(pull_outbox, 'gy', split_axis=0, concat_axis=0, tiled=True)  19.8 us
    reshape x2, local copies, waits for them, and re-layouts, body(): jnp.take(windows, send_flat, axis=0)  17.5 us
  transfers between devices with their start and end apart: 23, of which 14 were waited for; matrix products, arithmetic and copies ran while one was open for 3% of the time, Pallas kernels for 0%

commit v1 on v0

v1 whole, which is shorter than its diff:
```python
import functools

import jax
import jax.numpy as jnp
import numpy as np
from jax import lax
from jax.experimental import pallas as pl
from jax.experimental.pallas import tpu as pltpu
from jax.sharding import PartitionSpec as P

QF = 8
PEERS = 16
RB = 12
BRICKS = 6


def weights_of(f):
    return np.array(
        [
            -f * (f - 1.0) * (f - 2.0) / 6.0,
            (f + 1.0) * (f - 1.0) * (f - 2.0) / 2.0,
            -(f + 1.0) * f * (f - 2.0) / 2.0,
            (f + 1.0) * f * (f - 1.0) / 6.0,
        ]
    )


WEIGHTS = np.stack([weights_of(k / QF) for k in range(QF)])
PAIRS = np.stack([[np.dot(w[: 4 - d], w[d:]) for d in range(4)] for w in WEIGHTS])

VMEM = pl.BlockSpec(memory_space=pltpu.VMEM)
SMEM = pl.BlockSpec(memory_space=pltpu.SMEM)
F32 = jnp.float32


def params(mib=48):
    return pltpu.CompilerParams(vmem_limit_bytes=mib * 1024 * 1024)


def turned_shape(lead=PEERS):
    return jax.ShapeDtypeStruct((lead, RB, 8, 128), F32)


def gradients(st, top, bottom, left, right, rb, k):
    rows = pl.ds(rb * 8, 8)
    x = st[k, rows]
    before = st[k, jnp.maximum(rb * 8 - 1, 0)]
    before = jnp.where(rb == 0, top[k], before)
    after = st[k, jnp.minimum(rb * 8 + 8, 95)]
    after = jnp.where(rb == RB - 1, bottom[k], after)
    up = jnp.concatenate([x[1:], after[None]], axis=0)
    down = jnp.concatenate([before[None], x[:-1]], axis=0)
    col = lax.broadcasted_iota(jnp.int32, x.shape, 1)
    lo = left[k, rows][:, None, :]
    hi = right[k, rows][:, None, :]
    nxt = jnp.where(col == 15, hi, pltpu.roll(x, 15, 1))
    prv = jnp.where(col == 0, lo, pltpu.roll(x, 1, 1))
    return (
        (up - down) * 0.5,
        (nxt - prv) * 0.5,
        (pltpu.roll(x, 127, 2) - pltpu.roll(x, 1, 2)) * 0.5,
    )


def source_kernel(k, v, st, top, bottom, left, right, out):
    g = gradients(st, top, bottom, left, right, pl.program_id(0), k)
    a = -0.5 * (v[0] * g[0] + v[1] * g[1] + v[2] * g[2])
    out[:, 0] = a.reshape(128, 128).T.reshape(PEERS, 8, 128)


def whole(shape):
    return pl.BlockSpec(shape, lambda i: (0,) * len(shape))


STATE_SPECS = [
    whole((2, 96, 16, 128)),
    whole((2, 16, 128)),
    whole((2, 16, 128)),
    whole((2, 96, 128)),
    whole((2, 96, 128)),
]
NATURAL3 = pl.BlockSpec((3, 8, 16, 128), lambda i: (0, i, 0, 0))
TURNED = pl.BlockSpec((PEERS, 1, 8, 128), lambda i: (0, i, 0, 0))


def source(k, velocity, state_args):
    return pl.pallas_call(
        functools.partial(source_kernel, k),
        grid=(RB,),
        in_specs=[NATURAL3] + STATE_SPECS,
        out_specs=TURNED,
        out_shape=turned_shape(),
        compiler_params=params(),
        name="source%d" % k,
    )(velocity, *state_args)


def force_kernel(adj1, adj0, st, top, bottom, left, right, out):
    rb = pl.program_id(0)
    b1 = (adj1[:, 0].reshape(128, 128).T * -0.5).reshape(8, 16, 128)
    b0 = (adj0[:, 0].reshape(128, 128).T * -0.5).reshape(8, 16, 128)
    g1 = gradients(st, top, bottom, left, right, rb, 1)
    g0 = gradients(st, top, bottom, left, right, rb, 0)
    for c in range(3):
        out[c] = b1 * g1[c] + b0 * g0[c]


def force(adj1, adj0, state_args):
    return pl.pallas_call(
        force_kernel,
        grid=(RB,),
        in_specs=[TURNED, TURNED] + STATE_SPECS,
        out_specs=NATURAL3,
        out_shape=jax.ShapeDtypeStruct((3, 96, 16, 128), F32),
        compiler_params=params(),
        name="force",
    )(adj1, adj0, *state_args)


def lanes():
    return lax.broadcasted_iota(jnp.int32, (8, 128), 1)


def column_taps(x):
    col = lax.broadcasted_iota(jnp.int32, x.shape, 2) % 16
    up = pltpu.roll(x, 16, 2)
    dn = pltpu.roll(x, 112, 2)
    after = jnp.concatenate([up[1:], up[:1]], axis=0)
    before = jnp.concatenate([dn[-1:], dn[:-1]], axis=0)
    return (
        pltpu.roll(jnp.where(col == 15, before, x), 1, 2),
        x,
        pltpu.roll(jnp.where(col == 0, after, x), 127, 2),
        pltpu.roll(jnp.where(col < 2, after, x), 126, 2),
    )


def column_taps_adjoint(t0, t1, t2, t3):
    col = lax.broadcasted_iota(jnp.int32, t1.shape, 2) % 16
    p0 = pltpu.roll(t0, 127, 2)
    p2 = pltpu.roll(t2, 1, 2)
    p3 = pltpu.roll(t3, 2, 2)
    own = t1 + jnp.where(col == 15, 0.0, p0) + jnp.where(col == 0, 0.0, p2) + jnp.where(col < 2, 0.0, p3)
    after = jnp.where(col == 0, p2, 0.0) + jnp.where(col < 2, p3, 0.0)
    before = jnp.where(col == 15, p0, 0.0)
    after = pltpu.roll(after, 112, 2)
    before = pltpu.roll(before, 16, 2)
    after = jnp.concatenate([after[-1:], after[:-1]], axis=0)
    before = jnp.concatenate([before[1:], before[:1]], axis=0)
    return own + after + before


def fill_taps(taps, e, x):
    for t, y in enumerate(column_taps(x)):
        taps[t, :, e] = y


def brick_plan(tab, wt, d, k):
    p = tab[d, 32 + k]
    s = p // 2
    l = tab[s, d * 2 + p % 2]
    wr = [wt[tab[d, 38 + k], t] for t in range(4)]
    wc = [wt[tab[d, 44 + k], t] for t in range(4)]
    return s, l, wr, wc


def brick_forward(taps, s, l, wr, wc):
    lane = lanes()
    c = []
    for i in range(4):
        e = 2 * l + i
        acc = wc[0] * taps[0, s, e]
        for t in range(1, 4):
            acc = acc + wc[t] * taps[t, s, e]
        c.append(acc)
    outs = []
    for h in range(2):
        prv, cur, nxt = c[h], c[h + 1], c[h + 2]
        outs.append(
            wr[0] * pltpu.roll(jnp.where(lane >= 112, prv, cur), 16, 1)
            + wr[1] * cur
            + wr[2] * pltpu.roll(jnp.where(lane < 16, nxt, cur), 112, 1)
            + wr[3] * pltpu.roll(jnp.where(lane < 32, nxt, cur), 96, 1)
        )
    return outs


def brick_adjoint(acc, s, l, wr, wc, v):
    lane = lanes()
    zero = jnp.zeros((8, 128), F32)
    c = [zero, zero, zero, zero]
    for h in range(2):
        p0 = wr[0] * pltpu.roll(v[h], 112, 1)
        p2 = wr[2] * pltpu.roll(v[h], 16, 1)
        p3 = wr[3] * pltpu.roll(v[h], 32, 1)
        c[h] = c[h] + jnp.where(lane >= 112, p0, 0.0)
        c[h + 1] = (
            c[h + 1]
            + wr[1] * v[h]
            + jnp.where(lane >= 112, 0.0, p0)
            + jnp.where(lane < 16, 0.0, p2)
            + jnp.where(lane < 32, 0.0, p3)
        )
        c[h + 2] = c[h + 2] + jnp.where(lane < 16, p2, 0.0) + jnp.where(lane < 32, p3, 0.0)
    for i in range(4):
        e = 2 * l + i
        for t in range(4):
            acc[t, s, e] = acc[t, s, e] + wc[t] * c[i]


def pull_kernel(tab, wt, x, prv, nxt, out, taps):
    fill_taps(taps, 0, prv[...])
    fill_taps(taps, RB + 1, nxt[...])

    @pl.loop(0, RB)
    def _(rb):
        fill_taps(taps, rb + 1, x[:, rb])

    @pl.loop(0, PEERS)
    def _(d):
        for k in range(BRICKS):
            o = brick_forward(taps, *brick_plan(tab, wt, d, k))
            for h in range(2):
                out[d, 2 * k + h] = o[h]


TAPS = pltpu.VMEM((4, PEERS, RB + 2, 8, 128), F32)


def pull(tab, wt, x, prv, nxt):
    return pl.pallas_call(
        pull_kernel,
        in_specs=[SMEM, SMEM, VMEM, VMEM, VMEM],
        out_specs=VMEM,
        out_shape=turned_shape(),
        scratch_shapes=[TAPS],
        compiler_params=params(),
        name="pull",
    )(tab, wt, x, prv, nxt)


def clear(acc):
    @pl.loop(0, RB + 2)
    def _(e):
        acc[:, :, e] = jnp.zeros((4, PEERS, 8, 128), F32)


def spill(acc, out, lo, hi):
    def gather(e):
        return column_taps_adjoint(*[acc[t, :, e] for t in range(4)])

    lo[...] = gather(0)
    hi[...] = gather(RB + 1)

    @pl.loop(0, RB)
    def _(rb):
        out[:, rb] = gather(rb + 1)


def push_kernel(tab, wt, v, out, lo, hi, acc):
    clear(acc)

    @pl.loop(0, PEERS)
    def _(d):
        for k in range(BRICKS):
            brick_adjoint(acc, *brick_plan(tab, wt, d, k), [v[d, 2 * k], v[d, 2 * k + 1]])

    spill(acc, out, lo, hi)


EDGE = jax.ShapeDtypeStruct((PEERS, 8, 128), F32)


def push(tab, wt, v):
    return pl.pallas_call(
        push_kernel,
        in_specs=[SMEM, SMEM, VMEM],
        out_specs=[VMEM, VMEM, VMEM],
        out_shape=[turned_shape(), EDGE, EDGE],
        scratch_shapes=[TAPS],
        compiler_params=params(),
        name="push",
    )(tab, wt, v)


def normal_kernel(tab, wt, kt, x, prv, nxt, out, lo, hi, taps, acc):
    clear(acc)
    for q in range(2):
        fill_taps(taps.at[q], 0, prv[:, q])
        fill_taps(taps.at[q], RB + 1, nxt[:, q])

    @pl.loop(0, RB)
    def _(rb):
        for q in range(2):
            fill_taps(taps.at[q], rb + 1, x[:, q, rb])

    @pl.loop(0, PEERS)
    def _(d):
        sub = lax.broadcasted_iota(jnp.int32, (8, 128), 0)
        for k in range(BRICKS):
            plan = brick_plan(tab, wt, d, k)
            f = tab[d, 50 + k] % QF
            t0 = brick_forward(taps.at[0], *plan)
            t1 = brick_forward(taps.at[1], *plan)
            v = []
            for h in range(2):

                def plane(a):
                    return pltpu.roll(jnp.where(sub >= a, t0[h], t1[h]), 8 - a, 0)

                y = kt[f, 0] * plane(4)
                for dd in range(1, 4):
                    y = y + kt[f, dd] * (plane(4 - dd) + plane(4 + dd))
                v.append(y)
            brick_adjoint(acc, *plan, v)

    spill(acc, out, lo, hi)


def normal(tab, wt, kt, x, prv, nxt):
    return pl.pallas_call(
        normal_kernel,
        in_specs=[SMEM, SMEM, SMEM, VMEM, VMEM, VMEM],
        out_specs=[VMEM, VMEM, VMEM],
        out_shape=[turned_shape(), EDGE, EDGE],
        scratch_shapes=[pltpu.VMEM((2, 4, PEERS, RB + 2, 8, 128), F32), TAPS],
        compiler_params=params(),
        name="normal",
    )(tab, wt, kt, x, prv, nxt)


def depth_matrix(wt, q, transpose):
    n = q // QF
    f = q % QF
    i = lax.broadcasted_iota(jnp.int32, (128, 128), 0)
    j = lax.broadcasted_iota(jnp.int32, (128, 128), 1)
    off = (i - j if transpose else j - i) + (257 - n)
    off = jnp.bitwise_and(off, 127)
    w = jnp.zeros((128, 128), F32)
    for m in range(4):
        w = jnp.where(off == m, wt[f, m], w)
    return w


def depth_product(wt, q, transpose, r, k):
    w = depth_matrix(wt, q, transpose)
    pair = [r[:, 2 * k + h].reshape(128, 128) for h in range(2)]
    y = jnp.dot(w, jnp.concatenate(pair, axis=1), precision=lax.Precision.HIGHEST, preferred_element_type=F32)
    return y[:, :128], y[:, 128:]


def depth_kernel(code, wt, r, a, out):
    @pl.loop(0, BRICKS)
    def _(k):
        ys = depth_product(wt, code[k], False, r, k)
        for h in range(2):
            u = ys[h] + a[:, 2 * k + h].reshape(128, 128)
            tiles = pltpu.roll(u, 4, 0).reshape(PEERS, 8, 128)
            out[:, 0, 2 * k + h] = tiles
            out[:, 1, 2 * k + h] = jnp.concatenate([tiles[1:], tiles[:1]], axis=0)


def depth(code, wt, r, a):
    return pl.pallas_call(
        depth_kernel,
        in_specs=[SMEM, SMEM, VMEM, VMEM],
        out_specs=VMEM,
        out_shape=jax.ShapeDtypeStruct((PEERS, 2, RB, 8, 128), F32),
        compiler_params=params(),
        name="depth",
    )(code, wt, r, a)


def depth_adjoint_kernel(code, wt, r, out):
    @pl.loop(0, BRICKS)
    def _(k):
        ys = depth_product(wt, code[k], True, r, k)
        for h in range(2):
            out[:, 2 * k + h] = ys[h].reshape(PEERS, 8, 128)


def depth_adjoint(code, wt, r):
    return pl.pallas_call(
        depth_adjoint_kernel,
        in_specs=[SMEM, SMEM, VMEM],
        out_specs=VMEM,
        out_shape=turned_shape(),
        compiler_params=params(),
        name="depth_adjoint",
    )(code, wt, r)


def to_next(x, axis, count):
    return lax.ppermute(x, axis, [(i, (i + 1) % count) for i in range(count)])


def to_prev(x, axis, count):
    return lax.ppermute(x, axis, [((i + 1) % count, i) for i in range(count)])


def swap(x):
    return lax.all_to_all(x, "gy", split_axis=0, concat_axis=0, tiled=True)


def body(velocity, states, pull_plan, send_plan, codes):
    gx = lax.axis_size("gx")
    gy = lax.axis_size("gy")
    top = to_next(states[:, -1], "gx", gx)
    bottom = to_prev(states[:, 0], "gx", gx)
    left = to_next(states[:, :, -1], "gy", gy)
    right = to_prev(states[:, :, 0], "gy", gy)
    state_args = (states, top, bottom, left, right)
    wt = jnp.asarray(WEIGHTS, F32)
    kt = jnp.asarray(PAIRS, F32)
    code = codes[2].reshape(BRICKS)
    mine = jnp.concatenate(
        [send_plan.reshape(32), pull_plan.reshape(BRICKS), codes.reshape(3 * BRICKS), jnp.zeros((72,), jnp.int32)]
    )
    tab = swap(jnp.broadcast_to(mine, (PEERS, 128)))

    a0 = source(0, velocity, state_args)
    a1 = source(1, velocity, state_args)
    x = swap(a0)
    o = pull(tab, wt, x, to_next(x[:, RB - 1], "gx", gx), to_prev(x[:, 0], "gx", gx))
    u = swap(depth(code, wt, swap(o), a1))
    y, lo, hi = normal(tab, wt, kt, u, to_next(u[:, :, RB - 1], "gx", gx), to_prev(u[:, :, 0], "gx", gx))
    y = y.at[:, RB - 1].add(to_prev(lo, "gx", gx)).at[:, 0].add(to_next(hi, "gx", gx))
    adj1 = swap(y)
    v = swap(depth_adjoint(code, wt, adj1))
    y, lo, hi = push(tab, wt, v)
    y = y.at[:, RB - 1].add(to_prev(lo, "gx", gx)).at[:, 0].add(to_next(hi, "gx", gx))
    adj0 = swap(y)
    return force(adj1, adj0, state_args)


def solution(mesh):
    return jax.shard_map(
        body,
        mesh=mesh,
        in_specs=(
            P(None, "gx", "gy", None),
            P(None, "gx", "gy", None),
            P("gx", "gy"),
            P("gx", "gy", None, None),
            P(None, "gx", "gy"),
        ),
        out_specs=P(None, "gx", "gy", None),
        check_vma=False,
    )
```

time: 666 us -> 195 us (0.29)
  waiting for transfers between devices: 296 us -> 39.4 us
  local copies, waits for them, and re-layouts: 125 us -> 7.61 us
  starting transfers between devices: 102 us -> 21.3 us
  Pallas kernels: 0 us -> 43.4 us
  other arithmetic: 35.2 us -> 0.16 us
  matrix products: 26.5 us -> 0 us
    all_to_all x3 -> x2, waiting for transfers between devices: 266 us -> 19.8 us  [swap(): return lax.all_to_all(x, 'gy', split_axis=0, concat_axis=0, tiled=True)]
    reshape x6 -> x2, local copies, waits for them, and re-layouts: 45.3 us -> 0.17 us  [the longest x1 0.09 us: body(): send_plan.reshape(32)]
    pallas_call x0 -> x8, Pallas kernels: none -> 43.4 us  [the longest x1 12.8 us: normal(): pl.pallas_call(normal_kernel, in_specs=[SMEM, SMEM, SMEM, VMEM, VMEM, VME...]
    ppermute x20 -> x12, starting transfers between devices: 54.1 us -> 13.9 us  [the longest x6 11.7 us: to_prev(): return lax.ppermute(x, axis, [((i + 1) % count, i) for i in range(count)])]
    all_to_all x3 -> x2, starting transfers between devices: 47.5 us -> 7.37 us  [swap(): return lax.all_to_all(x, 'gy', split_axis=0, concat_axis=0, tiled=True)]
    dot_general x14 -> x0, matrix products: 26.5 us -> none  [the longest x2 6.23 us: interpolate_adjoint(): jnp.einsum('ncz,nabc->nabz', weight_depth, along_rows, precision=high)]
    all_to_all x4 -> x1, local copies, waits for them, and re-layouts: 24.3 us -> 0.17 us  [swap(): return lax.all_to_all(x, 'gy', split_axis=0, concat_axis=0, tiled=True)]
    gather x4 -> x0, local copies, waits for them, and re-layouts: 15.4 us -> none  [the longest x2 7.93 us: body(): jnp.take(windows, send_flat, axis=0)]
  transfers between devices with their start and end apart: 23 -> 14, of which waited for: 14 -> 10; matrix products, arithmetic and copies ran while one was open for 3% -> 1% of each run, Pallas kernels for 0% -> 1%
where the time goes in v1:
time: 195 us
  blocking collectives  82.5 us (42%)
  Pallas kernels  43.4 us (22%)
  waiting for transfers between devices  39.4 us (20%)
  starting transfers between devices  21.3 us (11%)
  local copies, waits for them, and re-layouts  7.61 us (4%)
    all_to_all x5, blocking collectives, swap(): return lax.all_to_all(x, 'gy', split_axis=0, concat_axis=0, tiled=True)  82.5 us
    all_to_all x2, waiting for transfers between devices, swap(): return lax.all_to_all(x, 'gy', split_axis=0, concat_axis=0, tiled=True)  19.8 us
    pallas_call x1, Pallas kernels, normal(): pl.pallas_call(normal_kernel, in_specs=[SMEM, SMEM, SMEM, VMEM, VMEM, VME...  12.8 us
    ppermute x6, waiting for transfers between devices, to_next(): return lax.ppermute(x, axis, [(i, (i + 1) % count) for i in range(count)])  12.5 us
    ppermute x6, starting transfers between devices, to_prev(): return lax.ppermute(x, axis, [((i + 1) % count, i) for i in range(count)])  11.7 us
    pallas_call x2, Pallas kernels, source(): pl.pallas_call(functools.partial(source_kernel, k), grid=(RB,), in_specs=...  7.62 us
    all_to_all x2, starting transfers between devices, swap(): return lax.all_to_all(x, 'gy', split_axis=0, concat_axis=0, tiled=True)  7.37 us
    pallas_call x1, Pallas kernels, pull(): pl.pallas_call(pull_kernel, in_specs=[SMEM, SMEM, VMEM, VMEM, VMEM], out_...  7.25 us
  transfers between devices with their start and end apart: 14, of which 10 were waited for; matrix products, arithmetic and copies ran while one was open for 1% of the time, Pallas kernels for 1%

profile of v1, /device:TPU:0, one launch (start us, length us, event | category | flops | bytes accessed | tf_op | source)
XLA Modules:
  0.0 194.5 jit_solution(3990286480965891765)
XLA Ops:
  0.0 1.5 fusion.4
  1.5 1.8 collective-permute-start.2
  3.3 3.7 %collective-permute-start.3 = (f32[2,96,128]{2,1,0:T(8,128)S(1)}, f32[2,96,128]{2,1,0:T(8,128)S(1)}, u32[]{:S(2)}, u32[]{:S(2)}) collective-permute-start(f32[2,96,128]{2,1,0:T(8,128)S(1)} %bitcast.51), channel_id=1, source_target_pairs={{1,0},{2,1},{3,2},{4,3},{5,4},{6,5},{7,6},{8,7},{9,8},{10,9},{11,1... | collective-permute-start | bytes 294920 | tf_op jit(solution)/shard_map/ppermute | solution.py:398
  7.7 3.2 %collective-permute-start.1 = (f32[2,16,128]{2,1,0:T(8,128)S(1)}, f32[2,16,128]{2,1,0:T(8,128)S(1)}, u32[]{:S(2)}, u32[]{:S(2)}) collective-permute-start(f32[2,16,128]{2,1,0:T(8,128)S(1)} %get-tuple-element.69), channel_id=1, source_target_pairs={{16,0},{32,16},{48,32},{64,48},{80,64},{96,80},{112,96},{0,112},{1... | collective-permute-start | bytes 49160 | tf_op jit(solution)/shard_map/ppermute | solution.py:398
  10.9 1.4 collective-permute-done.1.bottom
  12.4 2.9 %collective-permute-done.top = f32[2,16,128]{2,1,0:T(8,128)S(1)} collective-permute-done((f32[2,16,128]{2,1,0:T(8,128)S(1)}, f32[2,16,128]{2,1,0:T(8,128)S(1)}, u32[]{:S(2)}, u32[]{:S(2)}) %collective-permute-start) | collective-permute-done | bytes 16416 | tf_op jit(solution)/shard_map/ppermute | solution.py:394
  16.7 1.7 copy-done.2
  18.4 5.1 %source0.1 = f32[16,12,8,128]{3,2,1,0:T(8,128)} custom-call(f32[3,96,16,128]{3,2,1,0:T(8,128)S(1)} %copy-done.2, f32[2,96,16,128]{3,2,1,0:T(8,128)S(1)} %copy-done, f32[2,16,128]{2,1,0:T(8,128)S(1)} %collective-permute-done.top, f32[2,16,128]{2,1,0:T(8,128)S(1)} %collective-permute-done.1.bottom, f32[2,96,128]{2,1,0:T(8,128)S(1)} %collective-permute-done.2.left, ...), custom_call_target="tpu_custom_call" | custom-call | tf_op jit(solution)/shard_map/source0/pallas_call | solution.py:87
  23.5 3.8 %all-to-all-start.1 = ((f32[16,12,8,128]{3,2,1,0:T(8,128)}), f32[16,12,8,128]{3,2,1,0:T(8,128)S(1)}, u32[]{:S(2)}, u32[]{:S(2)}) async-start(f32[16,12,8,128]{3,2,1,0:T(8,128)} %source0.1), calls=%async_computation.1 | async-start | bytes 1572864 | tf_op jit(solution)/shard_map/all_to_all | solution.py:402
  27.6 11.2 %all-to-all-done.1.x = f32[16,12,8,128]{3,2,1,0:T(8,128)S(1)} async-done(((f32[16,12,8,128]{3,2,1,0:T(8,128)}), f32[16,12,8,128]{3,2,1,0:T(8,128)S(1)}, u32[]{:S(2)}, u32[]{:S(2)}) %all-to-all-start.1) | async-done | bytes 786464 | tf_op jit(solution)/shard_map/all_to_all | solution.py:402
  40.1 11.5 %all_to_all.38 = s32[16,1,128]{2,1,0:T(1,128)S(1)} all-to-all(s32[16,1,128]{2,1,0:T(1,128)S(1)} %broadcast_in_dim.7), channel_id=1, replica_groups=mesh['gx'=8,'gy'=16] {'gy'}, dimensions={0} | all-to-all | bytes 16384 | tf_op jit(solution)/shard_map/all_to_all | solution.py:402
  51.6 7.3 %pull.1 = f32[16,12,8,128]{3,2,1,0:T(8,128)} custom-call(s32[16,128]{1,0:T(8,128)S(1)} %bitcast.48, f32[8,4]{1,0:T(8,128)S(1)} %copy-done.4, f32[16,12,8,128]{3,2,1,0:T(8,128)S(1)} %all-to-all-done.1.x, f32[16,8,128]{2,1,0:T(8,128)S(1)} %collective-permute-done.4.prv, f32[16,8,128]{2,1,0:T(8,128)S(1)} %collective-permute-done.5.nxt), custom_call_target="tpu_custom_call" | custom-call | tf_op jit(solution)/shard_map/pull/pallas_call | solution.py:231
  58.9 3.6 %all-to-all-start.2 = ((f32[16,12,8,128]{3,2,1,0:T(8,128)}), f32[16,12,8,128]{3,2,1,0:T(8,128)S(1)}, u32[]{:S(2)}, u32[]{:S(2)}) async-start(f32[16,12,8,128]{3,2,1,0:T(8,128)} %pull.1), calls=%async_computation.2 | async-start | bytes 1572864 | tf_op jit(solution)/shard_map/all_to_all | solution.py:402
  62.5 1.7 copy-done.3
  64.2 2.5 %source1.1.a = f32[16,12,8,128]{3,2,1,0:T(8,128)S(1)} custom-call(f32[3,96,16,128]{3,2,1,0:T(8,128)S(1)} %copy-done.3, f32[2,96,16,128]{3,2,1,0:T(8,128)S(1)} %copy-done.1, f32[2,16,128]{2,1,0:T(8,128)S(1)} %collective-permute-done.top, f32[2,16,128]{2,1,0:T(8,128)S(1)} %collective-permute-done.1.bottom, f32[2,96,128]{2,1,0:T(8,128)S(1)} %collective-permute-done.2.left, ...), custom_call_target="tpu_custom_call" | custom-call | tf_op jit(solution)/shard_map/source1/pallas_call | solution.py:87
  66.7 8.5 %all-to-all-done.2.r = f32[16,12,8,128]{3,2,1,0:T(8,128)S(1)} async-done(((f32[16,12,8,128]{3,2,1,0:T(8,128)}), f32[16,12,8,128]{3,2,1,0:T(8,128)S(1)}, u32[]{:S(2)}, u32[]{:S(2)}) %all-to-all-start.2) | async-done | bytes 786464 | tf_op jit(solution)/shard_map/all_to_all | solution.py:402
  75.2 2.2 %depth.1 = f32[16,2,12,8,128]{4,3,2,1,0:T(8,128)S(1)} custom-call(s32[6]{0:T(128)S(1)} %slice_bitcast_fusion.6.code, f32[8,4]{1,0:T(8,128)S(1)} %copy-done.4, f32[16,12,8,128]{3,2,1,0:T(8,128)S(1)} %all-to-all-done.2.r, f32[16,12,8,128]{3,2,1,0:T(8,128)S(1)} %source1.1.a), custom_call_target="tpu_custom_call" | custom-call | tf_op jit(solution)/shard_map/depth/pallas_call | solution.py:364
  77.6 24.4 %all_to_all.39 = f32[16,2,12,8,128]{4,3,1,2,0:T(8,128)S(1)} all-to-all(f32[16,2,12,8,128]{4,3,1,2,0:T(8,128)S(1)} %copy.33), channel_id=1, replica_groups=mesh['gx'=8,'gy'=16] {'gy'}, dimensions={0} | all-to-all | bytes 3145728 | tf_op jit(solution)/shard_map/all_to_all | solution.py:402
  102.0 1.5 collective-permute-start.7
  103.7 2.3 %collective-permute-done.7.nxt = f32[16,2,8,128]{3,2,1,0:T(8,128)S(1)} collective-permute-done((f32[16,2,8,128]{3,2,1,0:T(8,128)S(1)}, f32[16,2,8,128]{3,2,1,0:T(8,128)S(1)}, u32[]{:S(2)}, u32[]{:S(2)}) %collective-permute-start.7) | collective-permute-done | bytes 131104 | tf_op jit(solution)/shard_map/ppermute | solution.py:398
  106.0 3.2 %collective-permute-done.6.prv = f32[16,2,8,128]{3,2,1,0:T(8,128)S(1)} collective-permute-done((f32[16,2,8,128]{3,2,1,0:T(8,128)S(1)}, f32[16,2,8,128]{3,2,1,0:T(8,128)S(1)}, u32[]{:S(2)}, u32[]{:S(2)}) %collective-permute-start.6) | collective-permute-done | bytes 131104 | tf_op jit(solution)/shard_map/ppermute | solution.py:394
  109.2 12.8 %normal.1 = (f32[16,12,8,128]{3,2,1,0:T(8,128)S(1)}, f32[16,8,128]{2,1,0:T(8,128)S(1)}, f32[16,8,128]{2,1,0:T(8,128)S(1)}) custom-call(s32[16,128]{1,0:T(8,128)S(1)} %bitcast.49, f32[8,4]{1,0:T(8,128)S(1)} %copy-done.4, f32[8,4]{1,0:T(8,128)S(1)} %copy-done.5, f32[16,2,12,8,128]{4,3,2,1,0:T(8,128)S(1)} %copy.36.x, ...), custom_call_target="tpu_custom_call" | custom-call | tf_op jit(solution)/shard_map/normal/pallas_call | solution.py:321
  124.0 3.0 %collective-permute-done.9 = f32[16,8,128]{2,1,0:T(8,128)S(1)} collective-permute-done((f32[16,8,128]{2,1,0:T(8,128)S(1)}, f32[16,8,128]{2,1,0:T(8,128)S(1)}, u32[]{:S(2)}, u32[]{:S(2)}) %collective-permute-start.9) | collective-permute-done | bytes 65568 | tf_op jit(solution)/shard_map/ppermute | solution.py:394
  127.0 15.1 %all_to_all.40.r.adj1 = f32[16,12,8,128]{3,2,1,0:T(8,128)S(1)} all-to-all(f32[16,12,8,128]{3,2,1,0:T(8,128)S(1)} %fusion.1), channel_id=1, replica_groups=mesh['gx'=8,'gy'=16] {'gy'}, dimensions={0} | all-to-all | bytes 1572864 | tf_op jit(solution)/shard_map/all_to_all | solution.py:402
  142.1 2.2 %depth_adjoint.1 = f32[16,12,8,128]{3,2,1,0:T(8,128)S(1)} custom-call(s32[6]{0:T(128)S(1)} %slice_bitcast_fusion.6.code, f32[8,4]{1,0:T(8,128)S(1)} %copy-done.4, f32[16,12,8,128]{3,2,1,0:T(8,128)S(1)} %all_to_all.40.r.adj1), custom_call_target="tpu_custom_call" | custom-call | tf_op jit(solution)/shard_map/depth_adjoint/pallas_call | solution.py:383
  144.3 14.8 %all_to_all.41.v = f32[16,12,8,128]{3,2,1,0:T(8,128)S(1)} all-to-all(f32[16,12,8,128]{3,2,1,0:T(8,128)S(1)} %depth_adjoint.1), channel_id=1, replica_groups=mesh['gx'=8,'gy'=16] {'gy'}, dimensions={0} | all-to-all | bytes 1572864 | tf_op jit(solution)/shard_map/all_to_all | solution.py:402
  159.1 5.7 %push.1 = (f32[16,12,8,128]{3,2,1,0:T(8,128)S(1)}, f32[16,8,128]{2,1,0:T(8,128)S(1)}, f32[16,8,128]{2,1,0:T(8,128)S(1)}) custom-call(s32[16,128]{1,0:T(8,128)S(1)} %bitcast.50, f32[8,4]{1,0:T(8,128)S(1)} %copy-done.4, f32[16,12,8,128]{3,2,1,0:T(8,128)S(1)} %all_to_all.41.v), custom_call_target="tpu_custom_call" | custom-call | tf_op jit(solution)/shard_map/push/pallas_call | solution.py:275
  164.8 2.0 %collective-permute-start.10 = (f32[16,8,128]{2,1,0:T(8,128)S(1)}, f32[16,8,128]{2,1,0:T(8,128)S(1)}, u32[]{:S(2)}, u32[]{:S(2)}) collective-permute-start(f32[16,8,128]{2,1,0:T(8,128)S(1)} %get-tuple-element.63), channel_id=1, source_target_pairs={{16,0},{32,16},{48,32},{64,48},{80,64},{96,80},{112,96},{0,112},{1... | collective-permute-start | bytes 196616 | tf_op jit(solution)/shard_map/ppermute | solution.py:398
  166.8 1.9 collective-permute-done.10
  168.8 3.4 %collective-permute-done.11 = f32[16,8,128]{2,1,0:T(8,128)S(1)} collective-permute-done((f32[16,8,128]{2,1,0:T(8,128)S(1)}, f32[16,8,128]{2,1,0:T(8,128)S(1)}, u32[]{:S(2)}, u32[]{:S(2)}) %collective-permute-start.11) | collective-permute-done | bytes 65568 | tf_op jit(solution)/shard_map/ppermute | solution.py:394
  172.2 16.8 %all_to_all.42.adj0 = f32[16,12,8,128]{3,2,1,0:T(8,128)S(1)} all-to-all(f32[16,12,8,128]{3,2,1,0:T(8,128)S(1)} %fusion), channel_id=1, replica_groups=mesh['gx'=8,'gy'=16] {'gy'}, dimensions={0} | all-to-all | bytes 1572864 | tf_op jit(solution)/shard_map/all_to_all | solution.py:402
  188.9 5.6 %force.1 = f32[3,96,16,128]{3,2,1,0:T(8,128)} custom-call(f32[16,12,8,128]{3,2,1,0:T(8,128)S(1)} %all_to_all.40.r.adj1, f32[16,12,8,128]{3,2,1,0:T(8,128)S(1)} %all_to_all.42.adj0, f32[2,96,16,128]{3,2,1,0:T(8,128)S(1)} %copy-done.1, f32[2,16,128]{2,1,0:T(8,128)S(1)} %collective-permute-done.top, f32[2,16,128]{2,1,0:T(8,128)S(1)} %collective-permute-done.1.bottom, ...), custom_call_target="tpu_custom_call" | custom-call | tf_op jit(solution)/shard_map/force/pallas_call | solution.py:109
  (45 shorter events, 6.1 us)
Async XLA Ops:
  1.5 13.8 %collective-permute-start.2 = (f32[2,96,128]{2,1,0:T(8,128)S(1)}, f32[2,96,128]{2,1,0:T(8,128)S(1)}, u32[]{:S(2)}, u32[]{:S(2)}) collective-permute-start(f32[2,96,128]{2,1,0:T(8,128)S(1)} %bitcast.52), channel_id=1, source_target_pairs={{0,1},{1,2},{2,3},{3,4},{4,5},{5,6},{6,7},{7,8},{8,9},{9,10},{10,1... | collective-permute-start | bytes 294920 | tf_op jit(solution)/shard_map/ppermute | solution.py:394
  3.3 12.0 %collective-permute-start.3 = (f32[2,96,128]{2,1,0:T(8,128)S(1)}, f32[2,96,128]{2,1,0:T(8,128)S(1)}, u32[]{:S(2)}, u32[]{:S(2)}) collective-permute-start(f32[2,96,128]{2,1,0:T(8,128)S(1)} %bitcast.51), channel_id=1, source_target_pairs={{1,0},{2,1},{3,2},{4,3},{5,4},{6,5},{7,6},{8,7},{9,8},{10,9},{11,1... | collective-permute-start | bytes 294920 | tf_op jit(solution)/shard_map/ppermute | solution.py:398
  7.7 4.6 %collective-permute-start.1 = (f32[2,16,128]{2,1,0:T(8,128)S(1)}, f32[2,16,128]{2,1,0:T(8,128)S(1)}, u32[]{:S(2)}, u32[]{:S(2)}) collective-permute-start(f32[2,16,128]{2,1,0:T(8,128)S(1)} %get-tuple-element.69), channel_id=1, source_target_pairs={{16,0},{32,16},{48,32},{64,48},{80,64},{96,80},{112,96},{0,112},{1... | collective-permute-start | bytes 49160 | tf_op jit(solution)/shard_map/ppermute | solution.py:398
  10.9 4.4 %collective-permute-start = (f32[2,16,128]{2,1,0:T(8,128)S(1)}, f32[2,16,128]{2,1,0:T(8,128)S(1)}, u32[]{:S(2)}, u32[]{:S(2)}) collective-permute-start(f32[2,16,128]{2,1,0:T(8,128)S(1)} %get-tuple-element.70), channel_id=1, source_target_pairs={{0,16},{16,32},{32,48},{48,64},{64,80},{80,96},{96,112},{112,0},{1... | collective-permute-start | bytes 49160 | tf_op jit(solution)/shard_map/ppermute | solution.py:394
  15.3 1.4 copy-start
  16.7 1.7 copy-start.2
  23.5 3.8 %copy-start.6 = (s32[3,6,1]{1,2,0:T(1,128)S(1)}, s32[3,6,1]{1,2,0:T(1,128)}, u32[]{:S(2)}) copy-start(s32[3,6,1]{1,2,0:T(1,128)} %param.19) | copy-start | bytes 220
  23.5 3.9 %copy-start.7 = (s32[1,1,16,2]{2,3,1,0:T(2,128)S(1)}, s32[1,1,16,2]{2,3,1,0:T(2,128)}, u32[]{:S(2)}) copy-start(s32[1,1,16,2]{2,3,1,0:T(2,128)} %param.18) | copy-start | bytes 388
  23.5 16.5 %copy-start.8 = (s32[6,1]{0,1:T(1,128)S(1)}, s32[6,1]{0,1:T(1,128)}, u32[]{:S(2)}) copy-start(s32[6,1]{0,1:T(1,128)} %param.17) | copy-start | bytes 76
  23.5 28.1 %copy-start.4 = (f32[8,4]{1,0:T(8,128)S(1)}, f32[8,4]{1,0:T(8,128)}, u32[]{:S(2)}) copy-start(f32[8,4]{1,0:T(8,128)} %constant.100.clone.wt) | copy-start | bytes 388
  23.5 15.3 %all-to-all-start.1 = ((f32[16,12,8,128]{3,2,1,0:T(8,128)}), f32[16,12,8,128]{3,2,1,0:T(8,128)S(1)}, u32[]{:S(2)}, u32[]{:S(2)}) async-start(f32[16,12,8,128]{3,2,1,0:T(8,128)} %source0.1), calls=%async_computation.1 | async-start | bytes 1572864 | tf_op jit(solution)/shard_map/all_to_all | solution.py:402
  38.8 12.8 %collective-permute-start.5 = (f32[16,8,128]{2,1,0:T(8,128)S(1)}, f32[16,8,128]{2,1,0:T(8,128)S(1)}, u32[]{:S(2)}, u32[]{:S(2)}) collective-permute-start(f32[16,8,128]{2,1,0:T(8,128)S(1)} %get-tuple-element.71), channel_id=1, source_target_pairs={{16,0},{32,16},{48,32},{64,48},{80,64},{96,80},{112,96},{0,112},{1... | collective-permute-start | bytes 196616 | tf_op jit(solution)/shard_map/ppermute | solution.py:398
  40.0 11.6 %collective-permute-start.4 = (f32[16,8,128]{2,1,0:T(8,128)S(1)}, f32[16,8,128]{2,1,0:T(8,128)S(1)}, u32[]{:S(2)}, u32[]{:S(2)}) collective-permute-start(f32[16,8,128]{2,1,0:T(8,128)S(1)} %get-tuple-element.72), channel_id=1, source_target_pairs={{0,16},{16,32},{32,48},{48,64},{64,80},{80,96},{96,112},{112,0},{1... | collective-permute-start | bytes 196616 | tf_op jit(solution)/shard_map/ppermute | solution.py:394
  51.6 10.9 %copy-start.1 = (f32[2,96,16,128]{3,2,1,0:T(8,128)S(1)}, f32[2,96,16,128]{3,2,1,0:T(8,128)}, u32[]{:S(2)}) copy-start(f32[2,96,16,128]{3,2,1,0:T(8,128)} %st.5) | copy-start | bytes 4718596
  58.9 16.4 %all-to-all-start.2 = ((f32[16,12,8,128]{3,2,1,0:T(8,128)}), f32[16,12,8,128]{3,2,1,0:T(8,128)S(1)}, u32[]{:S(2)}, u32[]{:S(2)}) async-start(f32[16,12,8,128]{3,2,1,0:T(8,128)} %pull.1), calls=%async_computation.2 | async-start | bytes 1572864 | tf_op jit(solution)/shard_map/all_to_all | solution.py:402
  62.5 1.7 copy-start.3
  102.0 4.0 %collective-permute-start.7 = (f32[16,2,8,128]{3,2,1,0:T(8,128)S(1)}, f32[16,2,8,128]{3,2,1,0:T(8,128)S(1)}, u32[]{:S(2)}, u32[]{:S(2)}) collective-permute-start(f32[16,2,8,128]{3,2,1,0:T(8,128)S(1)} %get-tuple-element.65), channel_id=1, source_target_pairs={{16,0},{32,16},{48,32},{64,48},{80,64},{96,80},{112,96},{0,112},{1... | collective-permute-start | bytes 393224 | tf_op jit(solution)/shard_map/ppermute | solution.py:398
  103.5 5.7 %copy-start.5 = (f32[8,4]{1,0:T(8,128)S(1)}, f32[8,4]{1,0:T(8,128)}, u32[]{:S(2)}) copy-start(f32[8,4]{1,0:T(8,128)} %constant.101.clone.kt) | copy-start | bytes 388
  103.5 5.7 %collective-permute-start.6 = (f32[16,2,8,128]{3,2,1,0:T(8,128)S(1)}, f32[16,2,8,128]{3,2,1,0:T(8,128)S(1)}, u32[]{:S(2)}, u32[]{:S(2)}) collective-permute-start(f32[16,2,8,128]{3,2,1,0:T(8,128)S(1)} %get-tuple-element.66), channel_id=1, source_target_pairs={{0,16},{16,32},{32,48},{48,64},{64,80},{80,96},{96,112},{112,0},{1... | collective-permute-start | bytes 393224 | tf_op jit(solution)/shard_map/ppermute | solution.py:394
  122.1 1.9 collective-permute-start.8
  122.1 4.9 %collective-permute-start.9 = (f32[16,8,128]{2,1,0:T(8,128)S(1)}, f32[16,8,128]{2,1,0:T(8,128)S(1)}, u32[]{:S(2)}, u32[]{:S(2)}) collective-permute-start(f32[16,8,128]{2,1,0:T(8,128)S(1)} %get-tuple-element.61), channel_id=1, source_target_pairs={{0,16},{16,32},{32,48},{48,64},{64,80},{80,96},{96,112},{112,0},{1... | collective-permute-start | bytes 196616 | tf_op jit(solution)/shard_map/ppermute | solution.py:394
  164.8 3.9 %collective-permute-start.10 = (f32[16,8,128]{2,1,0:T(8,128)S(1)}, f32[16,8,128]{2,1,0:T(8,128)S(1)}, u32[]{:S(2)}, u32[]{:S(2)}) collective-permute-start(f32[16,8,128]{2,1,0:T(8,128)S(1)} %get-tuple-element.63), channel_id=1, source_target_pairs={{16,0},{32,16},{48,32},{64,48},{80,64},{96,80},{112,96},{0,112},{1... | collective-permute-start | bytes 196616 | tf_op jit(solution)/shard_map/ppermute | solution.py:398
  166.8 5.3 %collective-permute-start.11 = (f32[16,8,128]{2,1,0:T(8,128)S(1)}, f32[16,8,128]{2,1,0:T(8,128)S(1)}, u32[]{:S(2)}, u32[]{:S(2)}) collective-permute-start(f32[16,8,128]{2,1,0:T(8,128)S(1)} %get-tuple-element.64), channel_id=1, source_target_pairs={{0,16},{16,32},{32,48},{48,64},{64,80},{80,96},{96,112},{112,0},{1... | collective-permute-start | bytes 196616 | tf_op jit(solution)/shard_map/ppermute | solution.py:394

commit v2 on v1

v2 whole, which is shorter than its diff:
```python
import functools

import jax
import jax.numpy as jnp
import numpy as np
from jax import lax
from jax.experimental import pallas as pl
from jax.experimental.pallas import tpu as pltpu
from jax.sharding import PartitionSpec as P

QF = 8
PEERS = 16
RB = 12
BRICKS = 6


def weights_of(f):
    return np.array(
        [
            -f * (f - 1.0) * (f - 2.0) / 6.0,
            (f + 1.0) * (f - 1.0) * (f - 2.0) / 2.0,
            -(f + 1.0) * f * (f - 2.0) / 2.0,
            (f + 1.0) * f * (f - 1.0) / 6.0,
        ]
    )


WEIGHTS = np.stack([weights_of(k / QF) for k in range(QF)])
PAIRS = np.stack([[np.dot(w[: 4 - d], w[d:]) for d in range(4)] for w in WEIGHTS])

VMEM = pl.BlockSpec(memory_space=pltpu.VMEM)
SMEM = pl.BlockSpec(memory_space=pltpu.SMEM)
F32 = jnp.float32


def params(mib=48):
    return pltpu.CompilerParams(vmem_limit_bytes=mib * 1024 * 1024)


def turned_shape(blocks=RB):
    return jax.ShapeDtypeStruct((PEERS, blocks, 8, 128), F32)


def gradients(st, top, bottom, left, right, rb, k):
    rows = pl.ds(rb * 8, 8)
    x = st[k, rows]
    before = st[k, jnp.maximum(rb * 8 - 1, 0)]
    before = jnp.where(rb == 0, jnp.zeros_like(before) if top is None else top[...], before)
    after = st[k, jnp.minimum(rb * 8 + 8, 95)]
    after = jnp.where(rb == RB - 1, jnp.zeros_like(after) if bottom is None else bottom[...], after)
    up = jnp.concatenate([x[1:], after[None]], axis=0)
    down = jnp.concatenate([before[None], x[:-1]], axis=0)
    col = lax.broadcasted_iota(jnp.int32, x.shape, 1)
    lo = 0.0 if left is None else left[0, rows][:, None, :]
    hi = 0.0 if right is None else right[0, rows][:, None, :]
    nxt = jnp.where(col == 15, hi, pltpu.roll(x, 15, 1))
    prv = jnp.where(col == 0, lo, pltpu.roll(x, 1, 1))
    return (
        (up - down) * 0.5,
        (nxt - prv) * 0.5,
        (pltpu.roll(x, 127, 2) - pltpu.roll(x, 1, 2)) * 0.5,
    )


def turn(x):
    return x.reshape(128, 128).T.reshape(PEERS, 8, 128)


def contract(v, g):
    return -0.5 * (v[0] * g[0] + v[1] * g[1] + v[2] * g[2])


def pre_kernel(v, st, out, sides, to_prv, to_nxt):
    i = pl.program_id(0)
    for j in range(3):
        rb = 3 * i + j
        vb = v[:, 8 * j : 8 * j + 8]
        a = contract(vb, gradients(st, None, None, None, None, rb, 0))
        out[:, j] = turn(a)
        rows = pl.ds(rb * 8, 8)
        sides[0, rows] = 0.25 * vb[1, :, 0]
        sides[1, rows] = -0.25 * vb[1, :, 15]
        if j == 0:

            @pl.when(i == 0)
            def _():
                to_prv[0] = a[0]
                to_prv[1] = vb[0, 0]
                to_prv[2] = a[1]
                to_prv[3] = st[0, 0]

        if j == 2:

            @pl.when(i == RB // 3 - 1)
            def _():
                to_nxt[0] = a[7]
                to_nxt[1] = vb[0, 7]
                to_nxt[2] = st[0, 95]


def pre(velocity, states):
    return pl.pallas_call(
        pre_kernel,
        grid=(RB // 3,),
        in_specs=[pl.BlockSpec((3, 24, 16, 128), lambda i: (0, i, 0, 0)), state_spec(0)],
        out_specs=[
            pl.BlockSpec((PEERS, 3, 8, 128), lambda i: (0, i, 0, 0)),
            whole((2, 96, 128)),
            whole((4, 16, 128)),
            whole((3, 16, 128)),
        ],
        out_shape=[
            turned_shape(RB + 1),
            jax.ShapeDtypeStruct((2, 96, 128), F32),
            jax.ShapeDtypeStruct((4, 16, 128), F32),
            jax.ShapeDtypeStruct((3, 16, 128), F32),
        ],
        compiler_params=params(16),
        cost_estimate=COST,
        name="pre",
    )(velocity, states)


def rims_kernel(prv, nxt, sides, left, right, ends, to_prv, to_nxt):
    col = lax.broadcasted_iota(jnp.int32, (16, 128), 0)

    def side(row):
        lo = sides[0, row : row + 1] * left[0, row : row + 1]
        hi = sides[1, row : row + 1] * right[0, row : row + 1]
        return jnp.where(col == 0, lo, 0.0) + jnp.where(col == 15, hi, 0.0)

    to_prv[0] = prv[0] + side(0)
    to_prv[1] = prv[1]
    to_prv[2] = prv[2] + side(1)
    to_prv[3] = prv[3]
    to_prv[4] = ends[0]
    to_nxt[0] = nxt[0] + side(95)
    to_nxt[1] = nxt[1]
    to_nxt[2] = nxt[2]
    to_nxt[3] = ends[1]


def rims(prv, nxt, sides, left, right, ends):
    return pl.pallas_call(
        rims_kernel,
        in_specs=[VMEM] * 6,
        out_specs=[VMEM, VMEM],
        out_shape=[jax.ShapeDtypeStruct((5, 16, 128), F32), jax.ShapeDtypeStruct((4, 16, 128), F32)],
        compiler_params=params(16),
        name="rims",
    )(prv, nxt, sides, left, right, ends)


def columns_kernel(a, sides, left, right, out):
    col = lax.broadcasted_iota(jnp.int32, (8, 16, 128), 1)
    for j in range(3):
        rows = pl.ds(8 * j, 8)
        lo = (sides[0, rows] * left[0, rows])[:, None, :]
        hi = (sides[1, rows] * right[0, rows])[:, None, :]
        out[:, j] = a[:, j] + turn(jnp.where(col == 0, lo, 0.0) + jnp.where(col == 15, hi, 0.0))


def columns(a, sides, left, right):
    block = pl.BlockSpec((PEERS, 3, 8, 128), lambda i: (0, i, 0, 0))
    side = pl.BlockSpec((1, 24, 128), lambda i: (0, i, 0))
    return pl.pallas_call(
        columns_kernel,
        grid=(RB // 3,),
        in_specs=[block, pl.BlockSpec((2, 24, 128), lambda i: (0, i, 0)), side, side],
        out_specs=block,
        out_shape=turned_shape(RB + 1),
        input_output_aliases={0: 0},
        compiler_params=params(16),
        cost_estimate=COST,
        name="columns",
    )(a, sides, left, right)


def source1_kernel(v, st, top, bottom, left, right, out):
    g = gradients(st, top, bottom, left, right, pl.program_id(0), 0)
    out[:, 0] = turn(contract(v, g))


def whole(shape):
    return pl.BlockSpec(shape, lambda i: (0,) * len(shape))


def state_spec(k):
    return pl.BlockSpec((1, 96, 16, 128), lambda i: (k, 0, 0, 0))


def edge_specs(k):
    side = pl.BlockSpec((1, 96, 128), lambda i: (k, 0, 0))
    return [whole((16, 128)), whole((16, 128)), side, side]


def natural3(f):
    return pl.BlockSpec((3, 8, 16, 128), lambda i: (0, f(i), 0, 0))


def turned(f):
    return pl.BlockSpec((PEERS, 1, 8, 128), lambda i: (0, f(i), 0, 0))


def same(i):
    return i


COST = pl.CostEstimate(flops=20_000_000, bytes_accessed=6_000_000, transcendentals=0)


def source1(velocity, states, edges):
    return pl.pallas_call(
        source1_kernel,
        grid=(RB,),
        in_specs=[natural3(same), state_spec(1)] + edge_specs(1),
        out_specs=turned(same),
        out_shape=turned_shape(RB),
        compiler_params=params(16),
        cost_estimate=COST,
        name="source1",
    )(velocity, states, *edges)


def close_kernel(a, my_prv, my_nxt, from_nxt, from_prv, table, out):
    i = pl.program_id(0)
    row = lax.broadcasted_iota(jnp.int32, (8, 16, 128), 0)
    zero = jnp.zeros((8, 16, 128), F32)
    lane = lax.broadcasted_iota(jnp.int32, (PEERS, 8, 128), 2)

    @pl.when(i == 0)
    def _():
        x = 0.25 * my_prv[1] * from_prv[2]
        out[:, 0] = a[:, 0] + turn(jnp.where(row == 0, x[None], zero))

    @pl.when(i == 1)
    def _():
        x = -0.25 * my_nxt[1] * from_nxt[3]
        out[:, 0] = a[:, 0] + turn(jnp.where(row == 7, x[None], zero))

    @pl.when(i == 2)
    def _():
        before = from_prv[0] - 0.25 * from_prv[1] * my_prv[3]
        after = from_nxt[0] + 0.25 * from_nxt[1] * my_nxt[2]
        x = jnp.where(row == 7, before[None], zero)
        x = jnp.where(row == 0, after[None], x)
        x = jnp.where(row == 1, from_nxt[2][None], x)
        inner = (lane >= 32) & (lane < 112)
        out[:, 0] = jnp.where(inner, table[...][None], turn(x))


def close(a, my_prv, my_nxt, from_nxt, from_prv, table):
    def block(i):
        return jnp.minimum(i * (RB - 1), RB)

    return pl.pallas_call(
        close_kernel,
        grid=(3,),
        in_specs=[
            turned(block),
            whole((5, 16, 128)),
            whole((4, 16, 128)),
            whole((5, 16, 128)),
            whole((4, 16, 128)),
            whole((1, 128)),
        ],
        out_specs=turned(block),
        out_shape=turned_shape(RB + 1),
        input_output_aliases={0: 0},
        compiler_params=params(16),
        name="close",
    )(a, my_prv, my_nxt, from_nxt, from_prv, table)


def force_block(adj1, adj0, s1, e1, s0, e0, rb, out):
    b1 = (adj1.reshape(128, 128).T * -0.5).reshape(8, 16, 128)
    b0 = (adj0.reshape(128, 128).T * -0.5).reshape(8, 16, 128)
    g1 = gradients(s1, *e1, rb, 0)
    g0 = gradients(s0, *e0, rb, 0)
    for c in range(3):
        out[c] = b1 * g1[c] + b0 * g0[c]


def force_kernel(adj1, adj0, s1, t1, b1, l1, r1, s0, t0, b0, l0, r0, out):
    rb = pl.program_id(0) + 1
    force_block(adj1[:, 0], adj0[:, 0], s1, (t1, b1, l1, r1), s0, (t0, b0, l0, r0), rb, out)


def force_edge_kernel(adj1, adj0, s1, t1, b1, l1, r1, s0, t0, b0, l0, r0, from_nxt, from_prv, prior, out):
    i = pl.program_id(0)
    lane = lax.broadcasted_iota(jnp.int32, (PEERS, 8, 128), 2)
    x = jnp.where((i == 0) & (lane < 32), from_prv[...], 0.0)
    x = x + jnp.where((i == 1) & (lane >= 112), from_nxt[...], 0.0)
    force_block(adj1[:, 0], adj0[:, 0] + x, s1, (t1, b1, l1, r1), s0, (t0, b0, l0, r0), i * (RB - 1), out)


def force(adj1, adj0, states, e1, e0):
    def specs(f):
        return [turned(f), turned(f), state_spec(1)] + edge_specs(1) + [state_spec(0)] + edge_specs(0)

    shape = jax.ShapeDtypeStruct((3, 96, 16, 128), F32)
    rim = adj0[:, RB]
    from_nxt = to_prev(rim, "gx", lax.axis_size("gx"))
    from_prv = to_next(rim, "gx", lax.axis_size("gx"))
    args = (adj1, adj0, states, *e1, states, *e0)

    def inner(i):
        return i + 1

    def outer(i):
        return i * (RB - 1)

    main = pl.pallas_call(
        force_kernel,
        grid=(RB - 2,),
        in_specs=specs(inner),
        out_specs=natural3(inner),
        out_shape=shape,
        compiler_params=params(24),
        cost_estimate=COST,
        name="force",
    )(*args)
    return pl.pallas_call(
        force_edge_kernel,
        grid=(2,),
        in_specs=specs(outer) + [whole((PEERS, 8, 128)), whole((PEERS, 8, 128)), pl.BlockSpec(memory_space=pl.ANY)],
        out_specs=natural3(outer),
        out_shape=shape,
        input_output_aliases={14: 0},
        compiler_params=params(24),
        name="force_edge",
    )(*args, from_nxt, from_prv, main)


def lanes():
    return lax.broadcasted_iota(jnp.int32, (8, 128), 1)


def column_taps(x):
    col = lax.broadcasted_iota(jnp.int32, x.shape, 2) % 16
    up = pltpu.roll(x, 16, 2)
    dn = pltpu.roll(x, 112, 2)
    after = jnp.concatenate([up[1:], up[:1]], axis=0)
    before = jnp.concatenate([dn[-1:], dn[:-1]], axis=0)
    return (
        pltpu.roll(jnp.where(col == 15, before, x), 1, 2),
        x,
        pltpu.roll(jnp.where(col == 0, after, x), 127, 2),
        pltpu.roll(jnp.where(col < 2, after, x), 126, 2),
    )


def column_taps_adjoint(t0, t1, t2, t3):
    col = lax.broadcasted_iota(jnp.int32, t1.shape, 2) % 16
    p0 = pltpu.roll(t0, 127, 2)
    p2 = pltpu.roll(t2, 1, 2)
    p3 = pltpu.roll(t3, 2, 2)
    own = t1 + jnp.where(col == 15, 0.0, p0) + jnp.where(col == 0, 0.0, p2) + jnp.where(col < 2, 0.0, p3)
    after = jnp.where(col == 0, p2, 0.0) + jnp.where(col < 2, p3, 0.0)
    before = jnp.where(col == 15, p0, 0.0)
    after = pltpu.roll(after, 112, 2)
    before = pltpu.roll(before, 16, 2)
    after = jnp.concatenate([after[-1:], after[:-1]], axis=0)
    before = jnp.concatenate([before[1:], before[:1]], axis=0)
    return own + after + before


def fill_taps(taps, e, x):
    for t, y in enumerate(column_taps(x)):
        taps[t, pl.ds(e * PEERS, PEERS)] = y


def fill_all(taps, x):
    @pl.loop(0, RB // 3)
    def _(i):
        for j in range(3):
            fill_taps(taps, 3 * i + j + 1, x(3 * i + j))

    for t, y in enumerate(column_taps(x(RB))):
        taps[t, pl.ds(0, PEERS)] = y
        taps[t, pl.ds((RB + 1) * PEERS, PEERS)] = y


def fill_weights(wv, values):
    for f in range(QF):
        for t in range(4):
            wv[f, t] = jnp.full((8, 128), float(values[f, t]), F32)


def brick_plan(tab, wv, b):
    base = tab[0, b]
    u = tab[1, b]
    v = tab[2, b]
    return base, [wv[u, t] for t in range(4)], [wv[v, t] for t in range(4)]


def brick_forward(taps, base, wr, wc):
    lane = lanes()
    c = []
    for i in range(4):
        acc = [wc[t] * taps[t, base + i * PEERS] for t in range(4)]
        c.append((acc[0] + acc[1]) + (acc[2] + acc[3]))
    outs = []
    for h in range(2):
        prv, cur, nxt = c[h], c[h + 1], c[h + 2]
        outs.append(
            (wr[0] * pltpu.roll(jnp.where(lane >= 112, prv, cur), 16, 1) + wr[1] * cur)
            + (
                wr[2] * pltpu.roll(jnp.where(lane < 16, nxt, cur), 112, 1)
                + wr[3] * pltpu.roll(jnp.where(lane < 32, nxt, cur), 96, 1)
            )
        )
    return outs


def brick_rows_adjoint(wr, v):
    lane = lanes()
    lo, own, hi = [], [], []
    for h in range(2):
        p0 = wr[0] * pltpu.roll(v[h], 112, 1)
        p2 = wr[2] * pltpu.roll(v[h], 16, 1)
        p3 = wr[3] * pltpu.roll(v[h], 32, 1)
        lo.append(jnp.where(lane >= 112, p0, 0.0))
        own.append(
            (wr[1] * v[h] + jnp.where(lane >= 112, 0.0, p0))
            + (jnp.where(lane < 16, 0.0, p2) + jnp.where(lane < 32, 0.0, p3))
        )
        hi.append(jnp.where(lane < 16, p2, 0.0) + jnp.where(lane < 32, p3, 0.0))
    return [lo[0], own[0] + lo[1], own[1] + hi[0], hi[1]]


def brick_add(acc, base, wc, c):
    for i in range(4):
        for t in range(4):
            acc[t, base + i * PEERS] = acc[t, base + i * PEERS] + wc[t] * c[i]


def pull_kernel(tab, x, out, taps, wv):
    fill_weights(wv, WEIGHTS)
    fill_all(taps, lambda rb: x[:, rb])

    @pl.loop(0, PEERS)
    def _(d):
        plans = [brick_plan(tab, wv, d * BRICKS + k) for k in range(BRICKS)]
        for k in range(BRICKS):
            base, wr, wc = plans[k]
            o = brick_forward(taps, base, wr, wc)
            for h in range(2):
                out[d, 2 * k + h] = o[h]


TAPS = pltpu.VMEM((4, PEERS * (RB + 2), 8, 128), F32)
WV = pltpu.VMEM((QF, 4, 8, 128), F32)


def pull(tab, x):
    return pl.pallas_call(
        pull_kernel,
        in_specs=[SMEM, VMEM],
        out_specs=VMEM,
        out_shape=turned_shape(),
        scratch_shapes=[TAPS, WV],
        compiler_params=params(24),
        name="pull",
    )(tab, x)


def clear(acc):
    @pl.loop(0, RB + 2)
    def _(e):
        acc[:, pl.ds(e * PEERS, PEERS)] = jnp.zeros((4, PEERS, 8, 128), F32)


def gather_taps(acc, e):
    return column_taps_adjoint(*[acc[t, pl.ds(e * PEERS, PEERS)] for t in range(4)])


def spill_inner(acc, out):
    @pl.loop(0, RB // 3)
    def _(i):
        for j in range(3):
            out[:, 3 * i + j] = gather_taps(acc, 3 * i + j + 1)


def push_kernel(tab, v, out, acc, wv):
    fill_weights(wv, WEIGHTS)
    clear(acc)

    @pl.loop(0, PEERS)
    def _(d):
        plans = [brick_plan(tab, wv, d * BRICKS + k) for k in range(BRICKS)]
        cs = [brick_rows_adjoint(plans[k][1], [v[d, 2 * k], v[d, 2 * k + 1]]) for k in range(BRICKS)]
        for k in range(BRICKS):
            brick_add(acc, plans[k][0], plans[k][2], cs[k])

    spill_inner(acc, out)
    out[:, RB] = gather_taps(acc, 0) + gather_taps(acc, RB + 1)


def push(tab, v):
    return pl.pallas_call(
        push_kernel,
        in_specs=[SMEM, VMEM],
        out_specs=VMEM,
        out_shape=turned_shape(RB + 1),
        scratch_shapes=[TAPS, WV],
        compiler_params=params(24),
        name="push",
    )(tab, v)


def normal_kernel(tab, x, prv, nxt, out, lo, hi, taps, acc, wv, kv):
    fill_weights(wv, WEIGHTS)
    fill_weights(kv, PAIRS)
    clear(acc)
    for q in range(2):
        fill_taps(taps.at[q], 0, prv[:, q])
        fill_taps(taps.at[q], RB + 1, nxt[:, q])

        @pl.loop(0, RB // 2)
        def _(i):
            for j in range(2):
                fill_taps(taps.at[q], 2 * i + j + 1, x[:, q, 2 * i + j])

    @pl.loop(0, PEERS)
    def _(d):
        sub = lax.broadcasted_iota(jnp.int32, (8, 128), 0)
        plans = [brick_plan(tab, wv, d * BRICKS + k) for k in range(BRICKS)]
        cs = []
        for k in range(BRICKS):
            base, wr, wc = plans[k]
            f = tab[3, d * BRICKS + k]
            kw = [kv[f, t] for t in range(4)]
            t0 = brick_forward(taps.at[0], base, wr, wc)
            t1 = brick_forward(taps.at[1], base, wr, wc)
            v = []
            for h in range(2):

                def plane(a):
                    return pltpu.roll(jnp.where(sub >= a, t0[h], t1[h]), 8 - a, 0)

                terms = [kw[0] * plane(4)]
                for dd in range(1, 4):
                    terms.append(kw[dd] * (plane(4 - dd) + plane(4 + dd)))
                v.append((terms[0] + terms[1]) + (terms[2] + terms[3]))
            cs.append(brick_rows_adjoint(wr, v))
        for k in range(BRICKS):
            brick_add(acc, plans[k][0], plans[k][2], cs[k])

    lo[...] = gather_taps(acc, 0)
    hi[...] = gather_taps(acc, RB + 1)
    spill_inner(acc, out)


EDGE = jax.ShapeDtypeStruct((PEERS, 8, 128), F32)


def normal(tab, x, prv, nxt):
    return pl.pallas_call(
        normal_kernel,
        in_specs=[SMEM, VMEM, VMEM, VMEM],
        out_specs=[VMEM, VMEM, VMEM],
        out_shape=[turned_shape(), EDGE, EDGE],
        scratch_shapes=[pltpu.VMEM((2, 4, PEERS * (RB + 2), 8, 128), F32), TAPS, WV, WV],
        compiler_params=params(32),
        name="normal",
    )(tab, x, prv, nxt)


def depth_matrix(wt, q, transpose):
    n = q // QF
    f = q % QF
    i = lax.broadcasted_iota(jnp.int32, (128, 128), 0)
    j = lax.broadcasted_iota(jnp.int32, (128, 128), 1)
    off = (i - j if transpose else j - i) + (257 - n)
    off = jnp.bitwise_and(off, 127)
    w = jnp.zeros((128, 128), F32)
    for m in range(4):
        w = jnp.where(off == m, wt[f, m], w)
    return w


def depth_product(wt, q, transpose, r, k):
    w = depth_matrix(wt, q, transpose)
    pair = [r[:, 2 * k + h].reshape(128, 128) for h in range(2)]
    y = jnp.dot(w, jnp.concatenate(pair, axis=1), precision=lax.Precision.HIGHEST, preferred_element_type=F32)
    return y[:, :128], y[:, 128:]


def depth_kernel(code, wt, r, a, out):
    @pl.loop(0, BRICKS)
    def _(k):
        ys = depth_product(wt, code[k], False, r, k)
        for h in range(2):
            u = ys[h] + a[:, 2 * k + h].reshape(128, 128)
            tiles = pltpu.roll(u, 4, 0).reshape(PEERS, 8, 128)
            out[:, 0, 2 * k + h] = tiles
            out[:, 1, 2 * k + h] = jnp.concatenate([tiles[1:], tiles[:1]], axis=0)


def depth(code, wt, r, a):
    return pl.pallas_call(
        depth_kernel,
        in_specs=[SMEM, SMEM, VMEM, VMEM],
        out_specs=VMEM,
        out_shape=jax.ShapeDtypeStruct((PEERS, 2, RB, 8, 128), F32),
        compiler_params=params(24),
        name="depth",
    )(code, wt, r, a)


def depth_adjoint_kernel(code, wt, r, out):
    @pl.loop(0, BRICKS)
    def _(k):
        ys = depth_product(wt, code[k], True, r, k)
        for h in range(2):
            out[:, 2 * k + h] = ys[h].reshape(PEERS, 8, 128)


def depth_adjoint(code, wt, r):
    return pl.pallas_call(
        depth_adjoint_kernel,
        in_specs=[SMEM, SMEM, VMEM],
        out_specs=VMEM,
        out_shape=turned_shape(),
        compiler_params=params(24),
        name="depth_adjoint",
    )(code, wt, r)


def to_next(x, axis, count):
    return lax.ppermute(x, axis, [(i, (i + 1) % count) for i in range(count)])


def to_prev(x, axis, count):
    return lax.ppermute(x, axis, [((i + 1) % count, i) for i in range(count)])


def swap(x):
    return lax.all_to_all(x, "gy", split_axis=0, concat_axis=0, tiled=True)


def brick_table(raw):
    t = raw.astype(jnp.int32)
    slot = t[:, 32:38]
    sends = t[:, :32].reshape(PEERS, PEERS, 2).transpose(1, 0, 2).reshape(PEERS, 1, 32)
    hit = slot[:, :, None] == jnp.arange(32)[None, None, :]
    local = jnp.sum(jnp.where(hit, sends, 0), axis=2)
    rows = [2 * PEERS * local + slot // 2, t[:, 38:44], t[:, 44:50], t[:, 50:56] % QF]
    return jnp.stack(rows).reshape(4, PEERS * BRICKS)


def body(velocity, states, pull_plan, send_plan, codes):
    gx = lax.axis_size("gx")
    gy = lax.axis_size("gy")
    left = to_next(states[:, :, -1], "gy", gy)
    right = to_prev(states[:, :, 0], "gy", gy)
    ends = jnp.stack([states[1, 0], states[1, -1]])
    a0, sides, my_prv, my_nxt = pre(velocity, states)
    wt = jnp.asarray(WEIGHTS, F32)
    code = codes[2].reshape(BRICKS)
    mine = [send_plan.reshape(32), pull_plan.reshape(BRICKS), codes.reshape(3 * BRICKS)]
    table = jnp.concatenate([jnp.zeros((32,), jnp.int32)] + mine + [jnp.zeros((40,), jnp.int32)])
    table = table.astype(F32).reshape(1, 128)

    my_prv, my_nxt = rims(my_prv, my_nxt, sides, left, right, ends)
    from_nxt = to_prev(my_prv, "gx", gx)
    from_prv = to_next(my_nxt, "gx", gx)
    a0 = close(columns(a0, sides, left, right), my_prv, my_nxt, from_nxt, from_prv, table)
    e0 = (from_prv[2], from_nxt[3], left, right)
    e1 = (from_prv[3], from_nxt[4], left, right)
    a1 = source1(velocity, states, e1)

    x = swap(a0)
    tab = brick_table(x[:, RB, 0, 32:88])
    r = swap(pull(tab, x))
    u = swap(depth(code, wt, r, a1))
    y, lo, hi = normal(tab, u, to_next(u[:, :, RB - 1], "gx", gx), to_prev(u[:, :, 0], "gx", gx))
    y = y.at[:, RB - 1].add(to_prev(lo, "gx", gx)).at[:, 0].add(to_next(hi, "gx", gx))
    adj1 = swap(y)
    v = swap(depth_adjoint(code, wt, adj1))
    adj0 = swap(push(tab, v))
    return force(adj1, adj0, states, e1, e0)


def solution(mesh):
    return jax.shard_map(
        body,
        mesh=mesh,
        in_specs=(
            P(None, "gx", "gy", None),
            P(None, "gx", "gy", None),
            P("gx", "gy"),
            P("gx", "gy", None, None),
            P(None, "gx", "gy"),
        ),
        out_specs=P(None, "gx", "gy", None),
        check_vma=False,
    )
```

time: 195 us -> 176 us (0.903); the launches traced: 195 us -> 173 us
  waiting for transfers between devices: 39.4 us -> 20.3 us
  Pallas kernels: 43.4 us -> 40 us
  blocking collectives: 82.5 us -> 80 us
  starting transfers between devices: 21.3 us -> 23.3 us
    all_to_all x2 -> x1, waiting for transfers between devices: 19.8 us -> 7.28 us  [swap(): return lax.all_to_all(x, 'gy', split_axis=0, concat_axis=0, tiled=True)]
    ppermute x6 -> x5, starting transfers between devices: 11.7 us -> 17.4 us  [to_prev(): return lax.ppermute(x, axis, [((i + 1) % count, i) for i in range(count)])]
    all_to_all x2 -> x1, starting transfers between devices: 7.37 us -> 3.67 us  [swap(): return lax.all_to_all(x, 'gy', split_axis=0, concat_axis=0, tiled=True)]
    pallas_call x6 -> x10, Pallas kernels: 39 us -> 35.6 us  [the longest x1 12.4 us: normal(): pl.pallas_call(normal_kernel, in_specs=[SMEM, VMEM, VMEM, VMEM], out_spec...]
    ppermute x6 -> x5, waiting for transfers between devices: 7.08 us -> 3.78 us  [to_prev(): return lax.ppermute(x, axis, [((i + 1) % count, i) for i in range(count)])]
    ppermute x6 -> x5, waiting for transfers between devices: 12.5 us -> 9.28 us  [to_next(): return lax.ppermute(x, axis, [(i, (i + 1) % count) for i in range(count)])]
    all_to_all x5, blocking collectives: 82.5 us -> 80 us  [swap(): return lax.all_to_all(x, 'gy', split_axis=0, concat_axis=0, tiled=True)]
    unnamed x19 -> x17, local copies, waits for them, and re-layouts: 4.84 us -> 4.84 us
  transfers between devices with their start and end apart: 14 -> 11, of which waited for: 10 -> 6; matrix products, arithmetic and copies ran while one was open for 1% -> 1% of each run, Pallas kernels for 1% -> 6%
where the time goes in v2:
time: 176 us; the launch traced here: 173 us
  blocking collectives  80 us (45%)
  Pallas kernels  40 us (23%)
  starting transfers between devices  23.3 us (13%)
  waiting for transfers between devices  20.3 us (12%)
  local copies, waits for them, and re-layouts  8.49 us (5%)
    all_to_all x5, blocking collectives, swap(): return lax.all_to_all(x, 'gy', split_axis=0, concat_axis=0, tiled=True)  80 us
    ppermute x5, starting transfers between devices, to_prev(): return lax.ppermute(x, axis, [((i + 1) % count, i) for i in range(count)])  17.4 us
    pallas_call x1, Pallas kernels, normal(): pl.pallas_call(normal_kernel, in_specs=[SMEM, VMEM, VMEM, VMEM], out_spec...  12.4 us
    ppermute x5, waiting for transfers between devices, to_next(): return lax.ppermute(x, axis, [(i, (i + 1) % count) for i in range(count)])  9.28 us
    all_to_all x1, waiting for transfers between devices, swap(): return lax.all_to_all(x, 'gy', split_axis=0, concat_axis=0, tiled=True)  7.28 us
    pallas_call x1, Pallas kernels, pull(): pl.pallas_call(pull_kernel, in_specs=[SMEM, VMEM], out_specs=VMEM, out_sh...  5.74 us
    pallas_call x1, Pallas kernels, push(): pl.pallas_call(push_kernel, in_specs=[SMEM, VMEM], out_specs=VMEM, out_sh...  5.54 us
    unnamed x17, local copies, waits for them, and re-layouts  4.84 us
  transfers between devices with their start and end apart: 11, of which 6 were waited for; matrix products, arithmetic and copies ran while one was open for 1% of the time, Pallas kernels for 6%

profile of v2, /device:TPU:0, one launch (start us, length us, event | category | flops | bytes accessed | tf_op | source)
XLA Modules:
  0.0 172.9 jit_solution(12843302823632126676)
XLA Ops:
  0.0 1.5 fusion.6
  1.5 1.8 %collective-permute-start = (f32[2,96,128]{2,1,0:T(8,128)S(1)}, f32[2,96,128]{2,1,0:T(8,128)S(1)}, u32[]{:S(2)}, u32[]{:S(2)}) collective-permute-start(f32[2,96,128]{2,1,0:T(8,128)S(1)} %bitcast.51), channel_id=1, source_target_pairs={{0,1},{1,2},{2,3},{3,4},{4,5},{5,6},{6,7},{7,8},{8,9},{9,10},{10,1... | collective-permute-start | bytes 294920 | tf_op jit(solution)/shard_map/ppermute | solution.py:632
  3.3 3.7 %collective-permute-start.1 = (f32[2,96,128]{2,1,0:T(8,128)S(1)}, f32[2,96,128]{2,1,0:T(8,128)S(1)}, u32[]{:S(2)}, u32[]{:S(2)}) collective-permute-start(f32[2,96,128]{2,1,0:T(8,128)S(1)} %bitcast.50), channel_id=1, source_target_pairs={{1,0},{2,1},{3,2},{4,3},{5,4},{6,5},{7,6},{8,7},{9,8},{10,9},{11,1... | collective-permute-start | bytes 294920 | tf_op jit(solution)/shard_map/ppermute | solution.py:636
  7.0 0.7 slice_bitcast_fusion.8
  7.7 1.4 copy-done
  9.1 1.7 copy-done.2
  10.8 2.2 %pre.1 = (f32[16,13,8,128]{3,2,1,0:T(8,128)S(1)}, f32[2,96,128]{2,1,0:T(8,128)S(1)}, f32[4,16,128]{2,1,0:T(8,128)S(1)}, f32[3,16,128]{2,1,0:T(8,128)S(1)}) custom-call(f32[3,96,16,128]{3,2,1,0:T(8,128)S(1)} %copy-done.2, f32[2,96,16,128]{3,2,1,0:T(8,128)S(1)} %copy-done), custom_call_target="tpu_custom_call" | custom-call | flops 20000000 | bytes 6000000 | tf_op jit(solution)/shard_map/pre/pallas_call | solution.py:102
  13.0 3.2 %collective-permute-start.2 = (f32[5,16,128]{2,1,0:T(8,128)S(1)}, f32[5,16,128]{2,1,0:T(8,128)S(1)}, u32[]{:S(2)}, u32[]{:S(2)}) collective-permute-start(f32[5,16,128]{2,1,0:T(8,128)S(1)} %get-tuple-element.42.my_prv), channel_id=1, source_target_pairs={{16,0},{32,16},{48,32},{64,48},{80,64},{96,80},{112,96},{0,112},{1... | collective-permute-start | bytes 122888 | tf_op jit(solution)/shard_map/ppermute | solution.py:636
  16.7 0.9 columns.1.a
  17.6 3.2 %collective-permute-done.3.from_prv = f32[4,16,128]{2,1,0:T(8,128)S(1)} collective-permute-done((f32[4,16,128]{2,1,0:T(8,128)S(1)}, f32[4,16,128]{2,1,0:T(8,128)S(1)}, u32[]{:S(2)}, u32[]{:S(2)}) %collective-permute-start.3) | collective-permute-done | bytes 32800 | tf_op jit(solution)/shard_map/ppermute | solution.py:632
  21.2 14.9 %all_to_all.30.x = f32[16,13,8,128]{3,2,1,0:T(8,128)S(1)} all-to-all(f32[16,13,8,128]{3,2,1,0:T(8,128)S(1)} %close.1), channel_id=1, replica_groups=mesh['gx'=8,'gy'=16] {'gy'}, dimensions={0} | all-to-all | bytes 1703936 | tf_op jit(solution)/shard_map/all_to_all | solution.py:640
  37.5 5.7 %pull.1 = f32[16,12,8,128]{3,2,1,0:T(8,128)} custom-call(s32[4,96]{1,0:T(4,128)S(1)} %pad_add_fusion.tab, f32[16,13,8,128]{3,2,1,0:T(8,128)S(1)} %all_to_all.30.x), custom_call_target="tpu_custom_call" | custom-call | tf_op jit(solution)/shard_map/pull/pallas_call | solution.py:457
  43.2 3.7 %all-to-all-start.1 = ((f32[16,12,8,128]{3,2,1,0:T(8,128)}), f32[16,12,8,128]{3,2,1,0:T(8,128)S(1)}, u32[]{:S(2)}, u32[]{:S(2)}) async-start(f32[16,12,8,128]{3,2,1,0:T(8,128)} %pull.1), calls=%async_computation.1 | async-start | bytes 1572864 | tf_op jit(solution)/shard_map/all_to_all | solution.py:640
  46.9 1.7 copy-done.3
  48.6 2.5 %source1.1.a = f32[16,12,8,128]{3,2,1,0:T(8,128)S(1)} custom-call(f32[3,96,16,128]{3,2,1,0:T(8,128)S(1)} %copy-done.3, f32[2,96,16,128]{3,2,1,0:T(8,128)S(1)} %copy-done.1, f32[16,128]{1,0:T(8,128)S(1)} %get-tuple-element.56.top.t1, f32[16,128]{1,0:T(8,128)S(1)} %get-tuple-element.54.bottom.b1, f32[2,96,128]{2,1,0:T(8,128)S(1)} %collective-permute-done.left.l1.l0, ...), custom_call_target="tpu_custom_call" | custom-call | flops 20000000 | bytes 6000000 | tf_op jit(solution)/shard_map/source1/pallas_call | solution.py:213
  51.1 7.3 %all-to-all-done.1.r = f32[16,12,8,128]{3,2,1,0:T(8,128)S(1)} async-done(((f32[16,12,8,128]{3,2,1,0:T(8,128)}), f32[16,12,8,128]{3,2,1,0:T(8,128)S(1)}, u32[]{:S(2)}, u32[]{:S(2)}) %all-to-all-start.1) | async-done | bytes 786464 | tf_op jit(solution)/shard_map/all_to_all | solution.py:640
  58.4 2.2 %depth.1 = f32[16,2,12,8,128]{4,3,2,1,0:T(8,128)S(1)} custom-call(s32[6]{0:T(128)S(1)} %slice_bitcast_fusion.9.code, f32[8,4]{1,0:T(8,128)S(1)} %copy-done.4, f32[16,12,8,128]{3,2,1,0:T(8,128)S(1)} %all-to-all-done.1.r, f32[16,12,8,128]{3,2,1,0:T(8,128)S(1)} %source1.1.a), custom_call_target="tpu_custom_call" | custom-call | tf_op jit(solution)/shard_map/depth/pallas_call | solution.py:602
  60.7 20.4 %all_to_all.31 = f32[16,2,12,8,128]{4,3,1,2,0:T(8,128)S(1)} all-to-all(f32[16,2,12,8,128]{4,3,1,2,0:T(8,128)S(1)} %copy.48), channel_id=1, replica_groups=mesh['gx'=8,'gy'=16] {'gy'}, dimensions={0} | all-to-all | bytes 3145728 | tf_op jit(solution)/shard_map/all_to_all | solution.py:640
  81.1 7.5 %collective-permute-start.5 = (f32[16,2,8,128]{3,2,1,0:T(8,128)S(1)}, f32[16,2,8,128]{3,2,1,0:T(8,128)S(1)}, u32[]{:S(2)}, u32[]{:S(2)}) collective-permute-start(f32[16,2,8,128]{3,2,1,0:T(8,128)S(1)} %get-tuple-element.47), channel_id=1, source_target_pairs={{16,0},{32,16},{48,32},{64,48},{80,64},{96,80},{112,96},{0,112},{1... | collective-permute-start | bytes 393224 | tf_op jit(solution)/shard_map/ppermute | solution.py:636
  88.8 2.3 %collective-permute-done.5.nxt = f32[16,2,8,128]{3,2,1,0:T(8,128)S(1)} collective-permute-done((f32[16,2,8,128]{3,2,1,0:T(8,128)S(1)}, f32[16,2,8,128]{3,2,1,0:T(8,128)S(1)}, u32[]{:S(2)}, u32[]{:S(2)}) %collective-permute-start.5) | collective-permute-done | bytes 131104 | tf_op jit(solution)/shard_map/ppermute | solution.py:636
  91.1 3.1 %collective-permute-done.4.prv = f32[16,2,8,128]{3,2,1,0:T(8,128)S(1)} collective-permute-done((f32[16,2,8,128]{3,2,1,0:T(8,128)S(1)}, f32[16,2,8,128]{3,2,1,0:T(8,128)S(1)}, u32[]{:S(2)}, u32[]{:S(2)}) %collective-permute-start.4) | collective-permute-done | bytes 131104 | tf_op jit(solution)/shard_map/ppermute | solution.py:632
  94.2 12.4 %normal.1 = (f32[16,12,8,128]{3,2,1,0:T(8,128)S(1)}, f32[16,8,128]{2,1,0:T(8,128)S(1)}, f32[16,8,128]{2,1,0:T(8,128)S(1)}) custom-call(s32[4,96]{1,0:T(4,128)S(1)} %pad_add_fusion.tab, f32[16,2,12,8,128]{4,3,2,1,0:T(8,128)S(1)} %copy.51.x, f32[16,2,8,128]{3,2,1,0:T(8,128)S(1)} %collective-permute-done.4.prv, f32[16,2,8,128]{3,2,1,0:T(8,128)S(1)} %collective-permute-done.5.nxt), custom_call_target="tpu_custom_call" | custom-call | tf_op jit(solution)/shard_map/normal/pallas_call | solution.py:559
  107.2 1.4 collective-permute-done.6
  108.6 3.0 %collective-permute-done.7 = f32[16,8,128]{2,1,0:T(8,128)S(1)} collective-permute-done((f32[16,8,128]{2,1,0:T(8,128)S(1)}, f32[16,8,128]{2,1,0:T(8,128)S(1)}, u32[]{:S(2)}, u32[]{:S(2)}) %collective-permute-start.7) | collective-permute-done | bytes 65568 | tf_op jit(solution)/shard_map/ppermute | solution.py:632
  111.6 14.9 %all_to_all.32.r.adj1 = f32[16,12,8,128]{3,2,1,0:T(8,128)S(1)} all-to-all(f32[16,12,8,128]{3,2,1,0:T(8,128)S(1)} %fusion), channel_id=1, replica_groups=mesh['gx'=8,'gy'=16] {'gy'}, dimensions={0} | all-to-all | bytes 1572864 | tf_op jit(solution)/shard_map/all_to_all | solution.py:640
  126.5 2.2 %depth_adjoint.1 = f32[16,12,8,128]{3,2,1,0:T(8,128)S(1)} custom-call(s32[6]{0:T(128)S(1)} %slice_bitcast_fusion.9.code, f32[8,4]{1,0:T(8,128)S(1)} %copy-done.4, f32[16,12,8,128]{3,2,1,0:T(8,128)S(1)} %all_to_all.32.r.adj1), custom_call_target="tpu_custom_call" | custom-call | tf_op jit(solution)/shard_map/depth_adjoint/pallas_call | solution.py:621
  128.7 14.8 %all_to_all.33.v = f32[16,12,8,128]{3,2,1,0:T(8,128)S(1)} all-to-all(f32[16,12,8,128]{3,2,1,0:T(8,128)S(1)} %depth_adjoint.1), channel_id=1, replica_groups=mesh['gx'=8,'gy'=16] {'gy'}, dimensions={0} | all-to-all | bytes 1572864 | tf_op jit(solution)/shard_map/all_to_all | solution.py:640
  143.4 5.5 %push.1 = f32[16,13,8,128]{3,2,1,0:T(8,128)S(1)} custom-call(s32[4,96]{1,0:T(4,128)S(1)} %pad_add_fusion.tab, f32[16,12,8,128]{3,2,1,0:T(8,128)S(1)} %all_to_all.33.v), custom_call_target="tpu_custom_call" | custom-call | tf_op jit(solution)/shard_map/push/pallas_call | solution.py:501
  149.0 15.1 %all_to_all.34.adj0 = f32[16,13,8,128]{3,2,1,0:T(8,128)S(1)} all-to-all(f32[16,13,8,128]{3,2,1,0:T(8,128)S(1)} %push.1), channel_id=1, replica_groups=mesh['gx'=8,'gy'=16] {'gy'}, dimensions={0} | all-to-all | bytes 1703936 | tf_op jit(solution)/shard_map/all_to_all | solution.py:640
  164.0 2.9 %collective-permute-start.8 = (f32[16,8,128]{2,1,0:T(8,128)S(1)}, f32[16,8,128]{2,1,0:T(8,128)S(1)}, u32[]{:S(2)}, u32[]{:S(2)}) collective-permute-start(f32[16,8,128]{2,1,0:T(8,128)S(1)} %slice_bitcast_fusion.2), channel_id=1, source_target_pairs={{16,0},{32,16},{48,32},{64,48},{80,64},{96,80},{112,96},{0,112},{1... | collective-permute-start | bytes 196616 | tf_op jit(solution)/shard_map/ppermute | solution.py:636
  167.0 4.7 %force.1.prior = f32[3,96,16,128]{3,2,1,0:T(8,128)} custom-call(f32[16,12,8,128]{3,2,1,0:T(8,128)S(1)} %all_to_all.32.r.adj1, f32[16,13,8,128]{3,2,1,0:T(8,128)S(1)} %all_to_all.34.adj0, f32[2,96,16,128]{3,2,1,0:T(8,128)S(1)} %copy-done.1, f32[16,128]{1,0:T(8,128)S(1)} %get-tuple-element.56.top.t1, f32[16,128]{1,0:T(8,128)S(1)} %get-tuple-element.54.bottom.b1, ...), custom_call_target="tpu_custom_call" | custom-call | flops 20000000 | bytes 6000000 | tf_op jit(solution)/shard_map/force/pallas_call | solution.py:313
  171.7 1.2 force_edge.1
  (57 shorter events, 3.0 us)
Async XLA Ops:
  1.5 11.5 %collective-permute-start = (f32[2,96,128]{2,1,0:T(8,128)S(1)}, f32[2,96,128]{2,1,0:T(8,128)S(1)}, u32[]{:S(2)}, u32[]{:S(2)}) collective-permute-start(f32[2,96,128]{2,1,0:T(8,128)S(1)} %bitcast.51), channel_id=1, source_target_pairs={{0,1},{1,2},{2,3},{3,4},{4,5},{5,6},{6,7},{7,8},{8,9},{9,10},{10,1... | collective-permute-start | bytes 294920 | tf_op jit(solution)/shard_map/ppermute | solution.py:632
  3.3 9.7 %collective-permute-start.1 = (f32[2,96,128]{2,1,0:T(8,128)S(1)}, f32[2,96,128]{2,1,0:T(8,128)S(1)}, u32[]{:S(2)}, u32[]{:S(2)}) collective-permute-start(f32[2,96,128]{2,1,0:T(8,128)S(1)} %bitcast.50), channel_id=1, source_target_pairs={{1,0},{2,1},{3,2},{4,3},{5,4},{6,5},{7,6},{8,7},{9,8},{10,9},{11,1... | collective-permute-start | bytes 294920 | tf_op jit(solution)/shard_map/ppermute | solution.py:636
  7.7 1.4 copy-start
  9.1 1.7 copy-start.2
  10.8 5.5 %copy-start.5 = (s32[3,6,1]{1,2,0:T(1,128)S(1)}, s32[3,6,1]{1,2,0:T(1,128)}, u32[]{:S(2)}) copy-start(s32[3,6,1]{1,2,0:T(1,128)} %param.14) | copy-start | bytes 220
  10.8 5.6 %copy-start.6 = (s32[1,1,16,2]{2,3,1,0:T(2,128)S(1)}, s32[1,1,16,2]{2,3,1,0:T(2,128)}, u32[]{:S(2)}) copy-start(s32[1,1,16,2]{2,3,1,0:T(2,128)} %param.13) | copy-start | bytes 388
  10.8 5.8 %copy-start.7 = (s32[6,1]{0,1:T(1,128)S(1)}, s32[6,1]{0,1:T(1,128)}, u32[]{:S(2)}) copy-start(s32[6,1]{0,1:T(1,128)} %param.12) | copy-start | bytes 76
  13.0 7.8 %collective-permute-start.2 = (f32[5,16,128]{2,1,0:T(8,128)S(1)}, f32[5,16,128]{2,1,0:T(8,128)S(1)}, u32[]{:S(2)}, u32[]{:S(2)}) collective-permute-start(f32[5,16,128]{2,1,0:T(8,128)S(1)} %get-tuple-element.42.my_prv), channel_id=1, source_target_pairs={{16,0},{32,16},{48,32},{64,48},{80,64},{96,80},{112,96},{0,112},{1... | collective-permute-start | bytes 122888 | tf_op jit(solution)/shard_map/ppermute | solution.py:636
  16.2 4.6 %collective-permute-start.3 = (f32[4,16,128]{2,1,0:T(8,128)S(1)}, f32[4,16,128]{2,1,0:T(8,128)S(1)}, u32[]{:S(2)}, u32[]{:S(2)}) collective-permute-start(f32[4,16,128]{2,1,0:T(8,128)S(1)} %get-tuple-element.43.my_nxt), channel_id=1, source_target_pairs={{0,16},{16,32},{32,48},{48,64},{64,80},{80,96},{96,112},{112,0},{1... | collective-permute-start | bytes 98312 | tf_op jit(solution)/shard_map/ppermute | solution.py:632
  37.5 9.5 %copy-start.1 = (f32[2,96,16,128]{3,2,1,0:T(8,128)S(1)}, f32[2,96,16,128]{3,2,1,0:T(8,128)}, u32[]{:S(2)}) copy-start(f32[2,96,16,128]{3,2,1,0:T(8,128)} %s0.3) | copy-start | bytes 4718596
  43.2 15.2 %all-to-all-start.1 = ((f32[16,12,8,128]{3,2,1,0:T(8,128)}), f32[16,12,8,128]{3,2,1,0:T(8,128)S(1)}, u32[]{:S(2)}, u32[]{:S(2)}) async-start(f32[16,12,8,128]{3,2,1,0:T(8,128)} %pull.1), calls=%async_computation.1 | async-start | bytes 1572864 | tf_op jit(solution)/shard_map/all_to_all | solution.py:640
  46.9 1.7 copy-start.3
  48.6 9.8 %copy-start.4 = (f32[8,4]{1,0:T(8,128)S(1)}, f32[8,4]{1,0:T(8,128)}, u32[]{:S(2)}) copy-start(f32[8,4]{1,0:T(8,128)} %constant.89.clone.wt) | copy-start | bytes 388
  81.1 10.0 %collective-permute-start.5 = (f32[16,2,8,128]{3,2,1,0:T(8,128)S(1)}, f32[16,2,8,128]{3,2,1,0:T(8,128)S(1)}, u32[]{:S(2)}, u32[]{:S(2)}) collective-permute-start(f32[16,2,8,128]{3,2,1,0:T(8,128)S(1)} %get-tuple-element.47), channel_id=1, source_target_pairs={{16,0},{32,16},{48,32},{64,48},{80,64},{96,80},{112,96},{0,112},{1... | collective-permute-start | bytes 393224 | tf_op jit(solution)/shard_map/ppermute | solution.py:636
  88.6 5.6 %collective-permute-start.4 = (f32[16,2,8,128]{3,2,1,0:T(8,128)S(1)}, f32[16,2,8,128]{3,2,1,0:T(8,128)S(1)}, u32[]{:S(2)}, u32[]{:S(2)}) collective-permute-start(f32[16,2,8,128]{3,2,1,0:T(8,128)S(1)} %get-tuple-element.48), channel_id=1, source_target_pairs={{0,16},{16,32},{32,48},{48,64},{64,80},{80,96},{96,112},{112,0},{1... | collective-permute-start | bytes 393224 | tf_op jit(solution)/shard_map/ppermute | solution.py:632
  106.6 2.0 %collective-permute-start.6 = (f32[16,8,128]{2,1,0:T(8,128)S(1)}, f32[16,8,128]{2,1,0:T(8,128)S(1)}, u32[]{:S(2)}, u32[]{:S(2)}) collective-permute-start(f32[16,8,128]{2,1,0:T(8,128)S(1)} %get-tuple-element.45), channel_id=1, source_target_pairs={{16,0},{32,16},{48,32},{64,48},{80,64},{96,80},{112,96},{0,112},{1... | collective-permute-start | bytes 196616 | tf_op jit(solution)/shard_map/ppermute | solution.py:636
  106.7 4.9 %collective-permute-start.7 = (f32[16,8,128]{2,1,0:T(8,128)S(1)}, f32[16,8,128]{2,1,0:T(8,128)S(1)}, u32[]{:S(2)}, u32[]{:S(2)}) collective-permute-start(f32[16,8,128]{2,1,0:T(8,128)S(1)} %get-tuple-element.46), channel_id=1, source_target_pairs={{0,16},{16,32},{32,48},{48,64},{64,80},{80,96},{96,112},{112,0},{1... | collective-permute-start | bytes 196616 | tf_op jit(solution)/shard_map/ppermute | solution.py:632
  164.0 7.7 %collective-permute-start.9 = (f32[16,8,128]{2,1,0:T(8,128)S(1)}, f32[16,8,128]{2,1,0:T(8,128)S(1)}, u32[]{:S(2)}, u32[]{:S(2)}) collective-permute-start(f32[16,8,128]{2,1,0:T(8,128)S(1)} %slice_bitcast_fusion.2), channel_id=1, source_target_pairs={{0,16},{16,32},{32,48},{48,64},{64,80},{80,96},{96,112},{112,0},{1... | collective-permute-start | bytes 196616 | tf_op jit(solution)/shard_map/ppermute | solution.py:632
  164.0 7.7 %collective-permute-start.8 = (f32[16,8,128]{2,1,0:T(8,128)S(1)}, f32[16,8,128]{2,1,0:T(8,128)S(1)}, u32[]{:S(2)}, u32[]{:S(2)}) collective-permute-start(f32[16,8,128]{2,1,0:T(8,128)S(1)} %slice_bitcast_fusion.2), channel_id=1, source_target_pairs={{16,0},{32,16},{48,32},{64,48},{80,64},{96,80},{112,96},{0,112},{1... | collective-permute-start | bytes 196616 | tf_op jit(solution)/shard_map/ppermute | solution.py:636

commit v3 on v2

v3 whole, which is shorter than its diff:
```python
import functools

import jax
import jax.numpy as jnp
import numpy as np
from jax import lax
from jax.experimental import pallas as pl
from jax.experimental.pallas import tpu as pltpu
from jax.sharding import PartitionSpec as P

QF = 8
PEERS = 16
RB = 12
BRICKS = 6


def weights_of(f):
    return np.array(
        [
            -f * (f - 1.0) * (f - 2.0) / 6.0,
            (f + 1.0) * (f - 1.0) * (f - 2.0) / 2.0,
            -(f + 1.0) * f * (f - 2.0) / 2.0,
            (f + 1.0) * f * (f - 1.0) / 6.0,
        ]
    )


WEIGHTS = np.stack([weights_of(k / QF) for k in range(QF)])
PAIRS = np.stack([[np.dot(w[: 4 - d], w[d:]) for d in range(4)] for w in WEIGHTS])


def shift_matrix():
    m = np.zeros((2, 8, 16, 3, 8, 16), np.float32)
    for r in range(8):
        for j in range(16):
            for n, d in enumerate((-1, 1, 2)):
                inside = 0 <= j + d < 16
                m[0 if inside else 1, r, (j + d) % 16, n, r, j] = 1.0
    return m.reshape(256, 384)


SHIFT = shift_matrix()
BF16 = jnp.bfloat16

VMEM = pl.BlockSpec(memory_space=pltpu.VMEM)
SMEM = pl.BlockSpec(memory_space=pltpu.SMEM)
F32 = jnp.float32


def params(mib=48):
    return pltpu.CompilerParams(vmem_limit_bytes=mib * 1024 * 1024)


def turned_shape(blocks=RB):
    return jax.ShapeDtypeStruct((PEERS, blocks, 8, 128), F32)


def gradients(st, top, bottom, left, right, rb, k):
    rows = pl.ds(rb * 8, 8)
    x = st[k, rows]
    before = st[k, jnp.maximum(rb * 8 - 1, 0)]
    before = jnp.where(rb == 0, jnp.zeros_like(before) if top is None else top[2 + k], before)
    after = st[k, jnp.minimum(rb * 8 + 8, 95)]
    after = jnp.where(rb == RB - 1, jnp.zeros_like(after) if bottom is None else bottom[3 + k], after)
    up = jnp.concatenate([x[1:], after[None]], axis=0)
    down = jnp.concatenate([before[None], x[:-1]], axis=0)
    col = lax.broadcasted_iota(jnp.int32, x.shape, 1)
    lo = 0.0 if left is None else left[k, rows][:, None, :]
    hi = 0.0 if right is None else right[k, rows][:, None, :]
    nxt = jnp.where(col == 15, hi, pltpu.roll(x, 15, 1))
    prv = jnp.where(col == 0, lo, pltpu.roll(x, 1, 1))
    return (
        (up - down) * 0.5,
        (nxt - prv) * 0.5,
        (pltpu.roll(x, 127, 2) - pltpu.roll(x, 1, 2)) * 0.5,
    )


def turn(x):
    return x.reshape(128, 128).T.reshape(PEERS, 8, 128)


def contract(v, g):
    return -0.5 * (v[0] * g[0] + v[1] * g[1] + v[2] * g[2])


CHUNKS = 4


def pre_kernel(v_hbm, st_hbm, out0, out1, sides, to_prv, to_nxt, v, st, sems):
    rows = 96 // CHUNKS
    copies = [pltpu.make_async_copy(st_hbm.at[k], st.at[k], sems.at[k]) for k in range(2)]
    for i in range(CHUNKS):
        part = pl.ds(i * rows, rows)
        copies.append(pltpu.make_async_copy(v_hbm.at[:, part], v.at[:, part], sems.at[2 + i]))
    for c in copies:
        c.start()
    copies[0].wait()
    copies[1].wait()
    for i in range(CHUNKS):
        copies[2 + i].wait()

        @pl.loop(i * RB // CHUNKS, (i + 1) * RB // CHUNKS)
        def _(rb):
            block = pl.ds(rb * 8, 8)
            vb = v[:, block]
            a = contract(vb, gradients(st, None, None, None, None, rb, 0))
            out0[:, rb] = turn(a)
            out1[:, rb] = turn(contract(vb, gradients(st, None, None, None, None, rb, 1)))
            sides[0, block] = 0.25 * vb[1, :, 0]
            sides[1, block] = -0.25 * vb[1, :, 15]

            @pl.when(rb == 0)
            def _():
                to_prv[0] = a[0]
                to_prv[2] = a[1]

            @pl.when(rb == RB - 1)
            def _():
                to_nxt[0] = a[7]

    to_prv[1] = v[0, 0]
    to_prv[3] = st[0, 0]
    to_prv[4] = st[1, 0]
    to_nxt[1] = v[0, 95]
    to_nxt[2] = st[0, 95]
    to_nxt[3] = st[1, 95]


def in_hbm(x):
    return pltpu.with_memory_space_constraint(x, pltpu.HBM)


def pre(velocity, states):
    hbm = pl.BlockSpec(memory_space=pltpu.HBM)
    return pl.pallas_call(
        pre_kernel,
        in_specs=[hbm, hbm],
        out_specs=[VMEM] * 5,
        out_shape=[
            turned_shape(RB + 1),
            turned_shape(),
            jax.ShapeDtypeStruct((2, 96, 128), F32),
            jax.ShapeDtypeStruct((5, 16, 128), F32),
            jax.ShapeDtypeStruct((4, 16, 128), F32),
        ],
        scratch_shapes=[
            pltpu.VMEM((3, 96, 16, 128), F32),
            pltpu.VMEM((2, 96, 16, 128), F32),
            pltpu.SemaphoreType.DMA((2 + CHUNKS,)),
        ],
        compiler_params=params(24),
        cost_estimate=COST,
        name="pre",
    )(in_hbm(velocity), in_hbm(states))


def rims_kernel(prv, nxt, sides, left, right, to_prv, to_nxt):
    col = lax.broadcasted_iota(jnp.int32, (16, 128), 0)

    def side(row):
        lo = sides[0, row : row + 1] * left[0, row : row + 1]
        hi = sides[1, row : row + 1] * right[0, row : row + 1]
        return jnp.where(col == 0, lo, 0.0) + jnp.where(col == 15, hi, 0.0)

    to_prv[0] = prv[0] + side(0)
    to_prv[1] = prv[1]
    to_prv[2] = prv[2] + side(1)
    to_prv[3] = prv[3]
    to_prv[4] = prv[4]
    to_nxt[0] = nxt[0] + side(95)
    to_nxt[1] = nxt[1]
    to_nxt[2] = nxt[2]
    to_nxt[3] = nxt[3]


def rims(prv, nxt, sides, left, right):
    return pl.pallas_call(
        rims_kernel,
        in_specs=[VMEM] * 5,
        out_specs=[VMEM, VMEM],
        out_shape=[jax.ShapeDtypeStruct((5, 16, 128), F32), jax.ShapeDtypeStruct((4, 16, 128), F32)],
        compiler_params=params(16),
        name="rims",
    )(prv, nxt, sides, left, right)


def columns_kernel(a0, a1, sides, left, right, out0, out1):
    col = lax.broadcasted_iota(jnp.int32, (8, 16, 128), 1)
    for k, (a, out) in enumerate(((a0, out0), (a1, out1))):
        for j in range(3):
            rows = pl.ds(8 * j, 8)
            lo = (sides[0, rows] * left[k, rows])[:, None, :]
            hi = (sides[1, rows] * right[k, rows])[:, None, :]
            out[:, j] = a[:, j] + turn(jnp.where(col == 0, lo, 0.0) + jnp.where(col == 15, hi, 0.0))


def columns(a0, a1, sides, left, right):
    block = pl.BlockSpec((PEERS, 3, 8, 128), lambda i: (0, i, 0, 0))
    side = pl.BlockSpec((2, 24, 128), lambda i: (0, i, 0))
    return pl.pallas_call(
        columns_kernel,
        grid=(RB // 3,),
        in_specs=[block, block, side, side, side],
        out_specs=[block, block],
        out_shape=[turned_shape(RB + 1), turned_shape()],
        input_output_aliases={0: 0, 1: 1},
        compiler_params=params(16),
        cost_estimate=COST,
        name="columns",
    )(a0, a1, sides, left, right)


def whole(shape):
    return pl.BlockSpec(shape, lambda i: (0,) * len(shape))


def natural3(f):
    return pl.BlockSpec((3, 8, 16, 128), lambda i: (0, f(i), 0, 0))


def turned(f):
    return pl.BlockSpec((PEERS, 1, 8, 128), lambda i: (0, f(i), 0, 0))


def same(i):
    return i


COST = pl.CostEstimate(flops=20_000_000, bytes_accessed=6_000_000, transcendentals=0)


def close_kernel(a0, a1, my_prv, my_nxt, from_nxt, from_prv, table, out0, out1):
    i = pl.program_id(0)
    row = lax.broadcasted_iota(jnp.int32, (8, 16, 128), 0)
    zero = jnp.zeros((8, 16, 128), F32)
    lane = lax.broadcasted_iota(jnp.int32, (PEERS, 8, 128), 2)

    @pl.when(i == 0)
    def _():
        for k, (a, out) in enumerate(((a0, out0), (a1, out1))):
            x = 0.25 * my_prv[1] * from_prv[2 + k]
            out[:, 0] = a[:, 0] + turn(jnp.where(row == 0, x[None], zero))

    @pl.when(i == 1)
    def _():
        for k, (a, out) in enumerate(((a0, out0), (a1, out1))):
            x = -0.25 * my_nxt[1] * from_nxt[3 + k]
            out[:, 0] = a[:, 0] + turn(jnp.where(row == 7, x[None], zero))

    @pl.when(i == 2)
    def _():
        before = from_prv[0] - 0.25 * from_prv[1] * my_prv[3]
        after = from_nxt[0] + 0.25 * from_nxt[1] * my_nxt[2]
        x = jnp.where(row == 7, before[None], zero)
        x = jnp.where(row == 0, after[None], x)
        x = jnp.where(row == 1, from_nxt[2][None], x)
        inner = (lane >= 32) & (lane < 112)
        out0[:, 0] = jnp.where(inner, table[...][None], turn(x))


def close(a0, a1, my_prv, my_nxt, from_nxt, from_prv, table):
    def block(i):
        return jnp.minimum(i * (RB - 1), RB)

    def kept(i):
        return jnp.minimum(i * (RB - 1), RB - 1)

    return pl.pallas_call(
        close_kernel,
        grid=(3,),
        in_specs=[
            turned(block),
            turned(kept),
            whole((5, 16, 128)),
            whole((4, 16, 128)),
            whole((5, 16, 128)),
            whole((4, 16, 128)),
            whole((1, 128)),
        ],
        out_specs=[turned(block), turned(kept)],
        out_shape=[turned_shape(RB + 1), turned_shape()],
        input_output_aliases={0: 0, 1: 1},
        compiler_params=params(16),
        name="close",
    )(a0, a1, my_prv, my_nxt, from_nxt, from_prv, table)


def force_block(adj1, adj0, st, edges, rb, out):
    b1 = (adj1.reshape(128, 128).T * -0.5).reshape(8, 16, 128)
    b0 = (adj0.reshape(128, 128).T * -0.5).reshape(8, 16, 128)
    g1 = gradients(st, *edges, rb, 1)
    g0 = gradients(st, *edges, rb, 0)
    for c in range(3):
        out[c] = b1 * g1[c] + b0 * g0[c]


def force_kernel(adj1, adj0, st, top, bottom, left, right, out):
    force_block(adj1[:, 0], adj0[:, 0], st, (top, bottom, left, right), pl.program_id(0) + 1, out)


def force_edge_kernel(adj1, adj0, st, top, bottom, left, right, from_nxt, from_prv, prior, out):
    i = pl.program_id(0)
    lane = lax.broadcasted_iota(jnp.int32, (PEERS, 8, 128), 2)
    x = jnp.where((i == 0) & (lane < 32), from_prv[...], 0.0)
    x = x + jnp.where((i == 1) & (lane >= 112), from_nxt[...], 0.0)
    force_block(adj1[:, 0], adj0[:, 0] + x, st, (top, bottom, left, right), i * (RB - 1), out)


def force(adj1, adj0, states, edges):
    fixed = [whole((2, 96, 16, 128)), whole((4, 16, 128)), whole((5, 16, 128)), whole((2, 96, 128)), whole((2, 96, 128))]
    shape = jax.ShapeDtypeStruct((3, 96, 16, 128), F32)
    rim = adj0[:, RB]
    from_nxt = to_prev(rim, "gx", lax.axis_size("gx"))
    from_prv = to_next(rim, "gx", lax.axis_size("gx"))
    args = (adj1, adj0, states, *edges)

    def inner(i):
        return i + 1

    def outer(i):
        return i * (RB - 1)

    main = pl.pallas_call(
        force_kernel,
        grid=(RB - 2,),
        in_specs=[turned(inner), turned(inner)] + fixed,
        out_specs=natural3(inner),
        out_shape=shape,
        compiler_params=params(24),
        cost_estimate=COST,
        name="force",
    )(*args)
    return pl.pallas_call(
        force_edge_kernel,
        grid=(2,),
        in_specs=[turned(outer), turned(outer)]
        + fixed
        + [whole((PEERS, 8, 128)), whole((PEERS, 8, 128)), pl.BlockSpec(memory_space=pl.ANY)],
        out_specs=natural3(outer),
        out_shape=shape,
        input_output_aliases={9: 0},
        compiler_params=params(24),
        name="force_edge",
    )(*args, from_nxt, from_prv, main)


def lanes():
    return lax.broadcasted_iota(jnp.int32, (8, 128), 1)


def split(x):
    hi = x.astype(BF16)
    return hi, (x - hi.astype(F32)).astype(BF16)


def load_taps(lhs, taps, e, x):
    col = lax.broadcasted_iota(jnp.int32, x.shape, 2) % 16
    after = jnp.concatenate([x[1:], x[:1]], axis=0)
    before = jnp.concatenate([x[-1:], x[:-1]], axis=0)
    xh, xl = split(x.reshape(128, 128))
    eh, el = split(jnp.where(col < 2, after, before).reshape(128, 128))
    rows = pl.ds(e * 128, 128)
    lhs[rows, 0:128] = xh
    lhs[rows, 128:256] = eh
    lhs[rows, 256:384] = xl
    lhs[rows, 384:512] = el
    taps[1, pl.ds(e * PEERS, PEERS)] = x


def shift_taps(lhs, shift, taps, blocks):
    m = shift[...]
    y = jnp.dot(lhs[0 : blocks * 128, 0:512], jnp.concatenate([m, m], axis=0), preferred_element_type=F32)
    for n, t in enumerate((0, 2, 3)):
        taps[t, 0 : blocks * PEERS] = y[:, n * 128 : n * 128 + 128].reshape(blocks * PEERS, 8, 128)


def shift_taps_adjoint(lhs, shift_t, acc, put):
    @pl.loop(0, RB + 2)
    def _(e):
        rows = pl.ds(e * 128, 128)
        for n, t in enumerate((0, 2, 3)):
            h, l = split(acc[t, pl.ds(e * PEERS, PEERS)].reshape(128, 128))
            lhs[rows, n * 128 : n * 128 + 128] = h
            lhs[rows, 384 + n * 128 : 512 + n * 128] = l

    m = shift_t[...]
    y = jnp.dot(lhs[...], jnp.concatenate([m, m], axis=0), preferred_element_type=F32)
    col = lax.broadcasted_iota(jnp.int32, (PEERS, 8, 128), 2) % 16
    for e in range(RB + 2):
        own = y[e * 128 : e * 128 + 128, :128].reshape(PEERS, 8, 128)
        rim = y[e * 128 : e * 128 + 128, 128:].reshape(PEERS, 8, 128)
        after = jnp.concatenate([rim[-1:], rim[:-1]], axis=0)
        before = jnp.concatenate([rim[1:], rim[:1]], axis=0)
        put(e, acc[1, e * PEERS : (e + 1) * PEERS] + own + jnp.where(col < 2, after, before))


def fill_weights(wv, values):
    for f in range(QF):
        for t in range(4):
            wv[f, t] = jnp.full((8, 128), float(values[f, t]), F32)


def brick_plan(tab, wv, b):
    base = tab[0, b]
    u = tab[1, b]
    v = tab[2, b]
    return base, [wv[u, t] for t in range(4)], [wv[v, t] for t in range(4)]


def brick_columns(taps, base, wc):
    c = []
    for i in range(4):
        acc = [wc[t] * taps[t, base + i * PEERS] for t in range(4)]
        c.append((acc[0] + acc[1]) + (acc[2] + acc[3]))
    return c


def brick_rows(wr, c):
    lane = lanes()
    outs = []
    for h in range(2):
        prv, cur, nxt = c[h], c[h + 1], c[h + 2]
        outs.append(
            (wr[0] * pltpu.roll(jnp.where(lane >= 112, prv, cur), 16, 1) + wr[1] * cur)
            + (
                wr[2] * pltpu.roll(jnp.where(lane < 16, nxt, cur), 112, 1)
                + wr[3] * pltpu.roll(jnp.where(lane < 32, nxt, cur), 96, 1)
            )
        )
    return outs


def brick_rows_adjoint(wr, v):
    lane = lanes()
    lo, own, hi = [], [], []
    for h in range(2):
        p0 = wr[0] * pltpu.roll(v[h], 112, 1)
        p2 = wr[2] * pltpu.roll(v[h], 16, 1)
        p3 = wr[3] * pltpu.roll(v[h], 32, 1)
        lo.append(jnp.where(lane >= 112, p0, 0.0))
        own.append(
            (wr[1] * v[h] + jnp.where(lane >= 112, 0.0, p0))
            + (jnp.where(lane < 16, 0.0, p2) + jnp.where(lane < 32, 0.0, p3))
        )
        hi.append(jnp.where(lane < 16, p2, 0.0) + jnp.where(lane < 32, p3, 0.0))
    return [lo[0], own[0] + lo[1], own[1] + hi[0], hi[1]]


def brick_add(acc, base, wc, c):
    for i in range(4):
        for t in range(4):
            acc[t, base + i * PEERS] = acc[t, base + i * PEERS] + wc[t] * c[i]


BUF = pltpu.VMEM((BRICKS, 4, 8, 128), F32)


def each_peer(first, second, bufs):
    for k in range(BRICKS):
        first(0, k, bufs[0])

    @pl.loop(0, PEERS // 2)
    def _(i):
        d = 2 * i
        for k in range(BRICKS):
            second(d, k, bufs[0])
            first(d + 1, k, bufs[1])
        for k in range(BRICKS):
            second(d + 1, k, bufs[1])
            first(jnp.minimum(d + 2, PEERS - 1), k, bufs[0])


def pull_kernel(tab, shift, x, out, taps, wv, lhs, *bufs):
    fill_weights(wv, WEIGHTS)
    load_taps(lhs, taps, 0, x[:, RB])

    @pl.loop(0, RB)
    def _(rb):
        load_taps(lhs, taps, rb + 1, x[:, rb])

    shift_taps(lhs, shift, taps, RB + 1)
    for t in range(4):
        taps[t, (RB + 1) * PEERS :] = taps[t, 0:PEERS]

    def first(d, k, buf):
        base, _, wc = brick_plan(tab, wv, d * BRICKS + k)
        c = brick_columns(taps, base, wc)
        for i in range(4):
            buf[k, i] = c[i]

    def second(d, k, buf):
        _, wr, _ = brick_plan(tab, wv, d * BRICKS + k)
        o = brick_rows(wr, [buf[k, i] for i in range(4)])
        for h in range(2):
            out[d, 2 * k + h] = o[h]

    each_peer(first, second, bufs)


TAPS = pltpu.VMEM((4, PEERS * (RB + 2), 8, 128), F32)
WV = pltpu.VMEM((QF, 4, 8, 128), F32)


LHS = pltpu.VMEM(((RB + 2) * 128, 768), BF16)


def pull(tab, shift, x):
    return pl.pallas_call(
        pull_kernel,
        in_specs=[SMEM, VMEM, VMEM],
        out_specs=VMEM,
        out_shape=turned_shape(),
        scratch_shapes=[TAPS, WV, LHS, BUF, BUF],
        compiler_params=params(24),
        name="pull",
    )(tab, shift, x)


def clear(acc):
    @pl.loop(0, RB + 2)
    def _(e):
        acc[:, pl.ds(e * PEERS, PEERS)] = jnp.zeros((4, PEERS, 8, 128), F32)


def push_kernel(tab, shift_t, v, out, acc, wv, lhs, *bufs):
    fill_weights(wv, WEIGHTS)
    clear(acc)

    def first(d, k, buf):
        _, wr, _ = brick_plan(tab, wv, d * BRICKS + k)
        c = brick_rows_adjoint(wr, [v[d, 2 * k], v[d, 2 * k + 1]])
        for i in range(4):
            buf[k, i] = c[i]

    def second(d, k, buf):
        base, _, wc = brick_plan(tab, wv, d * BRICKS + k)
        brick_add(acc, base, wc, [buf[k, i] for i in range(4)])

    each_peer(first, second, bufs)

    def put(e, block):
        if e == 0:
            out[:, RB] = block
        elif e == RB + 1:
            out[:, RB] = out[:, RB] + block
        else:
            out[:, e - 1] = block

    shift_taps_adjoint(lhs, shift_t, acc, put)


def push(tab, shift_t, v):
    return pl.pallas_call(
        push_kernel,
        in_specs=[SMEM, VMEM, VMEM],
        out_specs=VMEM,
        out_shape=turned_shape(RB + 1),
        scratch_shapes=[TAPS, WV, LHS, BUF, BUF],
        compiler_params=params(24),
        name="push",
    )(tab, shift_t, v)


def normal_kernel(tab, shift, shift_t, x, prv, nxt, out, lo, hi, taps, acc, wv, kv, lhs, *bufs):
    fill_weights(wv, WEIGHTS)
    fill_weights(kv, PAIRS)
    clear(acc)
    for q in range(2):
        load_taps(lhs, taps.at[q], 0, prv[:, q])
        load_taps(lhs, taps.at[q], RB + 1, nxt[:, q])

        @pl.loop(0, RB)
        def _(rb):
            load_taps(lhs, taps.at[q], rb + 1, x[:, q, rb])

        shift_taps(lhs, shift, taps.at[q], RB + 2)

    def first(d, k, buf):
        sub = lax.broadcasted_iota(jnp.int32, (8, 128), 0)
        base, _, wc = brick_plan(tab, wv, d * BRICKS + k)
        c0 = brick_columns(taps.at[0], base, wc)
        c1 = brick_columns(taps.at[1], base, wc)
        f = tab[3, d * BRICKS + k]
        kw = [kv[f, t] for t in range(4)]
        for i in range(4):
            at = [pltpu.roll(jnp.where(sub >= a, c0[i], c1[i]), 8 - a, 0) for a in range(1, 8)]
            near = kw[0] * at[3] + kw[1] * (at[2] + at[4])
            buf[k, i] = near + (kw[2] * (at[1] + at[5]) + kw[3] * (at[0] + at[6]))

    def second(d, k, buf):
        base, wr, wc = brick_plan(tab, wv, d * BRICKS + k)
        c = brick_rows_adjoint(wr, brick_rows(wr, [buf[k, i] for i in range(4)]))
        brick_add(acc, base, wc, c)

    each_peer(first, second, bufs)

    def put(e, block):
        if e == 0:
            lo[...] = block
        elif e == RB + 1:
            hi[...] = block
        else:
            out[:, e - 1] = block

    shift_taps_adjoint(lhs, shift_t, acc, put)


EDGE = jax.ShapeDtypeStruct((PEERS, 8, 128), F32)


def normal(tab, shift, shift_t, x, prv, nxt):
    return pl.pallas_call(
        normal_kernel,
        in_specs=[SMEM, VMEM, VMEM, VMEM, VMEM, VMEM],
        out_specs=[VMEM, VMEM, VMEM],
        out_shape=[turned_shape(), EDGE, EDGE],
        scratch_shapes=[
            pltpu.VMEM((2, 4, PEERS * (RB + 2), 8, 128), F32),
            TAPS,
            WV,
            WV,
            LHS,
            BUF,
            BUF,
        ],
        compiler_params=params(24),
        name="normal",
    )(tab, shift, shift_t, x, prv, nxt)


def depth_matrix(q, transpose):
    n = q // QF
    f = (q % QF).astype(F32) * (1.0 / QF)
    weights = (
        f * (f - 1.0) * (f - 2.0) * (-1.0 / 6.0),
        (f + 1.0) * (f - 1.0) * (f - 2.0) * 0.5,
        (f + 1.0) * f * (f - 2.0) * -0.5,
        (f + 1.0) * f * (f - 1.0) * (1.0 / 6.0),
    )
    i = lax.broadcasted_iota(jnp.int32, (128, 128), 0)
    j = lax.broadcasted_iota(jnp.int32, (128, 128), 1)
    off = (i - j if transpose else j - i) + (257 - n)
    off = jnp.bitwise_and(off, 127)
    w = jnp.zeros((128, 128), F32)
    for m in range(4):
        w = jnp.where(off == m, weights[m], w)
    return w


def depth_product(q, transpose, r, k):
    wh, wl = split(depth_matrix(q, transpose))
    xh, xl = split(jnp.concatenate([r[:, 2 * k + h].reshape(128, 128) for h in range(2)], axis=1))
    y = jnp.dot(
        jnp.concatenate([wh, wl, wh], axis=1), jnp.concatenate([xh, xh, xl], axis=0), preferred_element_type=F32
    )
    return y[:, :128], y[:, 128:]


def depth_kernel(code, r, a, out):
    @pl.loop(0, BRICKS)
    def _(k):
        ys = depth_product(code[k], False, r, k)
        for h in range(2):
            u = ys[h] + a[:, 2 * k + h].reshape(128, 128)
            tiles = pltpu.roll(u, 4, 0).reshape(PEERS, 8, 128)
            out[:, 0, 2 * k + h] = tiles
            out[:, 1, 2 * k + h] = jnp.concatenate([tiles[1:], tiles[:1]], axis=0)


def depth(code, r, a):
    return pl.pallas_call(
        depth_kernel,
        in_specs=[SMEM, VMEM, VMEM],
        out_specs=VMEM,
        out_shape=jax.ShapeDtypeStruct((PEERS, 2, RB, 8, 128), F32),
        compiler_params=params(24),
        name="depth",
    )(code, r, a)


def depth_adjoint_kernel(code, r, out):
    @pl.loop(0, BRICKS)
    def _(k):
        ys = depth_product(code[k], True, r, k)
        for h in range(2):
            out[:, 2 * k + h] = ys[h].reshape(PEERS, 8, 128)


def depth_adjoint(code, r):
    return pl.pallas_call(
        depth_adjoint_kernel,
        in_specs=[SMEM, VMEM],
        out_specs=VMEM,
        out_shape=turned_shape(),
        compiler_params=params(24),
        name="depth_adjoint",
    )(code, r)


def to_next(x, axis, count):
    return lax.ppermute(x, axis, [(i, (i + 1) % count) for i in range(count)])


def to_prev(x, axis, count):
    return lax.ppermute(x, axis, [((i + 1) % count, i) for i in range(count)])


def swap(x):
    return lax.all_to_all(x, "gy", split_axis=0, concat_axis=0, tiled=True)


def brick_table(raw):
    t = raw.astype(jnp.int32)
    slot = t[:, 32:38]
    sends = t[:, :32].reshape(PEERS, PEERS, 2).transpose(1, 0, 2).reshape(PEERS, 1, 32)
    hit = slot[:, :, None] == jnp.arange(32)[None, None, :]
    local = jnp.sum(jnp.where(hit, sends, 0), axis=2)
    rows = [2 * PEERS * local + slot // 2, t[:, 38:44], t[:, 44:50], t[:, 50:56] % QF]
    return jnp.stack(rows).reshape(4, PEERS * BRICKS)


def body(velocity, states, pull_plan, send_plan, codes):
    gx = lax.axis_size("gx")
    gy = lax.axis_size("gy")
    left = to_next(states[:, :, -1], "gy", gy)
    right = to_prev(states[:, :, 0], "gy", gy)
    a0, a1, sides, my_prv, my_nxt = pre(velocity, states)
    shift = jnp.asarray(SHIFT, BF16)
    shift_t = jnp.asarray(SHIFT.T, BF16)
    code = codes[2].reshape(BRICKS)
    mine = [send_plan.reshape(32), pull_plan.reshape(BRICKS), codes.reshape(3 * BRICKS)]
    table = jnp.concatenate([jnp.zeros((32,), jnp.int32)] + mine + [jnp.zeros((40,), jnp.int32)])
    table = table.astype(F32).reshape(1, 128)

    my_prv, my_nxt = rims(my_prv, my_nxt, sides, left, right)
    from_nxt = to_prev(my_prv, "gx", gx)
    from_prv = to_next(my_nxt, "gx", gx)
    a0, a1 = columns(a0, a1, sides, left, right)
    a0, a1 = close(a0, a1, my_prv, my_nxt, from_nxt, from_prv, table)
    a0, code = lax.optimization_barrier((a0, code))
    x = swap(a0)
    tab = brick_table(x[:, RB, 0, 32:88])
    r = swap(pull(tab, shift, x))
    u = swap(depth(code, r, a1))
    y, lo, hi = normal(tab, shift, shift_t, u, to_next(u[:, :, RB - 1], "gx", gx), to_prev(u[:, :, 0], "gx", gx))
    y = y.at[:, RB - 1].add(to_prev(lo, "gx", gx)).at[:, 0].add(to_next(hi, "gx", gx))
    adj1 = swap(y)
    v = swap(depth_adjoint(code, adj1))
    adj0 = swap(push(tab, shift_t, v))
    return force(adj1, adj0, states, (from_prv, from_nxt, left, right))


def solution(mesh):
    return jax.shard_map(
        body,
        mesh=mesh,
        in_specs=(
            P(None, "gx", "gy", None),
            P(None, "gx", "gy", None),
            P("gx", "gy"),
            P("gx", "gy", None, None),
            P(None, "gx", "gy"),
        ),
        out_specs=P(None, "gx", "gy", None),
        check_vma=False,
    )
```

time: 176 us -> 171 us (0.972)
  blocking collectives: 80 us -> 108 us
  waiting for transfers between devices: 20.3 us -> 9.41 us
  starting transfers between devices: 23.3 us -> 12.7 us
  Pallas kernels: 40 us -> 34.4 us
  local copies, waits for them, and re-layouts: 8.49 us -> 3.04 us
    all_to_all x5 -> x6, blocking collectives: 80 us -> 108 us  [swap(): return lax.all_to_all(x, 'gy', split_axis=0, concat_axis=0, tiled=True)]
    ppermute x5, starting transfers between devices: 17.4 us -> 9.94 us  [to_prev(): return lax.ppermute(x, axis, [((i + 1) % count, i) for i in range(count)])]
    all_to_all x1 -> x0, waiting for transfers between devices: 7.28 us -> none  [swap(): return lax.all_to_all(x, 'gy', split_axis=0, concat_axis=0, tiled=True)]
    pallas_call x12 -> x11, Pallas kernels: 40 us -> 34.4 us  [the longest x1 10.7 us: normal(): pl.pallas_call(normal_kernel, in_specs=[SMEM, VMEM, VMEM, VMEM, VMEM, VME...]
    unnamed x17 -> x13, local copies, waits for them, and re-layouts: 4.84 us -> 0.11 us
    all_to_all x1 -> x0, starting transfers between devices: 3.67 us -> none  [swap(): return lax.all_to_all(x, 'gy', split_axis=0, concat_axis=0, tiled=True)]
    ppermute x5, waiting for transfers between devices: 9.28 us -> 6.12 us  [to_next(): return lax.ppermute(x, axis, [(i, (i + 1) % count) for i in range(count)])]
  transfers between devices with their start and end apart: 11 -> 10, of which waited for: 6 -> 5; matrix products, arithmetic and copies ran while one was open for 1% -> 0% of each run, Pallas kernels for 6% -> 7%
where the time goes in v3:
time: 171 us; the launch traced here: 168 us
  blocking collectives  108 us (63%)
  Pallas kernels  34.4 us (20%)
  starting transfers between devices  12.7 us (7%)
  waiting for transfers between devices  9.41 us (6%)
  local copies, waits for them, and re-layouts  3.04 us (2%)
    all_to_all x6, blocking collectives, swap(): return lax.all_to_all(x, 'gy', split_axis=0, concat_axis=0, tiled=True)  108 us
    pallas_call x1, Pallas kernels, normal(): pl.pallas_call(normal_kernel, in_specs=[SMEM, VMEM, VMEM, VMEM, VMEM, VME...  10.7 us
    ppermute x5, starting transfers between devices, to_prev(): return lax.ppermute(x, axis, [((i + 1) % count, i) for i in range(count)])  9.94 us
    ppermute x5, waiting for transfers between devices, to_next(): return lax.ppermute(x, axis, [(i, (i + 1) % count) for i in range(count)])  6.12 us
    pallas_call x1, Pallas kernels, pre(): pl.pallas_call(pre_kernel, in_specs=[hbm, hbm], out_specs=[VMEM] * 5, out...  5.11 us
    pallas_call x1, Pallas kernels, force(): pl.pallas_call(force_kernel, grid=(RB - 2,), in_specs=[turned(inner), tur...  4.67 us
    pallas_call x1, Pallas kernels, push(): pl.pallas_call(push_kernel, in_specs=[SMEM, VMEM, VMEM], out_specs=VMEM,...  4.08 us
    pallas_call x1, Pallas kernels, pull(): pl.pallas_call(pull_kernel, in_specs=[SMEM, VMEM, VMEM], out_specs=VMEM,...  3.62 us
  transfers between devices with their start and end apart: 10, of which 5 were waited for; matrix products, arithmetic and copies ran while one was open for 0% of the time, Pallas kernels for 7%

profile of v3, /device:TPU:0, one launch (start us, length us, event | category | flops | bytes accessed | tf_op | source)
XLA Modules:
  0.0 168.0 jit_solution(17708882533236446995)
XLA Ops:
  0.0 1.5 fusion.6
  1.5 1.8 %collective-permute-start = (f32[2,96,128]{2,1,0:T(8,128)S(1)}, f32[2,96,128]{2,1,0:T(8,128)S(1)}, u32[]{:S(2)}, u32[]{:S(2)}) collective-permute-start(f32[2,96,128]{2,1,0:T(8,128)S(1)} %bitcast.39), channel_id=1, source_target_pairs={{0,1},{1,2},{2,3},{3,4},{4,5},{5,6},{6,7},{7,8},{8,9},{9,10},{10,1... | collective-permute-start | bytes 294920 | tf_op jit(solution)/shard_map/ppermute | solution.py:702
  3.3 3.7 %collective-permute-start.1 = (f32[2,96,128]{2,1,0:T(8,128)S(1)}, f32[2,96,128]{2,1,0:T(8,128)S(1)}, u32[]{:S(2)}, u32[]{:S(2)}) collective-permute-start(f32[2,96,128]{2,1,0:T(8,128)S(1)} %bitcast.38), channel_id=1, source_target_pairs={{1,0},{2,1},{3,2},{4,3},{5,4},{6,5},{7,6},{8,7},{9,8},{10,9},{11,1... | collective-permute-start | bytes 294920 | tf_op jit(solution)/shard_map/ppermute | solution.py:706
  7.0 5.1 %pre.1 = (f32[16,13,8,128]{3,2,1,0:T(8,128)S(1)}, f32[16,12,8,128]{3,2,1,0:T(8,128)S(1)}, f32[2,96,128]{2,1,0:T(8,128)S(1)}, f32[5,16,128]{2,1,0:T(8,128)S(1)}, f32[4,16,128]{2,1,0:T(8,128)S(1)}) custom-call(f32[3,96,16,128]{3,2,1,0:T(8,128)} %v_hbm.1, f32[2,96,16,128]{3,2,1,0:T(8,128)} %st.3), custom_call_target="tpu_custom_call" | custom-call | flops 20000000 | bytes 6000000 | tf_op jit(solution)/shard_map/pre/pallas_call | solution.py:136
  12.2 3.2 %collective-permute-start.2 = (f32[5,16,128]{2,1,0:T(8,128)S(1)}, f32[5,16,128]{2,1,0:T(8,128)S(1)}, u32[]{:S(2)}, u32[]{:S(2)}) collective-permute-start(f32[5,16,128]{2,1,0:T(8,128)S(1)} %get-tuple-element.52.my_prv), channel_id=1, source_target_pairs={{16,0},{32,16},{48,32},{64,48},{80,64},{96,80},{112,96},{0,112},{1... | collective-permute-start | bytes 122888 | tf_op jit(solution)/shard_map/ppermute | solution.py:706
  15.7 0.1 concatenate.24
  15.8 1.2 columns.1
  17.1 0.5 close.1
  17.6 19.5 %all_to_all.30.x = f32[16,13,8,128]{3,2,1,0:T(8,128)S(1)} all-to-all(f32[16,13,8,128]{3,2,1,0:T(8,128)S(1)} %get-tuple-element.55), channel_id=1, replica_groups=mesh['gx'=8,'gy'=16] {'gy'}, dimensions={0} | all-to-all | bytes 1703936 | tf_op jit(solution)/shard_map/all_to_all | solution.py:710
  37.5 0.3 select_reduce_fusion
  37.9 0.1 fusion.3
  38.4 3.6 %pull.1 = f32[16,12,8,128]{3,2,1,0:T(8,128)S(1)} custom-call(s32[4,96]{1,0:T(4,128)S(1)} %pad_add_fusion.tab, bf16[256,384]{1,0:T(8,128)(2,1)S(1)} %copy-done.2, f32[16,13,8,128]{3,2,1,0:T(8,128)S(1)} %all_to_all.30.x), custom_call_target="tpu_custom_call" | custom-call | tf_op jit(solution)/shard_map/pull/pallas_call | solution.py:509
  42.0 17.3 %all_to_all.31.r = f32[16,12,8,128]{3,2,1,0:T(8,128)S(1)} all-to-all(f32[16,12,8,128]{3,2,1,0:T(8,128)S(1)} %pull.1), channel_id=1, replica_groups=mesh['gx'=8,'gy'=16] {'gy'}, dimensions={0} | all-to-all | bytes 1572864 | tf_op jit(solution)/shard_map/all_to_all | solution.py:710
  59.4 1.7 %depth.1 = f32[16,2,12,8,128]{4,3,2,1,0:T(8,128)S(1)} custom-call(s32[6]{0:T(128)S(1)} %slice_bitcast_fusion.3.code, f32[16,12,8,128]{3,2,1,0:T(8,128)S(1)} %all_to_all.31.r, f32[16,12,8,128]{3,2,1,0:T(8,128)S(1)} %get-tuple-element.57.a), custom_call_target="tpu_custom_call" | custom-call | tf_op jit(solution)/shard_map/depth/pallas_call | solution.py:672
  61.1 0.1 copy.51
  61.2 24.5 %all_to_all.32 = f32[16,2,12,8,128]{4,3,1,2,0:T(8,128)S(1)} all-to-all(f32[16,2,12,8,128]{4,3,1,2,0:T(8,128)S(1)} %copy.51), channel_id=1, replica_groups=mesh['gx'=8,'gy'=16] {'gy'}, dimensions={0} | all-to-all | bytes 3145728 | tf_op jit(solution)/shard_map/all_to_all | solution.py:710
  85.8 0.5 collective-permute-start.4
  86.3 0.2 copy.54.x
  86.5 1.8 %collective-permute-done.5.nxt = f32[16,2,8,128]{3,2,1,0:T(8,128)S(1)} collective-permute-done((f32[16,2,8,128]{3,2,1,0:T(8,128)S(1)}, f32[16,2,8,128]{3,2,1,0:T(8,128)S(1)}, u32[]{:S(2)}, u32[]{:S(2)}) %collective-permute-start.5) | collective-permute-done | bytes 131104 | tf_op jit(solution)/shard_map/ppermute | solution.py:706
  88.3 3.1 %collective-permute-done.4.prv = f32[16,2,8,128]{3,2,1,0:T(8,128)S(1)} collective-permute-done((f32[16,2,8,128]{3,2,1,0:T(8,128)S(1)}, f32[16,2,8,128]{3,2,1,0:T(8,128)S(1)}, u32[]{:S(2)}, u32[]{:S(2)}) %collective-permute-start.4) | collective-permute-done | bytes 131104 | tf_op jit(solution)/shard_map/ppermute | solution.py:702
  91.4 10.7 %normal.1 = (f32[16,12,8,128]{3,2,1,0:T(8,128)S(1)}, f32[16,8,128]{2,1,0:T(8,128)S(1)}, f32[16,8,128]{2,1,0:T(8,128)S(1)}) custom-call(s32[4,96]{1,0:T(4,128)S(1)} %pad_add_fusion.tab, bf16[256,384]{1,0:T(8,128)(2,1)S(1)} %copy-done.2, bf16[384,256]{1,0:T(8,128)(2,1)S(1)} %copy-done.1, f32[16,2,12,8,128]{4,3,2,1,0:T(8,128)S(1)} %copy.54.x, ...), custom_call_target="tpu_custom_call" | custom-call | tf_op jit(solution)/shard_map/normal/pallas_call | solution.py:613
  102.1 0.5 collective-permute-start.7
  102.6 1.4 collective-permute-done.6
  104.0 3.0 %collective-permute-done.7 = f32[16,8,128]{2,1,0:T(8,128)S(1)} collective-permute-done((f32[16,8,128]{2,1,0:T(8,128)S(1)}, f32[16,8,128]{2,1,0:T(8,128)S(1)}, u32[]{:S(2)}, u32[]{:S(2)}) %collective-permute-start.7) | collective-permute-done | bytes 65568 | tf_op jit(solution)/shard_map/ppermute | solution.py:702
  107.0 16.3 %all_to_all.33.r.adj1 = f32[16,12,8,128]{3,2,1,0:T(8,128)S(1)} all-to-all(f32[16,12,8,128]{3,2,1,0:T(8,128)S(1)} %fusion), channel_id=1, replica_groups=mesh['gx'=8,'gy'=16] {'gy'}, dimensions={0} | all-to-all | bytes 1572864 | tf_op jit(solution)/shard_map/all_to_all | solution.py:710
  123.3 1.7 depth_adjoint.1
  125.0 15.0 %all_to_all.34.v = f32[16,12,8,128]{3,2,1,0:T(8,128)S(1)} all-to-all(f32[16,12,8,128]{3,2,1,0:T(8,128)S(1)} %depth_adjoint.1), channel_id=1, replica_groups=mesh['gx'=8,'gy'=16] {'gy'}, dimensions={0} | all-to-all | bytes 1572864 | tf_op jit(solution)/shard_map/all_to_all | solution.py:710
  140.1 4.1 %push.1 = f32[16,13,8,128]{3,2,1,0:T(8,128)S(1)} custom-call(s32[4,96]{1,0:T(4,128)S(1)} %pad_add_fusion.tab, bf16[384,256]{1,0:T(8,128)(2,1)S(1)} %copy-done.1, f32[16,12,8,128]{3,2,1,0:T(8,128)S(1)} %all_to_all.34.v), custom_call_target="tpu_custom_call" | custom-call | tf_op jit(solution)/shard_map/push/pallas_call | solution.py:554
  144.1 15.1 %all_to_all.35.adj0 = f32[16,13,8,128]{3,2,1,0:T(8,128)S(1)} all-to-all(f32[16,13,8,128]{3,2,1,0:T(8,128)S(1)} %push.1), channel_id=1, replica_groups=mesh['gx'=8,'gy'=16] {'gy'}, dimensions={0} | all-to-all | bytes 1703936 | tf_op jit(solution)/shard_map/all_to_all | solution.py:710
  159.2 2.9 %collective-permute-start.8 = (f32[16,8,128]{2,1,0:T(8,128)S(1)}, f32[16,8,128]{2,1,0:T(8,128)S(1)}, u32[]{:S(2)}, u32[]{:S(2)}) collective-permute-start(f32[16,8,128]{2,1,0:T(8,128)S(1)} %slice_bitcast_fusion.2), channel_id=1, source_target_pairs={{16,0},{32,16},{48,32},{64,48},{80,64},{96,80},{112,96},{0,112},{1... | collective-permute-start | bytes 196616 | tf_op jit(solution)/shard_map/ppermute | solution.py:706
  162.2 4.7 %force.1.prior = f32[3,96,16,128]{3,2,1,0:T(8,128)} custom-call(f32[16,12,8,128]{3,2,1,0:T(8,128)S(1)} %all_to_all.33.r.adj1, f32[16,13,8,128]{3,2,1,0:T(8,128)S(1)} %all_to_all.35.adj0, f32[2,96,16,128]{3,2,1,0:T(8,128)S(1)} %copy-done, f32[4,16,128]{2,1,0:T(8,128)S(1)} %collective-permute-done.3.from_prv.top, ...), custom_call_target="tpu_custom_call" | custom-call | flops 20000000 | bytes 6000000 | tf_op jit(solution)/shard_map/force/pallas_call | solution.py:324
  166.8 1.2 force_edge.1
  (47 shorter events, 1.4 us)
Async XLA Ops:
  1.5 10.6 %collective-permute-start = (f32[2,96,128]{2,1,0:T(8,128)S(1)}, f32[2,96,128]{2,1,0:T(8,128)S(1)}, u32[]{:S(2)}, u32[]{:S(2)}) collective-permute-start(f32[2,96,128]{2,1,0:T(8,128)S(1)} %bitcast.39), channel_id=1, source_target_pairs={{0,1},{1,2},{2,3},{3,4},{4,5},{5,6},{6,7},{7,8},{8,9},{9,10},{10,1... | collective-permute-start | bytes 294920 | tf_op jit(solution)/shard_map/ppermute | solution.py:702
  3.3 12.2 %copy-start.3 = (s32[3,6,1]{1,2,0:T(1,128)S(1)}, s32[3,6,1]{1,2,0:T(1,128)}, u32[]{:S(2)}) copy-start(s32[3,6,1]{1,2,0:T(1,128)} %param.15) | copy-start | bytes 220
  3.3 12.3 %copy-start.4 = (s32[1,1,16,2]{2,3,1,0:T(2,128)S(1)}, s32[1,1,16,2]{2,3,1,0:T(2,128)}, u32[]{:S(2)}) copy-start(s32[1,1,16,2]{2,3,1,0:T(2,128)} %param.14) | copy-start | bytes 388
  3.3 12.5 %copy-start.5 = (s32[6,1]{0,1:T(1,128)S(1)}, s32[6,1]{0,1:T(1,128)}, u32[]{:S(2)}) copy-start(s32[6,1]{0,1:T(1,128)} %param.13) | copy-start | bytes 76
  3.3 8.9 %collective-permute-start.1 = (f32[2,96,128]{2,1,0:T(8,128)S(1)}, f32[2,96,128]{2,1,0:T(8,128)S(1)}, u32[]{:S(2)}, u32[]{:S(2)}) collective-permute-start(f32[2,96,128]{2,1,0:T(8,128)S(1)} %bitcast.38), channel_id=1, source_target_pairs={{1,0},{2,1},{3,2},{4,3},{5,4},{6,5},{7,6},{8,7},{9,8},{10,9},{11,1... | collective-permute-start | bytes 294920 | tf_op jit(solution)/shard_map/ppermute | solution.py:706
  12.2 4.8 %collective-permute-start.3 = (f32[4,16,128]{2,1,0:T(8,128)S(1)}, f32[4,16,128]{2,1,0:T(8,128)S(1)}, u32[]{:S(2)}, u32[]{:S(2)}) collective-permute-start(f32[4,16,128]{2,1,0:T(8,128)S(1)} %get-tuple-element.53.my_nxt), channel_id=1, source_target_pairs={{0,16},{16,32},{32,48},{48,64},{64,80},{80,96},{96,112},{112,0},{1... | collective-permute-start | bytes 98312 | tf_op jit(solution)/shard_map/ppermute | solution.py:702
  12.2 4.9 %collective-permute-start.2 = (f32[5,16,128]{2,1,0:T(8,128)S(1)}, f32[5,16,128]{2,1,0:T(8,128)S(1)}, u32[]{:S(2)}, u32[]{:S(2)}) collective-permute-start(f32[5,16,128]{2,1,0:T(8,128)S(1)} %get-tuple-element.52.my_prv), channel_id=1, source_target_pairs={{16,0},{32,16},{48,32},{64,48},{80,64},{96,80},{112,96},{0,112},{1... | collective-permute-start | bytes 122888 | tf_op jit(solution)/shard_map/ppermute | solution.py:706
  17.1 21.3 %copy-start.2 = (bf16[256,384]{1,0:T(8,128)(2,1)S(1)}, bf16[256,384]{1,0:T(8,128)(2,1)}, u32[]{:S(2)}) copy-start(bf16[256,384]{1,0:T(8,128)(2,1)} %constant.91.clone.shift) | copy-start | bytes 589828
  85.7 2.5 %collective-permute-start.5 = (f32[16,2,8,128]{3,2,1,0:T(8,128)S(1)}, f32[16,2,8,128]{3,2,1,0:T(8,128)S(1)}, u32[]{:S(2)}, u32[]{:S(2)}) collective-permute-start(f32[16,2,8,128]{3,2,1,0:T(8,128)S(1)} %get-tuple-element.61), channel_id=1, source_target_pairs={{16,0},{32,16},{48,32},{64,48},{80,64},{96,80},{112,96},{0,112},{1... | collective-permute-start | bytes 393224 | tf_op jit(solution)/shard_map/ppermute | solution.py:706
  85.8 5.6 %copy-start.1 = (bf16[384,256]{1,0:T(8,128)(2,1)S(1)}, bf16[384,256]{1,0:T(8,128)(2,1)}, u32[]{:S(2)}) copy-start(bf16[384,256]{1,0:T(8,128)(2,1)} %constant.92.clone.shift_t) | copy-start | bytes 589828
  85.8 5.6 %collective-permute-start.4 = (f32[16,2,8,128]{3,2,1,0:T(8,128)S(1)}, f32[16,2,8,128]{3,2,1,0:T(8,128)S(1)}, u32[]{:S(2)}, u32[]{:S(2)}) collective-permute-start(f32[16,2,8,128]{3,2,1,0:T(8,128)S(1)} %get-tuple-element.62), channel_id=1, source_target_pairs={{0,16},{16,32},{32,48},{48,64},{64,80},{80,96},{96,112},{112,0},{1... | collective-permute-start | bytes 393224 | tf_op jit(solution)/shard_map/ppermute | solution.py:702
  102.1 1.9 %collective-permute-start.6 = (f32[16,8,128]{2,1,0:T(8,128)S(1)}, f32[16,8,128]{2,1,0:T(8,128)S(1)}, u32[]{:S(2)}, u32[]{:S(2)}) collective-permute-start(f32[16,8,128]{2,1,0:T(8,128)S(1)} %get-tuple-element.59), channel_id=1, source_target_pairs={{16,0},{32,16},{48,32},{64,48},{80,64},{96,80},{112,96},{0,112},{1... | collective-permute-start | bytes 196616 | tf_op jit(solution)/shard_map/ppermute | solution.py:706
  102.1 4.9 %collective-permute-start.7 = (f32[16,8,128]{2,1,0:T(8,128)S(1)}, f32[16,8,128]{2,1,0:T(8,128)S(1)}, u32[]{:S(2)}, u32[]{:S(2)}) collective-permute-start(f32[16,8,128]{2,1,0:T(8,128)S(1)} %get-tuple-element.60), channel_id=1, source_target_pairs={{0,16},{16,32},{32,48},{48,64},{64,80},{80,96},{96,112},{112,0},{1... | collective-permute-start | bytes 196616 | tf_op jit(solution)/shard_map/ppermute | solution.py:702
  140.1 22.1 %copy-start = (f32[2,96,16,128]{3,2,1,0:T(8,128)S(1)}, f32[2,96,16,128]{3,2,1,0:T(8,128)}, u32[]{:S(2)}) copy-start(f32[2,96,16,128]{3,2,1,0:T(8,128)} %st.3) | copy-start | bytes 4718596
  159.2 7.6 %collective-permute-start.9 = (f32[16,8,128]{2,1,0:T(8,128)S(1)}, f32[16,8,128]{2,1,0:T(8,128)S(1)}, u32[]{:S(2)}, u32[]{:S(2)}) collective-permute-start(f32[16,8,128]{2,1,0:T(8,128)S(1)} %slice_bitcast_fusion.2), channel_id=1, source_target_pairs={{0,16},{16,32},{32,48},{48,64},{64,80},{80,96},{96,112},{112,0},{1... | collective-permute-start | bytes 196616 | tf_op jit(solution)/shard_map/ppermute | solution.py:702
  159.2 7.6 %collective-permute-start.8 = (f32[16,8,128]{2,1,0:T(8,128)S(1)}, f32[16,8,128]{2,1,0:T(8,128)S(1)}, u32[]{:S(2)}, u32[]{:S(2)}) collective-permute-start(f32[16,8,128]{2,1,0:T(8,128)S(1)} %slice_bitcast_fusion.2), channel_id=1, source_target_pairs={{16,0},{32,16},{48,32},{64,48},{80,64},{96,80},{112,96},{0,112},{1... | collective-permute-start | bytes 196616 | tf_op jit(solution)/shard_map/ppermute | solution.py:706

commit v4 on v3

--- a/solution.py
+++ b/solution.py
@@ -523,7 +523,9 @@
         acc[:, pl.ds(e * PEERS, PEERS)] = jnp.zeros((4, PEERS, 8, 128), F32)
 
 
-def push_kernel(tab, shift_t, v, out, acc, wv, lhs, *bufs):
+def push_kernel(tab, shift_t, v, st_hbm, out, st, acc, wv, lhs, buf_a, buf_b, sem):
+    copy = pltpu.make_async_copy(st_hbm, st, sem)
+    copy.start()
     fill_weights(wv, WEIGHTS)
     clear(acc)
 
@@ -537,7 +539,7 @@
         base, _, wc = brick_plan(tab, wv, d * BRICKS + k)
         brick_add(acc, base, wc, [buf[k, i] for i in range(4)])
 
-    each_peer(first, second, bufs)
+    each_peer(first, second, (buf_a, buf_b))
 
     def put(e, block):
         if e == 0:
@@ -548,32 +550,43 @@
             out[:, e - 1] = block
 
     shift_taps_adjoint(lhs, shift_t, acc, put)
-
-
-def push(tab, shift_t, v):
+    copy.wait()
+
+
+def push(tab, shift_t, v, states):
     return pl.pallas_call(
         push_kernel,
-        in_specs=[SMEM, VMEM, VMEM],
-        out_specs=VMEM,
-        out_shape=turned_shape(RB + 1),
-        scratch_shapes=[TAPS, WV, LHS, BUF, BUF],
+        in_specs=[SMEM, VMEM, VMEM, pl.BlockSpec(memory_space=pltpu.HBM)],
+        out_specs=[VMEM, VMEM],
+        out_shape=[turned_shape(RB + 1), jax.ShapeDtypeStruct(states.shape, F32)],
+        scratch_shapes=[TAPS, WV, LHS, BUF, BUF, pltpu.SemaphoreType.DMA],
         compiler_params=params(24),
         name="push",
-    )(tab, shift_t, v)
+    )(tab, shift_t, v, in_hbm(states))
 
 
 def normal_kernel(tab, shift, shift_t, x, prv, nxt, out, lo, hi, taps, acc, wv, kv, lhs, *bufs):
     fill_weights(wv, WEIGHTS)
     fill_weights(kv, PAIRS)
     clear(acc)
+    sub3 = lax.broadcasted_iota(jnp.int32, (PEERS, 8, 128), 1) < 3
+    last = 8 * RB + 6 * (RB - 1) - 2
+
+    def block(e):
+        if e == 0:
+            return prv[:, 0:8], pltpu.roll(prv[:, 8:16], 6, 1)
+        if e == RB + 1:
+            return nxt[:, 0:8], nxt[:, 8:16]
+        if e == RB:
+            return x[:, 8 * RB - 8 : 8 * RB], pltpu.roll(x[:, last : last + 8], 6, 1)
+        return x[:, 8 * e - 8 : 8 * e], x[:, 8 * RB + 6 * (e - 1) : 8 * RB + 6 * (e - 1) + 8]
+
     for q in range(2):
-        load_taps(lhs, taps.at[q], 0, prv[:, q])
-        load_taps(lhs, taps.at[q], RB + 1, nxt[:, q])
-
-        @pl.loop(0, RB)
-        def _(rb):
-            load_taps(lhs, taps.at[q], rb + 1, x[:, q, rb])
-
+        for e in range(RB + 2):
+            own, rim = block(e)
+            own = pltpu.roll(own, 3, 1)
+            tile = jnp.where(sub3, rim, own) if q == 0 else jnp.where(sub3, own, rim)
+            load_taps(lhs, taps.at[q], e, tile)
         shift_taps(lhs, shift, taps.at[q], RB + 2)
 
     def first(d, k, buf):
@@ -584,7 +597,7 @@
         f = tab[3, d * BRICKS + k]
         kw = [kv[f, t] for t in range(4)]
         for i in range(4):
-            at = [pltpu.roll(jnp.where(sub >= a, c0[i], c1[i]), 8 - a, 0) for a in range(1, 8)]
+            at = [c0[i]] + [pltpu.roll(jnp.where(sub >= a, c0[i], c1[i]), 8 - a, 0) for a in range(1, 7)]
             near = kw[0] * at[3] + kw[1] * (at[2] + at[4])
             buf[k, i] = near + (kw[2] * (at[1] + at[5]) + kw[3] * (at[0] + at[6]))
 
@@ -657,15 +670,22 @@
     return y[:, :128], y[:, 128:]
 
 
+PACKED = 8 * RB + 6 * RB
+
+
 def depth_kernel(code, r, a, out):
-    @pl.loop(0, BRICKS)
-    def _(k):
+    sub = lax.broadcasted_iota(jnp.int32, (PEERS, 8, 128), 1)
+    for k in range(BRICKS):
         ys = depth_product(code[k], False, r, k)
         for h in range(2):
-            u = ys[h] + a[:, 2 * k + h].reshape(128, 128)
-            tiles = pltpu.roll(u, 4, 0).reshape(PEERS, 8, 128)
-            out[:, 0, 2 * k + h] = tiles
-            out[:, 1, 2 * k + h] = jnp.concatenate([tiles[1:], tiles[:1]], axis=0)
+            rb = 2 * k + h
+            tiles = ys[h].reshape(PEERS, 8, 128) + a[:, rb]
+            out[:, 8 * rb : 8 * rb + 8] = tiles
+            moved = pltpu.roll(tiles, 3, 1)
+            before = jnp.concatenate([moved[-1:], moved[:-1]], axis=0)
+            after = jnp.concatenate([moved[1:], moved[:1]], axis=0)
+            rim = jnp.where(sub < 3, before, after)
+            out[:, 8 * RB + 6 * rb : 8 * RB + 6 * rb + 6] = rim[:, :6]
 
 
 def depth(code, r, a):
@@ -673,15 +693,14 @@
         depth_kernel,
         in_specs=[SMEM, VMEM, VMEM],
         out_specs=VMEM,
-        out_shape=jax.ShapeDtypeStruct((PEERS, 2, RB, 8, 128), F32),
+        out_shape=jax.ShapeDtypeStruct((PEERS, PACKED, 128), F32),
         compiler_params=params(24),
         name="depth",
     )(code, r, a)
 
 
 def depth_adjoint_kernel(code, r, out):
-    @pl.loop(0, BRICKS)
-    def _(k):
+    for k in range(BRICKS):
         ys = depth_product(code[k], True, r, k)
         for h in range(2):
             out[:, 2 * k + h] = ys[h].reshape(PEERS, 8, 128)
@@ -743,11 +762,14 @@
     tab = brick_table(x[:, RB, 0, 32:88])
     r = swap(pull(tab, shift, x))
     u = swap(depth(code, r, a1))
-    y, lo, hi = normal(tab, shift, shift_t, u, to_next(u[:, :, RB - 1], "gx", gx), to_prev(u[:, :, 0], "gx", gx))
+    low = jnp.concatenate([u[:, 8 * RB - 8 : 8 * RB], u[:, PACKED - 8 :]], axis=1)
+    high = jnp.concatenate([u[:, :8], u[:, 8 * RB : 8 * RB + 8]], axis=1)
+    y, lo, hi = normal(tab, shift, shift_t, u, to_next(low, "gx", gx), to_prev(high, "gx", gx))
     y = y.at[:, RB - 1].add(to_prev(lo, "gx", gx)).at[:, 0].add(to_next(hi, "gx", gx))
     adj1 = swap(y)
     v = swap(depth_adjoint(code, adj1))
-    adj0 = swap(push(tab, shift_t, v))
+    y, states = push(tab, shift_t, v, states)
+    adj0 = swap(y)
     return force(adj1, adj0, states, (from_prv, from_nxt, left, right))
 
 

time: 171 us -> 169 us (0.988)
  starting transfers between devices: 12.7 us -> 19.9 us
  blocking collectives: 108 us -> 104 us
  waiting for transfers between devices: 9.41 us -> 7.57 us
    ppermute x5, starting transfers between devices: 9.94 us -> 18.1 us  [to_prev(): return lax.ppermute(x, axis, [((i + 1) % count, i) for i in range(count)])]
    all_to_all x6, blocking collectives: 108 us -> 104 us  [swap(): return lax.all_to_all(x, 'gy', split_axis=0, concat_axis=0, tiled=True)]
  transfers between devices with their start and end apart: 10 -> 10, of which waited for: 5 -> 4; matrix products, arithmetic and copies ran while one was open for 0% -> 0% of each run, Pallas kernels for 7% -> 7%
where the time goes in v4:
time: 169 us; the launch traced here: 168 us
  blocking collectives  104 us (62%)
  Pallas kernels  32.7 us (19%)
  starting transfers between devices  19.9 us (12%)
  waiting for transfers between devices  7.57 us (4%)
  local copies, waits for them, and re-layouts  2.73 us (2%)
    all_to_all x6, blocking collectives, swap(): return lax.all_to_all(x, 'gy', split_axis=0, concat_axis=0, tiled=True)  104 us
    ppermute x5, starting transfers between devices, to_prev(): return lax.ppermute(x, axis, [((i + 1) % count, i) for i in range(count)])  18.1 us
    pallas_call x1, Pallas kernels, normal(): pl.pallas_call(normal_kernel, in_specs=[SMEM, VMEM, VMEM, VMEM, VMEM, VME...  10.3 us
    ppermute x5, waiting for transfers between devices, to_next(): return lax.ppermute(x, axis, [(i, (i + 1) % count) for i in range(count)])  5.6 us
    pallas_call x1, Pallas kernels, pre(): pl.pallas_call(pre_kernel, in_specs=[hbm, hbm], out_specs=[VMEM] * 5, out...  5.11 us
    pallas_call x1, Pallas kernels, force(): pl.pallas_call(force_kernel, grid=(RB - 2,), in_specs=[turned(inner), tur...  4.67 us
    pallas_call x1, Pallas kernels, push(): pl.pallas_call(push_kernel, in_specs=[SMEM, VMEM, VMEM, pl.BlockSpec(memo...  4.08 us
    pallas_call x1, Pallas kernels, pull(): pl.pallas_call(pull_kernel, in_specs=[SMEM, VMEM, VMEM], out_specs=VMEM,...  3.62 us
  transfers between devices with their start and end apart: 10, of which 4 were waited for; matrix products, arithmetic and copies ran while one was open for 0% of the time, Pallas kernels for 7%

profile of v4, /device:TPU:0, one launch (start us, length us, event | category | flops | bytes accessed | tf_op | source)
XLA Modules:
  0.0 167.6 jit_solution(17801657257074099041)
XLA Ops:
  0.0 1.5 fusion.6
  1.5 1.8 %collective-permute-start = (f32[2,96,128]{2,1,0:T(8,128)S(1)}, f32[2,96,128]{2,1,0:T(8,128)S(1)}, u32[]{:S(2)}, u32[]{:S(2)}) collective-permute-start(f32[2,96,128]{2,1,0:T(8,128)S(1)} %bitcast.31), channel_id=1, source_target_pairs={{0,1},{1,2},{2,3},{3,4},{4,5},{5,6},{6,7},{7,8},{8,9},{9,10},{10,1... | collective-permute-start | bytes 294920 | tf_op jit(solution)/shard_map/ppermute | solution.py:721
  3.3 3.7 %collective-permute-start.1 = (f32[2,96,128]{2,1,0:T(8,128)S(1)}, f32[2,96,128]{2,1,0:T(8,128)S(1)}, u32[]{:S(2)}, u32[]{:S(2)}) collective-permute-start(f32[2,96,128]{2,1,0:T(8,128)S(1)} %bitcast.30), channel_id=1, source_target_pairs={{1,0},{2,1},{3,2},{4,3},{5,4},{6,5},{7,6},{8,7},{9,8},{10,9},{11,1... | collective-permute-start | bytes 294920 | tf_op jit(solution)/shard_map/ppermute | solution.py:725
  7.0 5.1 %pre.1 = (f32[16,13,8,128]{3,2,1,0:T(8,128)S(1)}, f32[16,12,8,128]{3,2,1,0:T(8,128)S(1)}, f32[2,96,128]{2,1,0:T(8,128)S(1)}, f32[5,16,128]{2,1,0:T(8,128)S(1)}, f32[4,16,128]{2,1,0:T(8,128)S(1)}) custom-call(f32[3,96,16,128]{3,2,1,0:T(8,128)} %v_hbm.1, f32[2,96,16,128]{3,2,1,0:T(8,128)} %st_hbm.3), custom_call_target="tpu_custom_call" | custom-call | flops 20000000 | bytes 6000000 | tf_op jit(solution)/shard_map/pre/pallas_call | solution.py:136
  12.2 3.2 %collective-permute-start.2 = (f32[5,16,128]{2,1,0:T(8,128)S(1)}, f32[5,16,128]{2,1,0:T(8,128)S(1)}, u32[]{:S(2)}, u32[]{:S(2)}) collective-permute-start(f32[5,16,128]{2,1,0:T(8,128)S(1)} %get-tuple-element.54.my_prv), channel_id=1, source_target_pairs={{16,0},{32,16},{48,32},{64,48},{80,64},{96,80},{112,96},{0,112},{1... | collective-permute-start | bytes 122888 | tf_op jit(solution)/shard_map/ppermute | solution.py:725
  15.6 0.1 concatenate.27
  15.7 0.1 concatenate.30
  15.8 1.2 columns.1
  17.1 0.5 close.1
  17.6 19.5 %all_to_all.30.x = f32[16,13,8,128]{3,2,1,0:T(8,128)S(1)} all-to-all(f32[16,13,8,128]{3,2,1,0:T(8,128)S(1)} %get-tuple-element.57), channel_id=1, replica_groups=mesh['gx'=8,'gy'=16] {'gy'}, dimensions={0} | all-to-all | bytes 1703936 | tf_op jit(solution)/shard_map/all_to_all | solution.py:729
  37.5 0.3 select_reduce_fusion
  37.9 0.1 fusion.3
  38.2 0.1 stack.17
  38.3 0.1 stack.16
  38.4 3.6 %pull.1 = f32[16,12,8,128]{3,2,1,0:T(8,128)S(1)} custom-call(s32[4,96]{1,0:T(4,128)S(1)} %pad_add_fusion.tab, bf16[256,384]{1,0:T(8,128)(2,1)S(1)} %copy-done.1, f32[16,13,8,128]{3,2,1,0:T(8,128)S(1)} %all_to_all.30.x), custom_call_target="tpu_custom_call" | custom-call | tf_op jit(solution)/shard_map/pull/pallas_call | solution.py:509
  42.0 17.4 %all_to_all.31.r = f32[16,12,8,128]{3,2,1,0:T(8,128)S(1)} all-to-all(f32[16,12,8,128]{3,2,1,0:T(8,128)S(1)} %pull.1), channel_id=1, replica_groups=mesh['gx'=8,'gy'=16] {'gy'}, dimensions={0} | all-to-all | bytes 1572864 | tf_op jit(solution)/shard_map/all_to_all | solution.py:729
  59.4 1.0 depth.1
  60.4 22.6 %all_to_all.32.x = f32[16,168,128]{2,1,0:T(8,128)S(1)} all-to-all(f32[16,168,128]{2,1,0:T(8,128)S(1)} %depth.1), channel_id=1, replica_groups=mesh['gx'=8,'gy'=16] {'gy'}, dimensions={0} | all-to-all | bytes 2752512 | tf_op jit(solution)/shard_map/all_to_all | solution.py:729
  83.0 2.9 %collective-permute-start.5 = (f32[16,16,128]{2,1,0:T(8,128)S(1)}, f32[16,16,128]{2,1,0:T(8,128)S(1)}, u32[]{:S(2)}, u32[]{:S(2)}) collective-permute-start(f32[16,16,128]{2,1,0:T(8,128)S(1)} %pad_maximum_fusion.1), channel_id=1, source_target_pairs={{16,0},{32,16},{48,32},{64,48},{80,64},{96,80},{112,96},{0,112},{1... | collective-permute-start | bytes 393224 | tf_op jit(solution)/shard_map/ppermute | solution.py:725
  86.0 2.6 %collective-permute-done.4.prv = f32[16,16,128]{2,1,0:T(8,128)S(1)} collective-permute-done((f32[16,16,128]{2,1,0:T(8,128)S(1)}, f32[16,16,128]{2,1,0:T(8,128)S(1)}, u32[]{:S(2)}, u32[]{:S(2)}) %collective-permute-start.4) | collective-permute-done | bytes 131104 | tf_op jit(solution)/shard_map/ppermute | solution.py:721
  88.6 10.3 %normal.1 = (f32[16,12,8,128]{3,2,1,0:T(8,128)S(1)}, f32[16,8,128]{2,1,0:T(8,128)S(1)}, f32[16,8,128]{2,1,0:T(8,128)S(1)}) custom-call(s32[4,96]{1,0:T(4,128)S(1)} %pad_add_fusion.tab, bf16[256,384]{1,0:T(8,128)(2,1)S(1)} %copy-done.1, bf16[384,256]{1,0:T(8,128)(2,1)S(1)} %copy-done, f32[16,168,128]{2,1,0:T(8,128)S(1)} %all_to_all.32.x, ...), custom_call_target="tpu_custom_call" | custom-call | tf_op jit(solution)/shard_map/normal/pallas_call | solution.py:626
  98.9 3.0 %collective-permute-start.6 = (f32[16,8,128]{2,1,0:T(8,128)S(1)}, f32[16,8,128]{2,1,0:T(8,128)S(1)}, u32[]{:S(2)}, u32[]{:S(2)}) collective-permute-start(f32[16,8,128]{2,1,0:T(8,128)S(1)} %get-tuple-element.61), channel_id=1, source_target_pairs={{16,0},{32,16},{48,32},{64,48},{80,64},{96,80},{112,96},{0,112},{1... | collective-permute-start | bytes 196616 | tf_op jit(solution)/shard_map/ppermute | solution.py:725
  101.9 1.9 %collective-permute-done.6 = f32[16,8,128]{2,1,0:T(8,128)S(1)} collective-permute-done((f32[16,8,128]{2,1,0:T(8,128)S(1)}, f32[16,8,128]{2,1,0:T(8,128)S(1)}, u32[]{:S(2)}, u32[]{:S(2)}) %collective-permute-start.6) | collective-permute-done | bytes 65568 | tf_op jit(solution)/shard_map/ppermute | solution.py:725
  103.8 3.0 %collective-permute-done.7 = f32[16,8,128]{2,1,0:T(8,128)S(1)} collective-permute-done((f32[16,8,128]{2,1,0:T(8,128)S(1)}, f32[16,8,128]{2,1,0:T(8,128)S(1)}, u32[]{:S(2)}, u32[]{:S(2)}) %collective-permute-start.7) | collective-permute-done | bytes 65568 | tf_op jit(solution)/shard_map/ppermute | solution.py:721
  106.8 14.9 %all_to_all.33.r.adj1 = f32[16,12,8,128]{3,2,1,0:T(8,128)S(1)} all-to-all(f32[16,12,8,128]{3,2,1,0:T(8,128)S(1)} %fusion), channel_id=1, replica_groups=mesh['gx'=8,'gy'=16] {'gy'}, dimensions={0} | all-to-all | bytes 1572864 | tf_op jit(solution)/shard_map/all_to_all | solution.py:729
  121.7 1.0 depth_adjoint.1
  122.7 14.7 %all_to_all.34.v = f32[16,12,8,128]{3,2,1,0:T(8,128)S(1)} all-to-all(f32[16,12,8,128]{3,2,1,0:T(8,128)S(1)} %depth_adjoint.1), channel_id=1, replica_groups=mesh['gx'=8,'gy'=16] {'gy'}, dimensions={0} | all-to-all | bytes 1572864 | tf_op jit(solution)/shard_map/all_to_all | solution.py:729
  137.5 4.1 %push.1 = (f32[16,13,8,128]{3,2,1,0:T(8,128)S(1)}, f32[2,96,16,128]{3,2,1,0:T(8,128)S(1)}) custom-call(s32[4,96]{1,0:T(4,128)S(1)} %pad_add_fusion.tab, bf16[384,256]{1,0:T(8,128)(2,1)S(1)} %copy-done, f32[16,12,8,128]{3,2,1,0:T(8,128)S(1)} %all_to_all.34.v, f32[2,96,16,128]{3,2,1,0:T(8,128)} %st_hbm.3), custom_call_target="tpu_custom_call" | custom-call | tf_op jit(solution)/shard_map/push/pallas_call | solution.py:557
  141.6 15.1 %all_to_all.35.adj0 = f32[16,13,8,128]{3,2,1,0:T(8,128)S(1)} all-to-all(f32[16,13,8,128]{3,2,1,0:T(8,128)S(1)} %get-tuple-element.63), channel_id=1, replica_groups=mesh['gx'=8,'gy'=16] {'gy'}, dimensions={0} | all-to-all | bytes 1703936 | tf_op jit(solution)/shard_map/all_to_all | solution.py:729
  156.6 5.2 %collective-permute-start.8 = (f32[16,8,128]{2,1,0:T(8,128)S(1)}, f32[16,8,128]{2,1,0:T(8,128)S(1)}, u32[]{:S(2)}, u32[]{:S(2)}) collective-permute-start(f32[16,8,128]{2,1,0:T(8,128)S(1)} %slice_bitcast_fusion), channel_id=1, source_target_pairs={{16,0},{32,16},{48,32},{64,48},{80,64},{96,80},{112,96},{0,112},{1... | collective-permute-start | bytes 196616 | tf_op jit(solution)/shard_map/ppermute | solution.py:725
  161.8 4.7 %force.1.prior = f32[3,96,16,128]{3,2,1,0:T(8,128)} custom-call(f32[16,12,8,128]{3,2,1,0:T(8,128)S(1)} %all_to_all.33.r.adj1, f32[16,13,8,128]{3,2,1,0:T(8,128)S(1)} %all_to_all.35.adj0, f32[2,96,16,128]{3,2,1,0:T(8,128)S(1)} %get-tuple-element.64.st, f32[4,16,128]{2,1,0:T(8,128)S(1)} %collective-permute-done.3.from_prv.top, ...), custom_call_target="tpu_custom_call" | custom-call | flops 20000000 | bytes 6000000 | tf_op jit(solution)/shard_map/force/pallas_call | solution.py:324
  166.5 1.2 force_edge.1
  (45 shorter events, 1.2 us)
Async XLA Ops:
  1.5 10.6 %collective-permute-start = (f32[2,96,128]{2,1,0:T(8,128)S(1)}, f32[2,96,128]{2,1,0:T(8,128)S(1)}, u32[]{:S(2)}, u32[]{:S(2)}) collective-permute-start(f32[2,96,128]{2,1,0:T(8,128)S(1)} %bitcast.31), channel_id=1, source_target_pairs={{0,1},{1,2},{2,3},{3,4},{4,5},{5,6},{6,7},{7,8},{8,9},{9,10},{10,1... | collective-permute-start | bytes 294920 | tf_op jit(solution)/shard_map/ppermute | solution.py:721
  3.3 12.2 %copy-start.2 = (s32[3,6,1]{1,2,0:T(1,128)S(1)}, s32[3,6,1]{1,2,0:T(1,128)}, u32[]{:S(2)}) copy-start(s32[3,6,1]{1,2,0:T(1,128)} %param.15) | copy-start | bytes 220
  3.3 12.3 %copy-start.3 = (s32[1,1,16,2]{2,3,1,0:T(2,128)S(1)}, s32[1,1,16,2]{2,3,1,0:T(2,128)}, u32[]{:S(2)}) copy-start(s32[1,1,16,2]{2,3,1,0:T(2,128)} %param.14) | copy-start | bytes 388
  3.3 12.5 %copy-start.4 = (s32[6,1]{0,1:T(1,128)S(1)}, s32[6,1]{0,1:T(1,128)}, u32[]{:S(2)}) copy-start(s32[6,1]{0,1:T(1,128)} %param.13) | copy-start | bytes 76
  3.3 8.9 %collective-permute-start.1 = (f32[2,96,128]{2,1,0:T(8,128)S(1)}, f32[2,96,128]{2,1,0:T(8,128)S(1)}, u32[]{:S(2)}, u32[]{:S(2)}) collective-permute-start(f32[2,96,128]{2,1,0:T(8,128)S(1)} %bitcast.30), channel_id=1, source_target_pairs={{1,0},{2,1},{3,2},{4,3},{5,4},{6,5},{7,6},{8,7},{9,8},{10,9},{11,1... | collective-permute-start | bytes 294920 | tf_op jit(solution)/shard_map/ppermute | solution.py:725
  12.2 4.8 %collective-permute-start.3 = (f32[4,16,128]{2,1,0:T(8,128)S(1)}, f32[4,16,128]{2,1,0:T(8,128)S(1)}, u32[]{:S(2)}, u32[]{:S(2)}) collective-permute-start(f32[4,16,128]{2,1,0:T(8,128)S(1)} %get-tuple-element.55.my_nxt), channel_id=1, source_target_pairs={{0,16},{16,32},{32,48},{48,64},{64,80},{80,96},{96,112},{112,0},{1... | collective-permute-start | bytes 98312 | tf_op jit(solution)/shard_map/ppermute | solution.py:721
  12.2 4.9 %collective-permute-start.2 = (f32[5,16,128]{2,1,0:T(8,128)S(1)}, f32[5,16,128]{2,1,0:T(8,128)S(1)}, u32[]{:S(2)}, u32[]{:S(2)}) collective-permute-start(f32[5,16,128]{2,1,0:T(8,128)S(1)} %get-tuple-element.54.my_prv), channel_id=1, source_target_pairs={{16,0},{32,16},{48,32},{64,48},{80,64},{96,80},{112,96},{0,112},{1... | collective-permute-start | bytes 122888 | tf_op jit(solution)/shard_map/ppermute | solution.py:725
  17.1 21.3 %copy-start.1 = (bf16[256,384]{1,0:T(8,128)(2,1)S(1)}, bf16[256,384]{1,0:T(8,128)(2,1)}, u32[]{:S(2)}) copy-start(bf16[256,384]{1,0:T(8,128)(2,1)} %constant.91.clone.shift) | copy-start | bytes 589828
  60.4 28.2 %copy-start = (bf16[384,256]{1,0:T(8,128)(2,1)S(1)}, bf16[384,256]{1,0:T(8,128)(2,1)}, u32[]{:S(2)}) copy-start(bf16[384,256]{1,0:T(8,128)(2,1)} %constant.92.clone.shift_t) | copy-start | bytes 589828
  83.0 5.6 %collective-permute-start.4 = (f32[16,16,128]{2,1,0:T(8,128)S(1)}, f32[16,16,128]{2,1,0:T(8,128)S(1)}, u32[]{:S(2)}, u32[]{:S(2)}) collective-permute-start(f32[16,16,128]{2,1,0:T(8,128)S(1)} %pad_maximum_fusion), channel_id=1, source_target_pairs={{0,16},{16,32},{32,48},{48,64},{64,80},{80,96},{96,112},{112,0},{1... | collective-permute-start | bytes 393224 | tf_op jit(solution)/shard_map/ppermute | solution.py:721
  83.0 5.6 %collective-permute-start.5 = (f32[16,16,128]{2,1,0:T(8,128)S(1)}, f32[16,16,128]{2,1,0:T(8,128)S(1)}, u32[]{:S(2)}, u32[]{:S(2)}) collective-permute-start(f32[16,16,128]{2,1,0:T(8,128)S(1)} %pad_maximum_fusion.1), channel_id=1, source_target_pairs={{16,0},{32,16},{48,32},{64,48},{80,64},{96,80},{112,96},{0,112},{1... | collective-permute-start | bytes 393224 | tf_op jit(solution)/shard_map/ppermute | solution.py:725
  98.9 4.9 %collective-permute-start.6 = (f32[16,8,128]{2,1,0:T(8,128)S(1)}, f32[16,8,128]{2,1,0:T(8,128)S(1)}, u32[]{:S(2)}, u32[]{:S(2)}) collective-permute-start(f32[16,8,128]{2,1,0:T(8,128)S(1)} %get-tuple-element.61), channel_id=1, source_target_pairs={{16,0},{32,16},{48,32},{64,48},{80,64},{96,80},{112,96},{0,112},{1... | collective-permute-start | bytes 196616 | tf_op jit(solution)/shard_map/ppermute | solution.py:725
  101.9 4.9 %collective-permute-start.7 = (f32[16,8,128]{2,1,0:T(8,128)S(1)}, f32[16,8,128]{2,1,0:T(8,128)S(1)}, u32[]{:S(2)}, u32[]{:S(2)}) collective-permute-start(f32[16,8,128]{2,1,0:T(8,128)S(1)} %get-tuple-element.62), channel_id=1, source_target_pairs={{0,16},{16,32},{32,48},{48,64},{64,80},{80,96},{96,112},{112,0},{1... | collective-permute-start | bytes 196616 | tf_op jit(solution)/shard_map/ppermute | solution.py:721
  156.6 9.9 %collective-permute-start.9 = (f32[16,8,128]{2,1,0:T(8,128)S(1)}, f32[16,8,128]{2,1,0:T(8,128)S(1)}, u32[]{:S(2)}, u32[]{:S(2)}) collective-permute-start(f32[16,8,128]{2,1,0:T(8,128)S(1)} %slice_bitcast_fusion), channel_id=1, source_target_pairs={{0,16},{16,32},{32,48},{48,64},{64,80},{80,96},{96,112},{112,0},{1... | collective-permute-start | bytes 196616 | tf_op jit(solution)/shard_map/ppermute | solution.py:721
  156.6 9.9 %collective-permute-start.8 = (f32[16,8,128]{2,1,0:T(8,128)S(1)}, f32[16,8,128]{2,1,0:T(8,128)S(1)}, u32[]{:S(2)}, u32[]{:S(2)}) collective-permute-start(f32[16,8,128]{2,1,0:T(8,128)S(1)} %slice_bitcast_fusion), channel_id=1, source_target_pairs={{16,0},{32,16},{48,32},{64,48},{80,64},{96,80},{112,96},{0,112},{1... | collective-permute-start | bytes 196616 | tf_op jit(solution)/shard_map/ppermute | solution.py:725

commit v5 on v4

--- a/solution.py
+++ b/solution.py
@@ -58,9 +58,10 @@
 def gradients(st, top, bottom, left, right, rb, k):
     rows = pl.ds(rb * 8, 8)
     x = st[k, rows]
-    before = st[k, jnp.maximum(rb * 8 - 1, 0)]
+    fixed = isinstance(rb, int)
+    before = st[k, max(rb * 8 - 1, 0) if fixed else jnp.maximum(rb * 8 - 1, 0)]
     before = jnp.where(rb == 0, jnp.zeros_like(before) if top is None else top[2 + k], before)
-    after = st[k, jnp.minimum(rb * 8 + 8, 95)]
+    after = st[k, min(rb * 8 + 8, 95) if fixed else jnp.minimum(rb * 8 + 8, 95)]
     after = jnp.where(rb == RB - 1, jnp.zeros_like(after) if bottom is None else bottom[3 + k], after)
     up = jnp.concatenate([x[1:], after[None]], axis=0)
     down = jnp.concatenate([before[None], x[:-1]], axis=0)
@@ -295,8 +296,17 @@
         out[c] = b1 * g1[c] + b0 * g0[c]
 
 
-def force_kernel(adj1, adj0, st, top, bottom, left, right, out):
-    force_block(adj1[:, 0], adj0[:, 0], st, (top, bottom, left, right), pl.program_id(0) + 1, out)
+def force_kernel(adj1, adj0, st, top, bottom, left, right, out_hbm, buf, sems):
+    copies = []
+    for n in range((RB - 2) // 2):
+        for rb in (2 * n + 1, 2 * n + 2):
+            rows = buf.at[:, pl.ds(8 * rb, 8)]
+            force_block(adj1[:, rb], adj0[:, rb], st, (top, bottom, left, right), rb, rows)
+        part = pl.ds(16 * n + 8, 16)
+        copies.append(pltpu.make_async_copy(buf.at[:, part], out_hbm.at[:, part], sems.at[n]))
+        copies[-1].start()
+    for c in copies:
+        c.wait()
 
 
 def force_edge_kernel(adj1, adj0, st, top, bottom, left, right, from_nxt, from_prv, prior, out):
@@ -315,18 +325,15 @@
     from_prv = to_next(rim, "gx", lax.axis_size("gx"))
     args = (adj1, adj0, states, *edges)
 
-    def inner(i):
-        return i + 1
-
     def outer(i):
         return i * (RB - 1)
 
     main = pl.pallas_call(
         force_kernel,
-        grid=(RB - 2,),
-        in_specs=[turned(inner), turned(inner)] + fixed,
-        out_specs=natural3(inner),
+        in_specs=[VMEM] * 7,
+        out_specs=pl.BlockSpec(memory_space=pltpu.HBM),
         out_shape=shape,
+        scratch_shapes=[pltpu.VMEM((3, 96, 16, 128), F32), pltpu.SemaphoreType.DMA(((RB - 2) // 2,))],
         compiler_params=params(24),
         cost_estimate=COST,
         name="force",

time: 169 us -> 168 us (level)
  Pallas kernels: 32.7 us -> 30.2 us
    pallas_call x1, Pallas kernels: 4.67 us -> 2.15 us  [force(): pl.pallas_call(force_kernel, in_specs=[VMEM] * 7, out_specs=pl.BlockSpec(...]
  transfers between devices with their start and end apart: 10 -> 10, of which waited for: 4 -> 4; matrix products, arithmetic and copies ran while one was open for 0% -> 0% of each run, Pallas kernels for 7% -> 5%
where the time goes in v5:
time: 168 us; the launch traced here: 165 us
  blocking collectives  104 us (62%)
  Pallas kernels  30.2 us (18%)
  starting transfers between devices  19.8 us (12%)
  waiting for transfers between devices  7.57 us (5%)
  local copies, waits for them, and re-layouts  2.73 us (2%)
    all_to_all x6, blocking collectives, swap(): return lax.all_to_all(x, 'gy', split_axis=0, concat_axis=0, tiled=True)  104 us
    ppermute x5, starting transfers between devices, to_prev(): return lax.ppermute(x, axis, [((i + 1) % count, i) for i in range(count)])  18 us
    pallas_call x1, Pallas kernels, normal(): pl.pallas_call(normal_kernel, in_specs=[SMEM, VMEM, VMEM, VMEM, VMEM, VME...  10.3 us
    ppermute x5, waiting for transfers between devices, to_next(): return lax.ppermute(x, axis, [(i, (i + 1) % count) for i in range(count)])  5.6 us
    pallas_call x1, Pallas kernels, pre(): pl.pallas_call(pre_kernel, in_specs=[hbm, hbm], out_specs=[VMEM] * 5, out...  5.11 us
    pallas_call x1, Pallas kernels, push(): pl.pallas_call(push_kernel, in_specs=[SMEM, VMEM, VMEM, pl.BlockSpec(memo...  4.09 us
    pallas_call x1, Pallas kernels, pull(): pl.pallas_call(pull_kernel, in_specs=[SMEM, VMEM, VMEM], out_specs=VMEM,...  3.63 us
  transfers between devices with their start and end apart: 10, of which 4 were waited for; matrix products, arithmetic and copies ran while one was open for 0% of the time, Pallas kernels for 5%

profile of v5, /device:TPU:0, one launch (start us, length us, event | category | flops | bytes accessed | tf_op | source)
XLA Modules:
  0.0 165.1 jit_solution(17546064586490162168)
XLA Ops:
  0.0 1.5 fusion.6
  1.5 1.8 %collective-permute-start = (f32[2,96,128]{2,1,0:T(8,128)S(1)}, f32[2,96,128]{2,1,0:T(8,128)S(1)}, u32[]{:S(2)}, u32[]{:S(2)}) collective-permute-start(f32[2,96,128]{2,1,0:T(8,128)S(1)} %bitcast.31), channel_id=1, source_target_pairs={{0,1},{1,2},{2,3},{3,4},{4,5},{5,6},{6,7},{7,8},{8,9},{9,10},{10,1... | collective-permute-start | bytes 294920 | tf_op jit(solution)/shard_map/ppermute | solution.py:728
  3.3 3.7 %collective-permute-start.1 = (f32[2,96,128]{2,1,0:T(8,128)S(1)}, f32[2,96,128]{2,1,0:T(8,128)S(1)}, u32[]{:S(2)}, u32[]{:S(2)}) collective-permute-start(f32[2,96,128]{2,1,0:T(8,128)S(1)} %bitcast.30), channel_id=1, source_target_pairs={{1,0},{2,1},{3,2},{4,3},{5,4},{6,5},{7,6},{8,7},{9,8},{10,9},{11,1... | collective-permute-start | bytes 294920 | tf_op jit(solution)/shard_map/ppermute | solution.py:732
  7.0 5.1 %pre.1 = (f32[16,13,8,128]{3,2,1,0:T(8,128)S(1)}, f32[16,12,8,128]{3,2,1,0:T(8,128)S(1)}, f32[2,96,128]{2,1,0:T(8,128)S(1)}, f32[5,16,128]{2,1,0:T(8,128)S(1)}, f32[4,16,128]{2,1,0:T(8,128)S(1)}) custom-call(f32[3,96,16,128]{3,2,1,0:T(8,128)} %v_hbm.1, f32[2,96,16,128]{3,2,1,0:T(8,128)} %st_hbm.3), custom_call_target="tpu_custom_call" | custom-call | flops 20000000 | bytes 6000000 | tf_op jit(solution)/shard_map/pre/pallas_call | solution.py:137
  12.2 3.2 %collective-permute-start.2 = (f32[5,16,128]{2,1,0:T(8,128)S(1)}, f32[5,16,128]{2,1,0:T(8,128)S(1)}, u32[]{:S(2)}, u32[]{:S(2)}) collective-permute-start(f32[5,16,128]{2,1,0:T(8,128)S(1)} %get-tuple-element.54.my_prv), channel_id=1, source_target_pairs={{16,0},{32,16},{48,32},{64,48},{80,64},{96,80},{112,96},{0,112},{1... | collective-permute-start | bytes 122888 | tf_op jit(solution)/shard_map/ppermute | solution.py:732
  15.6 0.1 concatenate.27
  15.7 0.1 concatenate.30
  15.8 1.2 columns.1
  17.1 0.5 close.1
  17.6 19.5 %all_to_all.30.x = f32[16,13,8,128]{3,2,1,0:T(8,128)S(1)} all-to-all(f32[16,13,8,128]{3,2,1,0:T(8,128)S(1)} %get-tuple-element.57), channel_id=1, replica_groups=mesh['gx'=8,'gy'=16] {'gy'}, dimensions={0} | all-to-all | bytes 1703936 | tf_op jit(solution)/shard_map/all_to_all | solution.py:736
  37.5 0.3 select_reduce_fusion
  37.9 0.1 fusion.3
  38.2 0.1 stack.17
  38.3 0.1 stack.16
  38.4 3.6 %pull.1 = f32[16,12,8,128]{3,2,1,0:T(8,128)S(1)} custom-call(s32[4,96]{1,0:T(4,128)S(1)} %pad_add_fusion.tab, bf16[256,384]{1,0:T(8,128)(2,1)S(1)} %copy-done.1, f32[16,13,8,128]{3,2,1,0:T(8,128)S(1)} %all_to_all.30.x), custom_call_target="tpu_custom_call" | custom-call | tf_op jit(solution)/shard_map/pull/pallas_call | solution.py:516
  42.0 17.4 %all_to_all.31.r = f32[16,12,8,128]{3,2,1,0:T(8,128)S(1)} all-to-all(f32[16,12,8,128]{3,2,1,0:T(8,128)S(1)} %pull.1), channel_id=1, replica_groups=mesh['gx'=8,'gy'=16] {'gy'}, dimensions={0} | all-to-all | bytes 1572864 | tf_op jit(solution)/shard_map/all_to_all | solution.py:736
  59.4 1.0 depth.1
  60.4 22.5 %all_to_all.32.x = f32[16,168,128]{2,1,0:T(8,128)S(1)} all-to-all(f32[16,168,128]{2,1,0:T(8,128)S(1)} %depth.1), channel_id=1, replica_groups=mesh['gx'=8,'gy'=16] {'gy'}, dimensions={0} | all-to-all | bytes 2752512 | tf_op jit(solution)/shard_map/all_to_all | solution.py:736
  83.0 2.9 %collective-permute-start.5 = (f32[16,16,128]{2,1,0:T(8,128)S(1)}, f32[16,16,128]{2,1,0:T(8,128)S(1)}, u32[]{:S(2)}, u32[]{:S(2)}) collective-permute-start(f32[16,16,128]{2,1,0:T(8,128)S(1)} %pad_maximum_fusion.1), channel_id=1, source_target_pairs={{16,0},{32,16},{48,32},{64,48},{80,64},{96,80},{112,96},{0,112},{1... | collective-permute-start | bytes 393224 | tf_op jit(solution)/shard_map/ppermute | solution.py:732
  86.0 2.6 %collective-permute-done.4.prv = f32[16,16,128]{2,1,0:T(8,128)S(1)} collective-permute-done((f32[16,16,128]{2,1,0:T(8,128)S(1)}, f32[16,16,128]{2,1,0:T(8,128)S(1)}, u32[]{:S(2)}, u32[]{:S(2)}) %collective-permute-start.4) | collective-permute-done | bytes 131104 | tf_op jit(solution)/shard_map/ppermute | solution.py:728
  88.6 10.3 %normal.1 = (f32[16,12,8,128]{3,2,1,0:T(8,128)S(1)}, f32[16,8,128]{2,1,0:T(8,128)S(1)}, f32[16,8,128]{2,1,0:T(8,128)S(1)}) custom-call(s32[4,96]{1,0:T(4,128)S(1)} %pad_add_fusion.tab, bf16[256,384]{1,0:T(8,128)(2,1)S(1)} %copy-done.1, bf16[384,256]{1,0:T(8,128)(2,1)S(1)} %copy-done, f32[16,168,128]{2,1,0:T(8,128)S(1)} %all_to_all.32.x, ...), custom_call_target="tpu_custom_call" | custom-call | tf_op jit(solution)/shard_map/normal/pallas_call | solution.py:633
  98.9 3.0 %collective-permute-start.6 = (f32[16,8,128]{2,1,0:T(8,128)S(1)}, f32[16,8,128]{2,1,0:T(8,128)S(1)}, u32[]{:S(2)}, u32[]{:S(2)}) collective-permute-start(f32[16,8,128]{2,1,0:T(8,128)S(1)} %get-tuple-element.61), channel_id=1, source_target_pairs={{16,0},{32,16},{48,32},{64,48},{80,64},{96,80},{112,96},{0,112},{1... | collective-permute-start | bytes 196616 | tf_op jit(solution)/shard_map/ppermute | solution.py:732
  101.9 1.9 %collective-permute-done.6 = f32[16,8,128]{2,1,0:T(8,128)S(1)} collective-permute-done((f32[16,8,128]{2,1,0:T(8,128)S(1)}, f32[16,8,128]{2,1,0:T(8,128)S(1)}, u32[]{:S(2)}, u32[]{:S(2)}) %collective-permute-start.6) | collective-permute-done | bytes 65568 | tf_op jit(solution)/shard_map/ppermute | solution.py:732
  103.9 3.0 %collective-permute-done.7 = f32[16,8,128]{2,1,0:T(8,128)S(1)} collective-permute-done((f32[16,8,128]{2,1,0:T(8,128)S(1)}, f32[16,8,128]{2,1,0:T(8,128)S(1)}, u32[]{:S(2)}, u32[]{:S(2)}) %collective-permute-start.7) | collective-permute-done | bytes 65568 | tf_op jit(solution)/shard_map/ppermute | solution.py:728
  106.9 14.9 %all_to_all.33.r.adj1 = f32[16,12,8,128]{3,2,1,0:T(8,128)S(1)} all-to-all(f32[16,12,8,128]{3,2,1,0:T(8,128)S(1)} %fusion), channel_id=1, replica_groups=mesh['gx'=8,'gy'=16] {'gy'}, dimensions={0} | all-to-all | bytes 1572864 | tf_op jit(solution)/shard_map/all_to_all | solution.py:736
  121.7 1.0 depth_adjoint.1
  122.7 14.8 %all_to_all.34.v = f32[16,12,8,128]{3,2,1,0:T(8,128)S(1)} all-to-all(f32[16,12,8,128]{3,2,1,0:T(8,128)S(1)} %depth_adjoint.1), channel_id=1, replica_groups=mesh['gx'=8,'gy'=16] {'gy'}, dimensions={0} | all-to-all | bytes 1572864 | tf_op jit(solution)/shard_map/all_to_all | solution.py:736
  137.5 4.1 %push.1 = (f32[16,13,8,128]{3,2,1,0:T(8,128)S(1)}, f32[2,96,16,128]{3,2,1,0:T(8,128)S(1)}) custom-call(s32[4,96]{1,0:T(4,128)S(1)} %pad_add_fusion.tab, bf16[384,256]{1,0:T(8,128)(2,1)S(1)} %copy-done, f32[16,12,8,128]{3,2,1,0:T(8,128)S(1)} %all_to_all.34.v, f32[2,96,16,128]{3,2,1,0:T(8,128)} %st_hbm.3), custom_call_target="tpu_custom_call" | custom-call | tf_op jit(solution)/shard_map/push/pallas_call | solution.py:564
  141.6 15.1 %all_to_all.35.adj0 = f32[16,13,8,128]{3,2,1,0:T(8,128)S(1)} all-to-all(f32[16,13,8,128]{3,2,1,0:T(8,128)S(1)} %get-tuple-element.63), channel_id=1, replica_groups=mesh['gx'=8,'gy'=16] {'gy'}, dimensions={0} | all-to-all | bytes 1703936 | tf_op jit(solution)/shard_map/all_to_all | solution.py:736
  156.7 5.1 %collective-permute-start.8 = (f32[16,8,128]{2,1,0:T(8,128)S(1)}, f32[16,8,128]{2,1,0:T(8,128)S(1)}, u32[]{:S(2)}, u32[]{:S(2)}) collective-permute-start(f32[16,8,128]{2,1,0:T(8,128)S(1)} %slice_bitcast_fusion), channel_id=1, source_target_pairs={{16,0},{32,16},{48,32},{64,48},{80,64},{96,80},{112,96},{0,112},{1... | collective-permute-start | bytes 196616 | tf_op jit(solution)/shard_map/ppermute | solution.py:732
  161.8 2.1 %force.1.prior = f32[3,96,16,128]{3,2,1,0:T(8,128)} custom-call(f32[16,12,8,128]{3,2,1,0:T(8,128)S(1)} %all_to_all.33.r.adj1, f32[16,13,8,128]{3,2,1,0:T(8,128)S(1)} %all_to_all.35.adj0, f32[2,96,16,128]{3,2,1,0:T(8,128)S(1)} %get-tuple-element.64.st, f32[4,16,128]{2,1,0:T(8,128)S(1)} %collective-permute-done.3.from_prv.top, ...), custom_call_target="tpu_custom_call" | custom-call | flops 20000000 | bytes 6000000 | tf_op jit(solution)/shard_map/force/pallas_call | solution.py:331
  163.9 1.2 force_edge.1
  (45 shorter events, 1.2 us)
Async XLA Ops:
  1.5 10.6 %collective-permute-start = (f32[2,96,128]{2,1,0:T(8,128)S(1)}, f32[2,96,128]{2,1,0:T(8,128)S(1)}, u32[]{:S(2)}, u32[]{:S(2)}) collective-permute-start(f32[2,96,128]{2,1,0:T(8,128)S(1)} %bitcast.31), channel_id=1, source_target_pairs={{0,1},{1,2},{2,3},{3,4},{4,5},{5,6},{6,7},{7,8},{8,9},{9,10},{10,1... | collective-permute-start | bytes 294920 | tf_op jit(solution)/shard_map/ppermute | solution.py:728
  3.3 12.2 %copy-start.2 = (s32[3,6,1]{1,2,0:T(1,128)S(1)}, s32[3,6,1]{1,2,0:T(1,128)}, u32[]{:S(2)}) copy-start(s32[3,6,1]{1,2,0:T(1,128)} %param.15) | copy-start | bytes 220
  3.3 12.3 %copy-start.3 = (s32[1,1,16,2]{2,3,1,0:T(2,128)S(1)}, s32[1,1,16,2]{2,3,1,0:T(2,128)}, u32[]{:S(2)}) copy-start(s32[1,1,16,2]{2,3,1,0:T(2,128)} %param.14) | copy-start | bytes 388
  3.3 12.5 %copy-start.4 = (s32[6,1]{0,1:T(1,128)S(1)}, s32[6,1]{0,1:T(1,128)}, u32[]{:S(2)}) copy-start(s32[6,1]{0,1:T(1,128)} %param.13) | copy-start | bytes 76
  3.3 8.9 %collective-permute-start.1 = (f32[2,96,128]{2,1,0:T(8,128)S(1)}, f32[2,96,128]{2,1,0:T(8,128)S(1)}, u32[]{:S(2)}, u32[]{:S(2)}) collective-permute-start(f32[2,96,128]{2,1,0:T(8,128)S(1)} %bitcast.30), channel_id=1, source_target_pairs={{1,0},{2,1},{3,2},{4,3},{5,4},{6,5},{7,6},{8,7},{9,8},{10,9},{11,1... | collective-permute-start | bytes 294920 | tf_op jit(solution)/shard_map/ppermute | solution.py:732
  12.2 4.8 %collective-permute-start.3 = (f32[4,16,128]{2,1,0:T(8,128)S(1)}, f32[4,16,128]{2,1,0:T(8,128)S(1)}, u32[]{:S(2)}, u32[]{:S(2)}) collective-permute-start(f32[4,16,128]{2,1,0:T(8,128)S(1)} %get-tuple-element.55.my_nxt), channel_id=1, source_target_pairs={{0,16},{16,32},{32,48},{48,64},{64,80},{80,96},{96,112},{112,0},{1... | collective-permute-start | bytes 98312 | tf_op jit(solution)/shard_map/ppermute | solution.py:728
  12.2 4.9 %collective-permute-start.2 = (f32[5,16,128]{2,1,0:T(8,128)S(1)}, f32[5,16,128]{2,1,0:T(8,128)S(1)}, u32[]{:S(2)}, u32[]{:S(2)}) collective-permute-start(f32[5,16,128]{2,1,0:T(8,128)S(1)} %get-tuple-element.54.my_prv), channel_id=1, source_target_pairs={{16,0},{32,16},{48,32},{64,48},{80,64},{96,80},{112,96},{0,112},{1... | collective-permute-start | bytes 122888 | tf_op jit(solution)/shard_map/ppermute | solution.py:732
  17.1 21.3 %copy-start.1 = (bf16[256,384]{1,0:T(8,128)(2,1)S(1)}, bf16[256,384]{1,0:T(8,128)(2,1)}, u32[]{:S(2)}) copy-start(bf16[256,384]{1,0:T(8,128)(2,1)} %constant.91.clone.shift) | copy-start | bytes 589828
  60.4 28.2 %copy-start = (bf16[384,256]{1,0:T(8,128)(2,1)S(1)}, bf16[384,256]{1,0:T(8,128)(2,1)}, u32[]{:S(2)}) copy-start(bf16[384,256]{1,0:T(8,128)(2,1)} %constant.92.clone.shift_t) | copy-start | bytes 589828
  83.0 5.6 %collective-permute-start.4 = (f32[16,16,128]{2,1,0:T(8,128)S(1)}, f32[16,16,128]{2,1,0:T(8,128)S(1)}, u32[]{:S(2)}, u32[]{:S(2)}) collective-permute-start(f32[16,16,128]{2,1,0:T(8,128)S(1)} %pad_maximum_fusion), channel_id=1, source_target_pairs={{0,16},{16,32},{32,48},{48,64},{64,80},{80,96},{96,112},{112,0},{1... | collective-permute-start | bytes 393224 | tf_op jit(solution)/shard_map/ppermute | solution.py:728
  83.0 5.6 %collective-permute-start.5 = (f32[16,16,128]{2,1,0:T(8,128)S(1)}, f32[16,16,128]{2,1,0:T(8,128)S(1)}, u32[]{:S(2)}, u32[]{:S(2)}) collective-permute-start(f32[16,16,128]{2,1,0:T(8,128)S(1)} %pad_maximum_fusion.1), channel_id=1, source_target_pairs={{16,0},{32,16},{48,32},{64,48},{80,64},{96,80},{112,96},{0,112},{1... | collective-permute-start | bytes 393224 | tf_op jit(solution)/shard_map/ppermute | solution.py:732
  98.9 4.9 %collective-permute-start.6 = (f32[16,8,128]{2,1,0:T(8,128)S(1)}, f32[16,8,128]{2,1,0:T(8,128)S(1)}, u32[]{:S(2)}, u32[]{:S(2)}) collective-permute-start(f32[16,8,128]{2,1,0:T(8,128)S(1)} %get-tuple-element.61), channel_id=1, source_target_pairs={{16,0},{32,16},{48,32},{64,48},{80,64},{96,80},{112,96},{0,112},{1... | collective-permute-start | bytes 196616 | tf_op jit(solution)/shard_map/ppermute | solution.py:732
  101.9 4.9 %collective-permute-start.7 = (f32[16,8,128]{2,1,0:T(8,128)S(1)}, f32[16,8,128]{2,1,0:T(8,128)S(1)}, u32[]{:S(2)}, u32[]{:S(2)}) collective-permute-start(f32[16,8,128]{2,1,0:T(8,128)S(1)} %get-tuple-element.62), channel_id=1, source_target_pairs={{0,16},{16,32},{32,48},{48,64},{64,80},{80,96},{96,112},{112,0},{1... | collective-permute-start | bytes 196616 | tf_op jit(solution)/shard_map/ppermute | solution.py:728
  156.7 7.3 %collective-permute-start.9 = (f32[16,8,128]{2,1,0:T(8,128)S(1)}, f32[16,8,128]{2,1,0:T(8,128)S(1)}, u32[]{:S(2)}, u32[]{:S(2)}) collective-permute-start(f32[16,8,128]{2,1,0:T(8,128)S(1)} %slice_bitcast_fusion), channel_id=1, source_target_pairs={{0,16},{16,32},{32,48},{48,64},{64,80},{80,96},{96,112},{112,0},{1... | collective-permute-start | bytes 196616 | tf_op jit(solution)/shard_map/ppermute | solution.py:728
  156.7 7.3 %collective-permute-start.8 = (f32[16,8,128]{2,1,0:T(8,128)S(1)}, f32[16,8,128]{2,1,0:T(8,128)S(1)}, u32[]{:S(2)}, u32[]{:S(2)}) collective-permute-start(f32[16,8,128]{2,1,0:T(8,128)S(1)} %slice_bitcast_fusion), channel_id=1, source_target_pairs={{16,0},{32,16},{48,32},{64,48},{80,64},{96,80},{112,96},{0,112},{1... | collective-permute-start | bytes 196616 | tf_op jit(solution)/shard_map/ppermute | solution.py:732

commit v6 on v5

--- a/solution.py
+++ b/solution.py
@@ -101,8 +101,7 @@
     for i in range(CHUNKS):
         copies[2 + i].wait()
 
-        @pl.loop(i * RB // CHUNKS, (i + 1) * RB // CHUNKS)
-        def _(rb):
+        for rb in range(i * RB // CHUNKS, (i + 1) * RB // CHUNKS):
             block = pl.ds(rb * 8, 8)
             vb = v[:, block]
             a = contract(vb, gradients(st, None, None, None, None, rb, 0))
@@ -111,13 +110,11 @@
             sides[0, block] = 0.25 * vb[1, :, 0]
             sides[1, block] = -0.25 * vb[1, :, 15]
 
-            @pl.when(rb == 0)
-            def _():
+            if rb == 0:
                 to_prv[0] = a[0]
                 to_prv[2] = a[1]
 
-            @pl.when(rb == RB - 1)
-            def _():
+            if rb == RB - 1:
                 to_nxt[0] = a[7]
 
     to_prv[1] = v[0, 0]

time: 168 us -> 168 us (level)
  blocking collectives: 104 us -> 106 us
  Pallas kernels: 30.2 us -> 28.5 us
    all_to_all x6, blocking collectives: 104 us -> 106 us  [swap(): return lax.all_to_all(x, 'gy', split_axis=0, concat_axis=0, tiled=True)]
  transfers between devices with their start and end apart: 10 -> 10, of which waited for: 4 -> 4; matrix products, arithmetic and copies ran while one was open for 0% -> 0% of each run, Pallas kernels for 5% -> 4%
where the time goes in v6:
time: 168 us; the launch traced here: 165 us
  blocking collectives  106 us (63%)
  Pallas kernels  28.5 us (17%)
  starting transfers between devices  19.7 us (12%)
  waiting for transfers between devices  7.57 us (5%)
  local copies, waits for them, and re-layouts  2.73 us (2%)
    all_to_all x6, blocking collectives, swap(): return lax.all_to_all(x, 'gy', split_axis=0, concat_axis=0, tiled=True)  106 us
    ppermute x5, starting transfers between devices, to_prev(): return lax.ppermute(x, axis, [((i + 1) % count, i) for i in range(count)])  17.9 us
    pallas_call x1, Pallas kernels, normal(): pl.pallas_call(normal_kernel, in_specs=[SMEM, VMEM, VMEM, VMEM, VMEM, VME...  10.3 us
    ppermute x5, waiting for transfers between devices, to_next(): return lax.ppermute(x, axis, [(i, (i + 1) % count) for i in range(count)])  5.6 us
    pallas_call x1, Pallas kernels, push(): pl.pallas_call(push_kernel, in_specs=[SMEM, VMEM, VMEM, pl.BlockSpec(memo...  4.11 us
    pallas_call x1, Pallas kernels, pull(): pl.pallas_call(pull_kernel, in_specs=[SMEM, VMEM, VMEM], out_specs=VMEM,...  3.63 us
    pallas_call x1, Pallas kernels, pre(): pl.pallas_call(pre_kernel, in_specs=[hbm, hbm], out_specs=[VMEM] * 5, out...  3.43 us
  transfers between devices with their start and end apart: 10, of which 4 were waited for; matrix products, arithmetic and copies ran while one was open for 0% of the time, Pallas kernels for 4%

profile of v6, /device:TPU:0, one launch (start us, length us, event | category | flops | bytes accessed | tf_op | source)
XLA Modules:
  0.0 165.1 jit_solution(14994948225656467034)
XLA Ops:
  0.0 1.5 fusion.6
  1.5 1.8 %collective-permute-start = (f32[2,96,128]{2,1,0:T(8,128)S(1)}, f32[2,96,128]{2,1,0:T(8,128)S(1)}, u32[]{:S(2)}, u32[]{:S(2)}) collective-permute-start(f32[2,96,128]{2,1,0:T(8,128)S(1)} %bitcast.31), channel_id=1, source_target_pairs={{0,1},{1,2},{2,3},{3,4},{4,5},{5,6},{6,7},{7,8},{8,9},{9,10},{10,1... | collective-permute-start | bytes 294920 | tf_op jit(solution)/shard_map/ppermute | solution.py:725
  3.3 3.7 %collective-permute-start.1 = (f32[2,96,128]{2,1,0:T(8,128)S(1)}, f32[2,96,128]{2,1,0:T(8,128)S(1)}, u32[]{:S(2)}, u32[]{:S(2)}) collective-permute-start(f32[2,96,128]{2,1,0:T(8,128)S(1)} %bitcast.30), channel_id=1, source_target_pairs={{1,0},{2,1},{3,2},{4,3},{5,4},{6,5},{7,6},{8,7},{9,8},{10,9},{11,1... | collective-permute-start | bytes 294920 | tf_op jit(solution)/shard_map/ppermute | solution.py:729
  7.0 3.4 %pre.1 = (f32[16,13,8,128]{3,2,1,0:T(8,128)S(1)}, f32[16,12,8,128]{3,2,1,0:T(8,128)S(1)}, f32[2,96,128]{2,1,0:T(8,128)S(1)}, f32[5,16,128]{2,1,0:T(8,128)S(1)}, f32[4,16,128]{2,1,0:T(8,128)S(1)}) custom-call(f32[3,96,16,128]{3,2,1,0:T(8,128)} %v_hbm.1, f32[2,96,16,128]{3,2,1,0:T(8,128)} %st_hbm.3), custom_call_target="tpu_custom_call" | custom-call | flops 20000000 | bytes 6000000 | tf_op jit(solution)/shard_map/pre/pallas_call | solution.py:134
  10.5 3.2 %collective-permute-start.2 = (f32[5,16,128]{2,1,0:T(8,128)S(1)}, f32[5,16,128]{2,1,0:T(8,128)S(1)}, u32[]{:S(2)}, u32[]{:S(2)}) collective-permute-start(f32[5,16,128]{2,1,0:T(8,128)S(1)} %get-tuple-element.54.my_prv), channel_id=1, source_target_pairs={{16,0},{32,16},{48,32},{64,48},{80,64},{96,80},{112,96},{0,112},{1... | collective-permute-start | bytes 122888 | tf_op jit(solution)/shard_map/ppermute | solution.py:729
  13.9 0.1 concatenate.27
  14.1 0.1 concatenate.30
  14.2 1.2 columns.1
  15.4 0.5 close.1
  15.9 21.1 %all_to_all.30.x = f32[16,13,8,128]{3,2,1,0:T(8,128)S(1)} all-to-all(f32[16,13,8,128]{3,2,1,0:T(8,128)S(1)} %get-tuple-element.57), channel_id=1, replica_groups=mesh['gx'=8,'gy'=16] {'gy'}, dimensions={0} | all-to-all | bytes 1703936 | tf_op jit(solution)/shard_map/all_to_all | solution.py:733
  37.5 0.3 select_reduce_fusion
  37.9 0.1 fusion.3
  38.1 0.1 stack.18
  38.2 0.1 stack.17
  38.4 3.6 %pull.1 = f32[16,12,8,128]{3,2,1,0:T(8,128)S(1)} custom-call(s32[4,96]{1,0:T(4,128)S(1)} %pad_add_fusion.tab, bf16[256,384]{1,0:T(8,128)(2,1)S(1)} %copy-done.1, f32[16,13,8,128]{3,2,1,0:T(8,128)S(1)} %all_to_all.30.x), custom_call_target="tpu_custom_call" | custom-call | tf_op jit(solution)/shard_map/pull/pallas_call | solution.py:513
  42.0 17.3 %all_to_all.31.r = f32[16,12,8,128]{3,2,1,0:T(8,128)S(1)} all-to-all(f32[16,12,8,128]{3,2,1,0:T(8,128)S(1)} %pull.1), channel_id=1, replica_groups=mesh['gx'=8,'gy'=16] {'gy'}, dimensions={0} | all-to-all | bytes 1572864 | tf_op jit(solution)/shard_map/all_to_all | solution.py:733
  59.4 1.0 depth.1
  60.4 22.5 %all_to_all.32.x = f32[16,168,128]{2,1,0:T(8,128)S(1)} all-to-all(f32[16,168,128]{2,1,0:T(8,128)S(1)} %depth.1), channel_id=1, replica_groups=mesh['gx'=8,'gy'=16] {'gy'}, dimensions={0} | all-to-all | bytes 2752512 | tf_op jit(solution)/shard_map/all_to_all | solution.py:733
  83.0 2.9 %collective-permute-start.5 = (f32[16,16,128]{2,1,0:T(8,128)S(1)}, f32[16,16,128]{2,1,0:T(8,128)S(1)}, u32[]{:S(2)}, u32[]{:S(2)}) collective-permute-start(f32[16,16,128]{2,1,0:T(8,128)S(1)} %pad_maximum_fusion.1), channel_id=1, source_target_pairs={{16,0},{32,16},{48,32},{64,48},{80,64},{96,80},{112,96},{0,112},{1... | collective-permute-start | bytes 393224 | tf_op jit(solution)/shard_map/ppermute | solution.py:729
  86.0 2.6 %collective-permute-done.4.prv = f32[16,16,128]{2,1,0:T(8,128)S(1)} collective-permute-done((f32[16,16,128]{2,1,0:T(8,128)S(1)}, f32[16,16,128]{2,1,0:T(8,128)S(1)}, u32[]{:S(2)}, u32[]{:S(2)}) %collective-permute-start.4) | collective-permute-done | bytes 131104 | tf_op jit(solution)/shard_map/ppermute | solution.py:725
  88.6 10.3 %normal.1 = (f32[16,12,8,128]{3,2,1,0:T(8,128)S(1)}, f32[16,8,128]{2,1,0:T(8,128)S(1)}, f32[16,8,128]{2,1,0:T(8,128)S(1)}) custom-call(s32[4,96]{1,0:T(4,128)S(1)} %pad_add_fusion.tab, bf16[256,384]{1,0:T(8,128)(2,1)S(1)} %copy-done.1, bf16[384,256]{1,0:T(8,128)(2,1)S(1)} %copy-done, f32[16,168,128]{2,1,0:T(8,128)S(1)} %all_to_all.32.x, ...), custom_call_target="tpu_custom_call" | custom-call | tf_op jit(solution)/shard_map/normal/pallas_call | solution.py:630
  98.9 2.9 %collective-permute-start.6 = (f32[16,8,128]{2,1,0:T(8,128)S(1)}, f32[16,8,128]{2,1,0:T(8,128)S(1)}, u32[]{:S(2)}, u32[]{:S(2)}) collective-permute-start(f32[16,8,128]{2,1,0:T(8,128)S(1)} %get-tuple-element.61), channel_id=1, source_target_pairs={{16,0},{32,16},{48,32},{64,48},{80,64},{96,80},{112,96},{0,112},{1... | collective-permute-start | bytes 196616 | tf_op jit(solution)/shard_map/ppermute | solution.py:729
  101.9 1.9 %collective-permute-done.6 = f32[16,8,128]{2,1,0:T(8,128)S(1)} collective-permute-done((f32[16,8,128]{2,1,0:T(8,128)S(1)}, f32[16,8,128]{2,1,0:T(8,128)S(1)}, u32[]{:S(2)}, u32[]{:S(2)}) %collective-permute-start.6) | collective-permute-done | bytes 65568 | tf_op jit(solution)/shard_map/ppermute | solution.py:729
  103.8 3.0 %collective-permute-done.7 = f32[16,8,128]{2,1,0:T(8,128)S(1)} collective-permute-done((f32[16,8,128]{2,1,0:T(8,128)S(1)}, f32[16,8,128]{2,1,0:T(8,128)S(1)}, u32[]{:S(2)}, u32[]{:S(2)}) %collective-permute-start.7) | collective-permute-done | bytes 65568 | tf_op jit(solution)/shard_map/ppermute | solution.py:725
  106.8 14.9 %all_to_all.33.r.adj1 = f32[16,12,8,128]{3,2,1,0:T(8,128)S(1)} all-to-all(f32[16,12,8,128]{3,2,1,0:T(8,128)S(1)} %fusion), channel_id=1, replica_groups=mesh['gx'=8,'gy'=16] {'gy'}, dimensions={0} | all-to-all | bytes 1572864 | tf_op jit(solution)/shard_map/all_to_all | solution.py:733
  121.7 1.0 depth_adjoint.1
  122.7 14.8 %all_to_all.34.v = f32[16,12,8,128]{3,2,1,0:T(8,128)S(1)} all-to-all(f32[16,12,8,128]{3,2,1,0:T(8,128)S(1)} %depth_adjoint.1), channel_id=1, replica_groups=mesh['gx'=8,'gy'=16] {'gy'}, dimensions={0} | all-to-all | bytes 1572864 | tf_op jit(solution)/shard_map/all_to_all | solution.py:733
  137.5 4.1 %push.1 = (f32[16,13,8,128]{3,2,1,0:T(8,128)S(1)}, f32[2,96,16,128]{3,2,1,0:T(8,128)S(1)}) custom-call(s32[4,96]{1,0:T(4,128)S(1)} %pad_add_fusion.tab, bf16[384,256]{1,0:T(8,128)(2,1)S(1)} %copy-done, f32[16,12,8,128]{3,2,1,0:T(8,128)S(1)} %all_to_all.34.v, f32[2,96,16,128]{3,2,1,0:T(8,128)} %st_hbm.3), custom_call_target="tpu_custom_call" | custom-call | tf_op jit(solution)/shard_map/push/pallas_call | solution.py:561
  141.6 15.1 %all_to_all.35.adj0 = f32[16,13,8,128]{3,2,1,0:T(8,128)S(1)} all-to-all(f32[16,13,8,128]{3,2,1,0:T(8,128)S(1)} %get-tuple-element.63), channel_id=1, replica_groups=mesh['gx'=8,'gy'=16] {'gy'}, dimensions={0} | all-to-all | bytes 1703936 | tf_op jit(solution)/shard_map/all_to_all | solution.py:733
  156.7 5.0 %collective-permute-start.8 = (f32[16,8,128]{2,1,0:T(8,128)S(1)}, f32[16,8,128]{2,1,0:T(8,128)S(1)}, u32[]{:S(2)}, u32[]{:S(2)}) collective-permute-start(f32[16,8,128]{2,1,0:T(8,128)S(1)} %slice_bitcast_fusion), channel_id=1, source_target_pairs={{16,0},{32,16},{48,32},{64,48},{80,64},{96,80},{112,96},{0,112},{1... | collective-permute-start | bytes 196616 | tf_op jit(solution)/shard_map/ppermute | solution.py:729
  161.7 2.1 %force.1.prior = f32[3,96,16,128]{3,2,1,0:T(8,128)} custom-call(f32[16,12,8,128]{3,2,1,0:T(8,128)S(1)} %all_to_all.33.r.adj1, f32[16,13,8,128]{3,2,1,0:T(8,128)S(1)} %all_to_all.35.adj0, f32[2,96,16,128]{3,2,1,0:T(8,128)S(1)} %get-tuple-element.64.st, f32[4,16,128]{2,1,0:T(8,128)S(1)} %collective-permute-done.3.from_prv.top, ...), custom_call_target="tpu_custom_call" | custom-call | flops 20000000 | bytes 6000000 | tf_op jit(solution)/shard_map/force/pallas_call | solution.py:328
  163.9 1.2 force_edge.1
  (45 shorter events, 1.2 us)
Async XLA Ops:
  1.5 9.0 %collective-permute-start = (f32[2,96,128]{2,1,0:T(8,128)S(1)}, f32[2,96,128]{2,1,0:T(8,128)S(1)}, u32[]{:S(2)}, u32[]{:S(2)}) collective-permute-start(f32[2,96,128]{2,1,0:T(8,128)S(1)} %bitcast.31), channel_id=1, source_target_pairs={{0,1},{1,2},{2,3},{3,4},{4,5},{5,6},{6,7},{7,8},{8,9},{9,10},{10,1... | collective-permute-start | bytes 294920 | tf_op jit(solution)/shard_map/ppermute | solution.py:725
  3.3 10.5 %copy-start.2 = (s32[3,6,1]{1,2,0:T(1,128)S(1)}, s32[3,6,1]{1,2,0:T(1,128)}, u32[]{:S(2)}) copy-start(s32[3,6,1]{1,2,0:T(1,128)} %param.15) | copy-start | bytes 220
  3.3 10.6 %copy-start.3 = (s32[1,1,16,2]{2,3,1,0:T(2,128)S(1)}, s32[1,1,16,2]{2,3,1,0:T(2,128)}, u32[]{:S(2)}) copy-start(s32[1,1,16,2]{2,3,1,0:T(2,128)} %param.14) | copy-start | bytes 388
  3.3 10.8 %copy-start.4 = (s32[6,1]{0,1:T(1,128)S(1)}, s32[6,1]{0,1:T(1,128)}, u32[]{:S(2)}) copy-start(s32[6,1]{0,1:T(1,128)} %param.13) | copy-start | bytes 76
  3.3 7.2 %collective-permute-start.1 = (f32[2,96,128]{2,1,0:T(8,128)S(1)}, f32[2,96,128]{2,1,0:T(8,128)S(1)}, u32[]{:S(2)}, u32[]{:S(2)}) collective-permute-start(f32[2,96,128]{2,1,0:T(8,128)S(1)} %bitcast.30), channel_id=1, source_target_pairs={{1,0},{2,1},{3,2},{4,3},{5,4},{6,5},{7,6},{8,7},{9,8},{10,9},{11,1... | collective-permute-start | bytes 294920 | tf_op jit(solution)/shard_map/ppermute | solution.py:729
  10.5 4.8 %collective-permute-start.3 = (f32[4,16,128]{2,1,0:T(8,128)S(1)}, f32[4,16,128]{2,1,0:T(8,128)S(1)}, u32[]{:S(2)}, u32[]{:S(2)}) collective-permute-start(f32[4,16,128]{2,1,0:T(8,128)S(1)} %get-tuple-element.55.my_nxt), channel_id=1, source_target_pairs={{0,16},{16,32},{32,48},{48,64},{64,80},{80,96},{96,112},{112,0},{1... | collective-permute-start | bytes 98312 | tf_op jit(solution)/shard_map/ppermute | solution.py:725
  10.5 4.9 %collective-permute-start.2 = (f32[5,16,128]{2,1,0:T(8,128)S(1)}, f32[5,16,128]{2,1,0:T(8,128)S(1)}, u32[]{:S(2)}, u32[]{:S(2)}) collective-permute-start(f32[5,16,128]{2,1,0:T(8,128)S(1)} %get-tuple-element.54.my_prv), channel_id=1, source_target_pairs={{16,0},{32,16},{48,32},{64,48},{80,64},{96,80},{112,96},{0,112},{1... | collective-permute-start | bytes 122888 | tf_op jit(solution)/shard_map/ppermute | solution.py:729
  15.4 23.0 %copy-start.1 = (bf16[256,384]{1,0:T(8,128)(2,1)S(1)}, bf16[256,384]{1,0:T(8,128)(2,1)}, u32[]{:S(2)}) copy-start(bf16[256,384]{1,0:T(8,128)(2,1)} %constant.91.clone.shift) | copy-start | bytes 589828
  60.4 28.2 %copy-start = (bf16[384,256]{1,0:T(8,128)(2,1)S(1)}, bf16[384,256]{1,0:T(8,128)(2,1)}, u32[]{:S(2)}) copy-start(bf16[384,256]{1,0:T(8,128)(2,1)} %constant.92.clone.shift_t) | copy-start | bytes 589828
  83.0 5.6 %collective-permute-start.4 = (f32[16,16,128]{2,1,0:T(8,128)S(1)}, f32[16,16,128]{2,1,0:T(8,128)S(1)}, u32[]{:S(2)}, u32[]{:S(2)}) collective-permute-start(f32[16,16,128]{2,1,0:T(8,128)S(1)} %pad_maximum_fusion), channel_id=1, source_target_pairs={{0,16},{16,32},{32,48},{48,64},{64,80},{80,96},{96,112},{112,0},{1... | collective-permute-start | bytes 393224 | tf_op jit(solution)/shard_map/ppermute | solution.py:725
  83.0 5.6 %collective-permute-start.5 = (f32[16,16,128]{2,1,0:T(8,128)S(1)}, f32[16,16,128]{2,1,0:T(8,128)S(1)}, u32[]{:S(2)}, u32[]{:S(2)}) collective-permute-start(f32[16,16,128]{2,1,0:T(8,128)S(1)} %pad_maximum_fusion.1), channel_id=1, source_target_pairs={{16,0},{32,16},{48,32},{64,48},{80,64},{96,80},{112,96},{0,112},{1... | collective-permute-start | bytes 393224 | tf_op jit(solution)/shard_map/ppermute | solution.py:729
  98.9 4.9 %collective-permute-start.6 = (f32[16,8,128]{2,1,0:T(8,128)S(1)}, f32[16,8,128]{2,1,0:T(8,128)S(1)}, u32[]{:S(2)}, u32[]{:S(2)}) collective-permute-start(f32[16,8,128]{2,1,0:T(8,128)S(1)} %get-tuple-element.61), channel_id=1, source_target_pairs={{16,0},{32,16},{48,32},{64,48},{80,64},{96,80},{112,96},{0,112},{1... | collective-permute-start | bytes 196616 | tf_op jit(solution)/shard_map/ppermute | solution.py:729
  101.9 4.9 %collective-permute-start.7 = (f32[16,8,128]{2,1,0:T(8,128)S(1)}, f32[16,8,128]{2,1,0:T(8,128)S(1)}, u32[]{:S(2)}, u32[]{:S(2)}) collective-permute-start(f32[16,8,128]{2,1,0:T(8,128)S(1)} %get-tuple-element.62), channel_id=1, source_target_pairs={{0,16},{16,32},{32,48},{48,64},{64,80},{80,96},{96,112},{112,0},{1... | collective-permute-start | bytes 196616 | tf_op jit(solution)/shard_map/ppermute | solution.py:725
  156.7 7.2 %collective-permute-start.9 = (f32[16,8,128]{2,1,0:T(8,128)S(1)}, f32[16,8,128]{2,1,0:T(8,128)S(1)}, u32[]{:S(2)}, u32[]{:S(2)}) collective-permute-start(f32[16,8,128]{2,1,0:T(8,128)S(1)} %slice_bitcast_fusion), channel_id=1, source_target_pairs={{0,16},{16,32},{32,48},{48,64},{64,80},{80,96},{96,112},{112,0},{1... | collective-permute-start | bytes 196616 | tf_op jit(solution)/shard_map/ppermute | solution.py:725
  156.7 7.2 %collective-permute-start.8 = (f32[16,8,128]{2,1,0:T(8,128)S(1)}, f32[16,8,128]{2,1,0:T(8,128)S(1)}, u32[]{:S(2)}, u32[]{:S(2)}) collective-permute-start(f32[16,8,128]{2,1,0:T(8,128)S(1)} %slice_bitcast_fusion), channel_id=1, source_target_pairs={{16,0},{32,16},{48,32},{64,48},{80,64},{96,80},{112,96},{0,112},{1... | collective-permute-start | bytes 196616 | tf_op jit(solution)/shard_map/ppermute | solution.py:729
